TPU v7x, 128 devices: a whole 4x4x4 slice. The times are simulated.
128 devices in a mesh: row: 16 (over z_hi, y, core), col: 8 (over z_lo, x).
Axes of the slice: x: 4, y: 4, z: 4 (z_hi: 2, z_lo: 2; z = z_hi * 2 + z_lo), core: 2. Of those that a mesh axis runs over, the one named last changes fastest.
Arguments:
- tokens: bfloat16 [4096, 2048], P('row', 'col'), may hold values from -6 to 6
- attn_gain: float32 [2048], replicated, may hold values from 0.5 to 6, as said below
- mlp_gain: float32 [2048], replicated, may hold values from 0.5 to 1.5
- trainer_qkv: float32 [2048, 3072], P(('row', 'col')), may hold values from -0.125 to 0.125
- trainer_out: float32 [2048, 2048], P(None, ('row', 'col')), may hold values from -0.125 to 0.125
- router: bfloat16 [2048, 64], replicated, may hold values from -0.125 to 0.125
- shared_gate: bfloat16 [2048, 2816], P(None, 'col'), may hold values from -0.125 to 0.125
- shared_up: bfloat16 [2048, 2816], P(None, 'col'), may hold values from -0.125 to 0.125
- shared_down: bfloat16 [2816, 2048], P('col'), may hold values from -0.109375 to 0.109375
- expert_gate_up: bfloat16 [128, 2048, 1408], P(('row', 'col')), may hold values from -0.125 to 0.125
- expert_down: bfloat16 [128, 704, 2048], P(('row', 'col')), may hold values from -0.15625 to 0.15625
- lengths: int32 [8], replicated, may hold values from 1 to 2176, as said below
- order: int32 [8], replicated, may hold values from 0 to 7, as said below
- routes: int32 [4096, 6], P('row'), may hold values from 0 to 63, all different within a row; in each aligned block of 256 rows (0 to 255, 256 to 511, ...) at most 40 rows name the same one
Outputs:
- hidden_states: bfloat16 [4096, 2048], P('row', 'col')
- kv_cache: bfloat16 [4096, 1024], P('row', 'col')
- qkv_block: bfloat16 [2048, 4096], P('row', 'col')
- out_block: bfloat16 [2048, 2048], P('col', 'row')
Inputs may be any that keep to these rules, and one draw needn't show every extreme that they name: `attn_gain`: positive and not all equal. `lengths`: request 0 has exactly 2176 tokens; every other request has at least one; they sum to 4096. `order`: each request once; request 0 is packed last. `routes`: each row names 6 different experts; in the rows of one device along row (aligned blocks of 256 rows) no expert is named by more than 40 rows, a bound that some block reaches.
All inputs are finite; a program needn't handle non-finite values.
Results may differ from a plain program's by a relative error of at most 0.022.
The roundings to bfloat16 on the way count: a program that leaves them out, or rounds other values in their place, can miss the bound.
Values may be sent and summed in bfloat16 or wider, within the bound.
No kernel may reach another device: no remote copies, remote signals or barrier semaphores. Data moves between devices by JAX's collectives and lax.ppermute only.
A program may use at most 128 MiB of HBM per device.

v0:
```python
import jax
import jax.numpy as jnp
from jax import lax
from jax.sharding import PartitionSpec as P

D = 2048
HEAD_DIM = 128
TOP = 6


epsilon = 1e-06
rope_base = 600000.0
masked_score = -1e30


def prompt_tables(lengths, order, first, height):
    prompt_ids = jnp.arange(lengths.shape[0], dtype=jnp.int32)
    picked = order[:, None] == prompt_ids[None, :]
    packed_len = jnp.sum(jnp.where(picked, lengths[None, :], 0), axis=1)
    packed_end = jnp.cumsum(packed_len)
    packed_start = packed_end - packed_len
    request_start = jnp.cumsum(lengths) - lengths
    positions = first + jnp.arange(height, dtype=jnp.int32)
    segment = jnp.sum((positions[:, None] >= packed_end[None, :]).astype(jnp.int32), axis=1)
    onehot = segment[:, None] == prompt_ids[None, :]
    within = positions - jnp.sum(jnp.where(onehot, packed_start[None, :], 0), axis=1)
    request = jnp.sum(jnp.where(onehot, order[None, :], 0), axis=1)
    offset = jnp.sum(
        jnp.where(request[:, None] == prompt_ids[None, :], request_start[None, :], 0), axis=1
    )
    return (segment, within, within + offset)


def rms_scale(values, gain):
    wide = values.astype(jnp.float32)
    return wide * lax.rsqrt(jnp.mean(wide * wide, axis=-1, keepdims=True) + epsilon) * gain


def rotary(values, within):
    half_dim = values.shape[-1] // 2
    inverse = rope_base ** (-jnp.arange(half_dim, dtype=jnp.float32) * 2.0 / values.shape[-1])
    angles = within.astype(jnp.float32)[:, None] * inverse[None, :]
    cosine = jnp.cos(angles)
    sine_part = jnp.sin(angles)
    lower = values[..., :half_dim]
    upper = values[..., half_dim:]
    return jnp.concatenate(
        [lower * cosine - upper * sine_part, upper * cosine + lower * sine_part], axis=-1
    )


def server_columns(trainer_rows, groups):
    height = trainer_rows.shape[0]
    kv_count = groups // 2
    query_part = trainer_rows[:, : 2 * groups * HEAD_DIM].reshape(height, groups, 2 * HEAD_DIM)
    key_part = trainer_rows[:, 2 * groups * HEAD_DIM : (2 * groups + kv_count) * HEAD_DIM].reshape(
        height, kv_count, 1, HEAD_DIM
    )
    value_part = trainer_rows[:, (2 * groups + kv_count) * HEAD_DIM :].reshape(
        height, kv_count, 1, HEAD_DIM
    )
    key_part = jnp.broadcast_to(key_part, (height, kv_count, 2, HEAD_DIM)).reshape(
        height, groups, HEAD_DIM
    )
    value_part = jnp.broadcast_to(value_part, (height, kv_count, 2, HEAD_DIM)).reshape(
        height, groups, HEAD_DIM
    )
    joined = jnp.concatenate([query_part, key_part, value_part], axis=2)
    return joined.reshape(height, groups * 4 * HEAD_DIM).astype(jnp.bfloat16)


def on_device(
    tokens,
    attn_gain,
    mlp_gain,
    trainer_qkv,
    trainer_out,
    router,
    shared_gate,
    shared_up,
    shared_down,
    expert_gate_up,
    expert_down,
    lengths,
    order,
    routes,
):
    tok_rows = tokens.shape[0]
    row_count = lax.axis_size("row")
    col_count = lax.axis_size("col")
    row_index = lax.axis_index("row")
    col_index = lax.axis_index("col")
    first = row_index * tok_rows
    qkv_block = lax.all_to_all(
        server_columns(trainer_qkv, col_count), "col", split_axis=1, concat_axis=0, tiled=True
    )
    out_block = lax.all_to_all(
        trainer_out.astype(jnp.bfloat16), "col", split_axis=0, concat_axis=1, tiled=True
    )
    seg_query, within_query, _ = prompt_tables(lengths, order, first, tok_rows)
    full_tokens = lax.all_gather(tokens, "col", axis=1, tiled=True)
    normed = rms_scale(full_tokens, attn_gain).astype(jnp.bfloat16)
    projected = jnp.dot(
        normed,
        lax.all_gather(qkv_block, "row", axis=0, tiled=True),
        preferred_element_type=jnp.float32,
    )
    queries = projected[:, : 2 * HEAD_DIM].reshape(tok_rows, 2, HEAD_DIM).transpose(1, 0, 2)
    queries = rotary(queries, within_query).astype(jnp.bfloat16)
    key_rows = rotary(projected[:, 2 * HEAD_DIM : 3 * HEAD_DIM], within_query).astype(jnp.bfloat16)
    value_rows = projected[:, 3 * HEAD_DIM :].astype(jnp.bfloat16)
    cache_out = jnp.where(col_index % 2 == 0, key_rows, value_rows)
    query_pos = first + jnp.arange(tok_rows, dtype=jnp.int32)
    scale = HEAD_DIM ** (-0.5)
    key_piece = lax.all_gather(key_rows, "row", axis=0, tiled=True)
    value_piece = lax.all_gather(value_rows, "row", axis=0, tiled=True)
    height = key_piece.shape[0]
    seg_key, _, _ = prompt_tables(lengths, order, jnp.int32(0), height)
    key_pos = jnp.arange(height, dtype=jnp.int32)
    allowed = (
        (seg_key[None, :] == seg_query[:, None])
        & (key_pos[None, :] <= query_pos[:, None])
        & (key_pos[None, :] >= 0)
    )
    row_peak = jnp.full((2, tok_rows), masked_score, jnp.float32)
    scores = (
        jnp.einsum("hqd,kd->hqk", queries, key_piece, preferred_element_type=jnp.float32) * scale
    )
    scores = jnp.where(allowed[None], scores, masked_score)
    new_peak = jnp.maximum(row_peak, jnp.max(scores, axis=2))
    numerators = jnp.where(allowed[None], jnp.exp(scores - new_peak[..., None]), 0.0)
    denominator = jnp.sum(numerators, axis=2)
    summed = jnp.einsum(
        "hqk,kd->hqd",
        numerators.astype(jnp.bfloat16),
        value_piece,
        preferred_element_type=jnp.float32,
    )
    _, denominator, summed = (new_peak, denominator, summed)
    attended = (
        (summed / denominator[..., None])
        .transpose(1, 0, 2)
        .reshape(tok_rows, 2 * HEAD_DIM)
        .astype(jnp.bfloat16)
    )
    attn_terms = jnp.dot(
        attended,
        lax.all_gather(out_block, "row", axis=1, tiled=True),
        preferred_element_type=jnp.float32,
    )
    attn_part = lax.psum_scatter(
        attn_terms.astype(jnp.bfloat16), "col", scatter_dimension=1, tiled=True
    ).astype(jnp.float32)
    resid = (tokens.astype(jnp.float32) + attn_part).astype(jnp.bfloat16)
    full_resid = lax.all_gather(resid, "col", axis=1, tiled=True)
    mlp_in = rms_scale(full_resid, mlp_gain).astype(jnp.bfloat16)
    logits = jnp.dot(mlp_in, router, preferred_element_type=jnp.float32)
    router_probs = jax.nn.softmax(logits, axis=-1)
    n_experts = row_count * col_count // 2
    expert_ids = jnp.arange(n_experts, dtype=jnp.int32)
    chosen = jnp.sum(
        jnp.where(routes[:, :, None] == expert_ids[None, None, :], router_probs[:, None, :], 0.0),
        axis=-1,
    )
    route_weight = (chosen / jnp.sum(chosen, axis=-1, keepdims=True)).astype(jnp.bfloat16)
    shared_hidden = (
        jax.nn.silu(jnp.dot(mlp_in, shared_gate, preferred_element_type=jnp.float32))
        * jnp.dot(mlp_in, shared_up, preferred_element_type=jnp.float32)
    ).astype(jnp.bfloat16)
    shared_part = jnp.dot(shared_hidden, shared_down, preferred_element_type=jnp.float32)
    capacity = max(2, tok_rows * TOP * 5 // (n_experts * 3))
    targets = jnp.arange(row_count, dtype=jnp.int32) * (col_count // 2) + col_index // 2
    matches = routes[:, :, None] == targets[None, None, :]
    member = jnp.any(matches, axis=1)
    slot_of = jnp.cumsum(member.astype(jnp.int32), axis=0) - 1
    chosen_weight = jnp.sum(
        jnp.where(matches, route_weight[:, :, None].astype(jnp.float32), 0.0), axis=1
    )
    placing = member[:, :, None] & (
        slot_of[:, :, None] == jnp.arange(capacity, dtype=jnp.int32)[None, None, :]
    )
    picker = placing.astype(jnp.bfloat16).reshape(tok_rows, row_count * capacity)
    combiner = (
        (placing.astype(jnp.float32) * chosen_weight[:, :, None])
        .astype(jnp.bfloat16)
        .reshape(tok_rows, row_count * capacity)
    )
    outgoing = jnp.einsum("ts,td->sd", picker, mlp_in, preferred_element_type=jnp.float32).astype(
        jnp.bfloat16
    )
    outgoing = outgoing.reshape(row_count, capacity, D)
    gate_up_slab = expert_gate_up[0]
    down_slab = expert_down[0]
    half_units = down_slab.shape[0]
    arrived = lax.all_to_all(outgoing, "row", split_axis=0, concat_axis=0, tiled=True)
    flat = arrived.reshape(-1, D)
    gate_up = jnp.dot(flat, gate_up_slab, preferred_element_type=jnp.float32)
    hidden = (jax.nn.silu(gate_up[:, :half_units]) * gate_up[:, half_units:]).astype(jnp.bfloat16)
    result = (
        jnp.dot(hidden, down_slab, preferred_element_type=jnp.float32)
        .astype(jnp.bfloat16)
        .reshape(arrived.shape)
    )
    came_back = lax.all_to_all(result, "row", split_axis=0, concat_axis=0, tiled=True)
    routed_part = jnp.dot(
        combiner, came_back.reshape(row_count * capacity, D), preferred_element_type=jnp.float32
    )
    layer_part = lax.psum_scatter(
        (routed_part + shared_part).astype(jnp.bfloat16), "col", scatter_dimension=1, tiled=True
    ).astype(jnp.float32)
    layer_out = (resid.astype(jnp.float32) + layer_part).astype(jnp.bfloat16)
    target_rows = first + jnp.arange(tok_rows, dtype=jnp.int32)
    shard_rows = lax.all_gather(layer_out, "row", axis=0, tiled=True)
    _, _, dest = prompt_tables(lengths, order, jnp.int32(0), shard_rows.shape[0])
    mover = (dest[None, :] == target_rows[:, None]).astype(jnp.bfloat16)
    placed = jnp.dot(mover, shard_rows, preferred_element_type=jnp.float32)
    hidden_states = placed.astype(jnp.bfloat16)
    return (hidden_states, cache_out, qkv_block, out_block)


def solution(mesh):
    in_specs = (
        P("row", "col"),
        P(),
        P(),
        P(("row", "col"), None),
        P(None, ("row", "col")),
        P(),
        P(None, "col"),
        P(None, "col"),
        P("col", None),
        P(("row", "col"), None, None),
        P(("row", "col"), None, None),
        P(),
        P(),
        P("row", None),
    )
    out_specs = (P("row", "col"), P("row", "col"), P("row", "col"), P("col", "row"))
    return jax.shard_map(
        on_device, mesh=mesh, in_specs=in_specs, out_specs=out_specs, check_vma=False
    )
```

profile of v0, /device:TPU:97, one launch (start us, length us, event | category | flops | bytes accessed | tf_op | source)
XLA Modules:
  0.0 526.2 jit_solution(7456053766495799101)
XLA Ops:
  9.8 9.4 %all_to_all.45 = bf16[16,8,512]{2,0,1:T(8,128)(2,1)} all-to-all(bf16[16,8,512]{2,0,1:T(8,128)(2,1)S(1)} %pad_maximum_fusion), channel_id=1, replica_groups=mesh['row'=16,'col'=8] {'col'}, dimensions={1} | all-to-all | bytes 262144 | tf_op jit(solution)/shard_map/all_to_all | solution.py:94
  21.0 23.2 %all-gather.8.cloned.1.call-done = bf16[256,2048]{1,0:T(8,128)(2,1)} async-done(((bf16[256,256]{1,0:T(8,128)(2,1)}), bf16[256,2048]{1,0:T(8,128)(2,1)}) %all-gather.8.cloned.1.call-update) | async-done | bytes 1048592 | tf_op jit(solution)/shard_map/all_gather | solution.py:101
  44.2 1.5 fusion.13
  46.3 53.1 %all-gather.10.cloned.1.call-done = bf16[2048,512]{1,0:T(8,128)(2,1)} async-done(((bf16[128,512]{1,0:T(8,128)(2,1)}), bf16[2048,512]{1,0:T(8,128)(2,1)}) %all-gather.10.cloned.1.call-update) | async-done | bytes 2097168 | tf_op jit(solution)/shard_map/all_gather | solution.py:105
  99.4 2.7 fusion.35
  105.4 5.2 all-to-all-start.1
  111.4 2.3 fusion.7
  116.4 31.7 %all-gather.12.cloned.1.call-done = bf16[4096,128]{1,0:T(8,128)(2,1)} async-done(((bf16[256,128]{1,0:T(8,128)(2,1)}), bf16[4096,128]{1,0:T(8,128)(2,1)}) %all-gather.12.cloned.1.call-update) | async-done | bytes 1048592 | tf_op jit(solution)/shard_map/all_gather | solution.py:115
  148.2 3.6 fusion
  151.8 3.2 copy-done.1
  155.0 2.6 fusion.1
  157.6 37.2 %all-gather.14.cloned.1.call-done = bf16[4096,128]{1,0:T(8,128)(2,1)} async-done(((bf16[256,128]{1,0:T(8,128)(2,1)}), bf16[4096,128]{1,0:T(8,128)(2,1)}) %all-gather.14.cloned.1.call-update) | async-done | bytes 1048592 | tf_op jit(solution)/shard_map/all_gather | solution.py:116
  194.8 6.2 %fusion.32 = bf16[256,2,128]{0,2,1:T(8,128)(2,1)S(1)} fusion(f32[2,256,4096]{2,1,0:T(8,128)} %copy-done.1, f32[2,256]{1,0:T(2,128)S(1)} %broadcast_maximum_fusion, pred[256,4096]{1,0:T(8,128)(4,1)} %fusion.7, bf16[4096,128]{1,0:T(8,128)(2,1)} %all-gather.14.cloned.1.call-done, f32[256,2]{0,1:T(2,128)S(1)} %bitcast.109), kind=kOutput, calls=%fused_computation.39 | convolution fusion | flops 547487744 | bytes 10620928 | tf_op jit(solution)/shard_map/hqk,kd->hqd/dot_general | solution.py:133
  201.0 39.9 %all-gather.16.cloned.1.call-done = bf16[256,2048]{0,1:T(8,128)(2,1)} async-done(((bf16[256,128]{0,1:T(8,128)(2,1)}), bf16[256,2048]{0,1:T(8,128)(2,1)}) %all-gather.16.cloned.1.call-update) | async-done | bytes 1048592 | tf_op jit(solution)/shard_map/all_gather | solution.py:148
  240.9 2.7 convolution_convert_fusion.2
  243.7 33.6 %reduce-scatter.3.cloned.1.call-done = bf16[256,256]{1,0:T(8,128)(2,1)} async-done(((bf16[256,2048]{1,0:T(8,128)(2,1)}), bf16[256,256]{1,0:T(8,128)(2,1)}) %reduce-scatter.3.cloned.1.call-update) | async-done | bytes 131088 | tf_op jit(solution)/shard_map/reduce_scatter | solution.py:151
  277.3 1.6 add_convert_fusion.1
  280.2 37.0 %all-gather.18.cloned.1.call-done = bf16[256,2048]{1,0:T(8,128)(2,1)} async-done(((bf16[256,256]{1,0:T(8,128)(2,1)}), bf16[256,2048]{1,0:T(8,128)(2,1)}) %all-gather.18.cloned.1.call-update) | async-done | bytes 1048592 | tf_op jit(solution)/shard_map/all_gather | solution.py:155
  318.8 2.2 convolution_convert_fusion.1
  321.0 43.4 %all_to_all.46 = bf16[16,40,2048]{2,1,0:T(8,128)(2,1)S(1)} all-to-all(bf16[16,40,2048]{2,1,0:T(8,128)(2,1)S(1)} %bitcast.94), channel_id=1, replica_groups=mesh['row'=16,'col'=8] {'row'}, dimensions={0} | all-to-all | bytes 5242880 | tf_op jit(solution)/shard_map/all_to_all | solution.py:195
  364.3 6.6 %fusion.3 = f32[640,1408]{1,0:T(8,128)S(1)} fusion(bf16[640,2048]{1,0:T(8,128)(2,1)S(1)} %bitcast.96, bf16[1,2048,1408]{2,1,0:T(8,128)(2,1)} %param.23), kind=kOutput, calls=%fused_computation.5 | convolution fusion | flops 3690987520 | bytes 11993088 | tf_op jit(solution)/shard_map/dot_general | solution.py:197
  371.0 3.8 convolution_convert_fusion
  374.8 7.4 %all-to-all-start.3 = ((bf16[16,40,2048]{2,1,0:T(8,128)(2,1)}), bf16[16,40,2048]{2,1,0:T(8,128)(2,1)}, u32[]{:S(2)}, u32[]{:S(2)}) async-start(bf16[16,40,2048]{2,1,0:T(8,128)(2,1)} %bitcast.95), calls=%async_computation.4 | async-start | bytes 5242880 | tf_op jit(solution)/shard_map/all_to_all | solution.py:204
  382.3 1.8 fusion.79
  384.4 2.8 fusion.74
  387.1 29.2 %all-to-all-done.3 = bf16[16,40,2048]{2,1,0:T(8,128)(2,1)} async-done(((bf16[16,40,2048]{2,1,0:T(8,128)(2,1)}), bf16[16,40,2048]{2,1,0:T(8,128)(2,1)}, u32[]{:S(2)}, u32[]{:S(2)}) %all-to-all-start.3) | async-done | bytes 2621472 | tf_op jit(solution)/shard_map/all_to_all | solution.py:204
  416.3 4.1 convolution_bitcast_fusion
  420.4 6.0 %fusion.12 = bf16[256,2048]{1,0:T(8,128)(2,1)} fusion(f32[256,2048]{1,0:T(8,128)} %convolution_bitcast_fusion, bf16[352,2048]{1,0:T(8,128)(2,1)} %param.22, bf16[2048,352]{0,1:T(8,128)(2,1)} %param.21, f32[256,352]{0,1:T(8,128)} %fusion.74, bf16[256,2048]{1,0:T(8,128)(2,1)} %all-gather.18.cloned.1.call-done, f32[2048]{0:T(1024)S(1)} %copy-done.11, ...), kind=kOutput, calls=%fused_computation.23 | convolution fusion | flops 741883904 | bytes 7447552 | tf_op jit(solution)/shard_map/dot_general | solution.py:170
  426.5 34.9 %reduce-scatter.5.cloned.1.call-done = bf16[256,256]{1,0:T(8,128)(2,1)} async-done(((bf16[256,2048]{1,0:T(8,128)(2,1)}), bf16[256,256]{1,0:T(8,128)(2,1)}) %reduce-scatter.5.cloned.1.call-update) | async-done | bytes 131088 | tf_op jit(solution)/shard_map/reduce_scatter | solution.py:208
  461.4 1.6 add_convert_fusion
  464.3 51.7 %all-gather.20.cloned.1.call-done = bf16[4096,256]{1,0:T(8,128)(2,1)} async-done(((bf16[256,256]{1,0:T(8,128)(2,1)}), bf16[4096,256]{1,0:T(8,128)(2,1)}) %all-gather.20.cloned.1.call-update) | async-done | bytes 2097168 | tf_op jit(solution)/shard_map/all_gather | solution.py:213
  516.0 3.0 fusion.26
  (101 shorter events, 16.8 us)
Async XLA Ops:
  7.2 363.8 %copy-start = (bf16[1,704,2048]{2,1,0:T(8,128)(2,1)S(1)}, bf16[1,704,2048]{2,1,0:T(8,128)(2,1)}, u32[]{:S(2)}) copy-start(bf16[1,704,2048]{2,1,0:T(8,128)(2,1)} %param.24) | copy-start | bytes 8650756
  7.2 37.1 %all-gather.8.cloned.1.call-start = ((), (), s32[]{:S(2)}) async-start(), calls=%async_computation.6 | async-start | bytes 1179648 | tf_op jit(solution)/shard_map/all_gather | solution.py:101
  7.9 91.5 %all-gather.10.cloned.1.call-start = ((), (), s32[]{:S(2)}) async-start(), calls=%async_computation.7 | async-start | bytes 2228224 | tf_op jit(solution)/shard_map/all_gather | solution.py:105
  19.2 128.9 %all-gather.12.cloned.1.call-start = ((), (), s32[]{:S(2)}) async-start(), calls=%async_computation.8 | async-start | bytes 1114112 | tf_op jit(solution)/shard_map/all_gather | solution.py:115
  20.3 0.6 copy-start.12
  46.3 58.5 %copy-start.9 = (f32[2048,16]{0,1:T(8,128)S(1)}, f32[2048,16]{0,1:T(8,128)}, u32[]{:S(2)}) copy-start(f32[2048,16]{0,1:T(8,128)} %param.18) | copy-start | bytes 393220
  99.4 2.7 copy-start.14
  104.2 90.6 %all-gather.14.cloned.1.call-start = ((), (), s32[]{:S(2)}) async-start(), calls=%async_computation.9 | async-start | bytes 1114112 | tf_op jit(solution)/shard_map/all_gather | solution.py:116
  105.4 9.2 %all-to-all-start.1 = ((bf16[8,256,16]{1,2,0:T(8,128)(2,1)}), bf16[8,256,16]{1,2,0:T(8,128)(2,1)S(1)}, u32[]{:S(2)}, u32[]{:S(2)}) async-start(bf16[8,256,16]{1,2,0:T(8,128)(2,1)} %bitcast.92), calls=%async_computation.1 | async-start | bytes 131072 | tf_op jit(solution)/shard_map/all_to_all | solution.py:97
  110.6 130.3 %all-gather.16.cloned.1.call-start = ((), (), s32[]{:S(2)}) async-start(), calls=%async_computation.10 | async-start | bytes 1114112 | tf_op jit(solution)/shard_map/all_gather | solution.py:148
  114.6 0.6 copy-start.6
  115.2 162.1 %reduce-scatter.3.cloned.1.call-start = ((), (), s32[]{:S(2)}) async-start(), calls=%async_computation.11 | async-start | bytes 1179648 | tf_op jit(solution)/shard_map/reduce_scatter | solution.py:151
  148.2 6.8 %copy-start.2 = (pred[256,4096]{1,0:T(8,128)(4,1)S(1)}, pred[256,4096]{1,0:T(8,128)(4,1)}, u32[]{:S(2)}) copy-start(pred[256,4096]{1,0:T(8,128)(4,1)} %fusion.7) | copy-start | bytes 3145732
  151.8 3.2 copy-start.1
  201.0 76.3 %copy-start.8 = (bf16[256,256]{1,0:T(8,128)(2,1)S(1)}, bf16[256,256]{1,0:T(8,128)(2,1)}, u32[]{:S(2)}) copy-start(bf16[256,256]{1,0:T(8,128)(2,1)} %param.14) | copy-start | bytes 393220
  201.0 77.9 %copy-start.10 = (s32[256,6]{0,1:T(8,128)S(1)}, s32[256,6]{0,1:T(8,128)}, u32[]{:S(2)}) copy-start(s32[256,6]{0,1:T(8,128)} %param.27) | copy-start | bytes 18436
  240.9 77.9 %copy-start.11 = (f32[2048]{0:T(1024)S(1)}, f32[2048]{0:T(1024)}, u32[]{:S(2)}) copy-start(f32[2048]{0:T(1024)} %param.16) | copy-start | bytes 24580
  243.6 73.6 %all-gather.18.cloned.1.call-start = ((), (), s32[]{:S(2)}) async-start(), calls=%async_computation.12 | async-start | bytes 1179648 | tf_op jit(solution)/shard_map/all_gather | solution.py:155
  374.8 7.5 %copy-start.15 = (bf16[2048,64]{0,1:T(8,128)(2,1)S(1)}, bf16[2048,64]{0,1:T(8,128)(2,1)}, u32[]{:S(2)}) copy-start(bf16[2048,64]{0,1:T(8,128)(2,1)} %param.19) | copy-start | bytes 786436
  374.8 41.5 %all-to-all-start.3 = ((bf16[16,40,2048]{2,1,0:T(8,128)(2,1)}), bf16[16,40,2048]{2,1,0:T(8,128)(2,1)}, u32[]{:S(2)}, u32[]{:S(2)}) async-start(bf16[16,40,2048]{2,1,0:T(8,128)(2,1)} %bitcast.95), calls=%async_computation.4 | async-start | bytes 5242880 | tf_op jit(solution)/shard_map/all_to_all | solution.py:204
  382.2 79.2 %reduce-scatter.5.cloned.1.call-start = ((), (), s32[]{:S(2)}) async-start(), calls=%async_computation.13 | async-start | bytes 1179648 | tf_op jit(solution)/shard_map/reduce_scatter | solution.py:208
  382.3 2.1 copy-start.3
  420.4 41.0 %copy-start.4 = (bf16[256,256]{1,0:T(8,128)(2,1)S(1)}, bf16[256,256]{1,0:T(8,128)(2,1)}, u32[]{:S(2)}) copy-start(bf16[256,256]{1,0:T(8,128)(2,1)} %add_convert_fusion.1) | copy-start | bytes 393220
  420.4 42.6 %copy-start.16 = (s32[8]{0:T(128)S(1)}, s32[8]{0:T(128)}, u32[]{:S(2)}) copy-start(s32[8]{0:T(128)} %param.25) | copy-start | bytes 100
  420.4 42.8 %copy-start.13 = (s32[8]{0:T(128)S(1)}, s32[8]{0:T(128)}, u32[]{:S(2)}) copy-start(s32[8]{0:T(128)} %param.26) | copy-start | bytes 100
  420.4 43.1 %copy-start.7 = (bf16[8,256,16]{1,2,0:T(8,128)(2,1)S(1)}, bf16[8,256,16]{1,2,0:T(8,128)(2,1)}, u32[]{:S(2)}) copy-start(bf16[8,256,16]{1,2,0:T(8,128)(2,1)} %copy-done.6) | copy-start | bytes 196612
  426.5 89.5 %all-gather.20.cloned.1.call-start = ((), (), s32[]{:S(2)}) async-start(), calls=%async_computation.14 | async-start | bytes 2228224 | tf_op jit(solution)/shard_map/all_gather | solution.py:213
  463.4 55.6 %copy-start.5 = (bf16[16,8,512]{2,0,1:T(8,128)(2,1)S(1)}, bf16[16,8,512]{2,0,1:T(8,128)(2,1)}, u32[]{:S(2)}) copy-start(bf16[16,8,512]{2,0,1:T(8,128)(2,1)} %all_to_all.45) | copy-start | bytes 393220
Sparse Core Ops, SparseCore 0:
  9.6 34.6 all-gather.7
  46.7 52.6 all-gather.9
  104.3 43.7 all-gather.11
  151.0 43.7 all-gather.13
  197.1 43.7 all-gather.15
  243.7 33.5 reduce-scatter.2
  279.4 37.7 all-gather.17
  426.6 34.7 reduce-scatter.4
  464.4 51.4 all-gather.19
where the time goes:
time: 531 us; the launch traced here: 526 us
  waiting for transfers between devices  374 us (70%)
  blocking collectives  52.8 us (10%)
  matrix products  45.5 us (9%)
  other arithmetic  19 us (4%)
  between operations  14.2 us (3%)
  starting transfers between devices  12.9 us (2%)
  local copies, waits for them, and re-layouts  8 us (2%)
    all_gather x1, waiting for transfers between devices, on_device(): lax.all_gather(qkv_block, 'row', axis=0, tiled=True)  53.1 us
    all_gather x1, waiting for transfers between devices, on_device(): shard_rows = lax.all_gather(layer_out, 'row', axis=0, tiled=True)  51.7 us
    all_to_all x1, blocking collectives, on_device(): lax.all_to_all(outgoing, 'row', split_axis=0, concat_axis=0, tiled=True)  43.4 us
    all_gather x1, waiting for transfers between devices, on_device(): lax.all_gather(out_block, 'row', axis=1, tiled=True)  39.9 us
    all_gather x1, waiting for transfers between devices, on_device(): value_piece = lax.all_gather(value_rows, 'row', axis=0, tiled=True)  37.2 us
    all_gather x1, waiting for transfers between devices, on_device(): full_resid = lax.all_gather(resid, 'col', axis=1, tiled=True)  37 us
    reduce_scatter x1, waiting for transfers between devices, on_device(): lax.psum_scatter((routed_part + shared_part).astype(jnp.bfloat16), 'col',...  34.9 us
    reduce_scatter x1, waiting for transfers between devices, on_device(): lax.psum_scatter(attn_terms.astype(jnp.bfloat16), 'col', scatter_dimensio...  33.6 us
  transfers between devices with their start and end apart: 11, of which 11 were waited for; matrix products, arithmetic and copies ran while one was open for 6% of the time, Pallas kernels for 0%

commit v1 on v0

v1 whole, which is shorter than its diff:
```python
import jax
import jax.numpy as jnp
from jax import lax
from jax.sharding import Mesh
from jax.sharding import PartitionSpec as P

D = 2048
HEAD_DIM = 128
TOP = 6
FIRST_LONG = 1920

ROW = ("zh", "y", "k")
COL = ("zl", "x")

epsilon = 1e-06
rope_base = 600000.0
masked_score = -1e30


def prompt_tables(lengths, order, positions):
    prompt_ids = jnp.arange(lengths.shape[0], dtype=jnp.int32)
    picked = order[:, None] == prompt_ids[None, :]
    packed_len = jnp.sum(jnp.where(picked, lengths[None, :], 0), axis=1)
    packed_end = jnp.cumsum(packed_len)
    packed_start = packed_end - packed_len
    request_start = jnp.cumsum(lengths) - lengths
    segment = jnp.sum((positions[:, None] >= packed_end[None, :]).astype(jnp.int32), axis=1)
    onehot = segment[:, None] == prompt_ids[None, :]
    within = positions - jnp.sum(jnp.where(onehot, packed_start[None, :], 0), axis=1)
    request = jnp.sum(jnp.where(onehot, order[None, :], 0), axis=1)
    offset = jnp.sum(
        jnp.where(request[:, None] == prompt_ids[None, :], request_start[None, :], 0), axis=1
    )
    return (segment, within, within + offset)


def rms_scale(values, gain):
    wide = values.astype(jnp.float32)
    return wide * lax.rsqrt(jnp.mean(wide * wide, axis=-1, keepdims=True) + epsilon) * gain


def rotary(values, within):
    half_dim = values.shape[-1] // 2
    inverse = rope_base ** (-jnp.arange(half_dim, dtype=jnp.float32) * 2.0 / values.shape[-1])
    angles = within.astype(jnp.float32)[:, None] * inverse[None, :]
    cosine = jnp.cos(angles)
    sine_part = jnp.sin(angles)
    lower = values[..., :half_dim]
    upper = values[..., half_dim:]
    return jnp.concatenate(
        [lower * cosine - upper * sine_part, upper * cosine + lower * sine_part], axis=-1
    )


def server_columns(trainer_rows, groups):
    height = trainer_rows.shape[0]
    kv_count = groups // 2
    query_part = trainer_rows[:, : 2 * groups * HEAD_DIM].reshape(height, groups, 2 * HEAD_DIM)
    key_part = trainer_rows[:, 2 * groups * HEAD_DIM : (2 * groups + kv_count) * HEAD_DIM].reshape(
        height, kv_count, 1, HEAD_DIM
    )
    value_part = trainer_rows[:, (2 * groups + kv_count) * HEAD_DIM :].reshape(
        height, kv_count, 1, HEAD_DIM
    )
    key_part = jnp.broadcast_to(key_part, (height, kv_count, 2, HEAD_DIM)).reshape(
        height, groups, HEAD_DIM
    )
    value_part = jnp.broadcast_to(value_part, (height, kv_count, 2, HEAD_DIM)).reshape(
        height, groups, HEAD_DIM
    )
    joined = jnp.concatenate([query_part, key_part, value_part], axis=2)
    return joined.reshape(height, groups * 4 * HEAD_DIM).astype(jnp.bfloat16)


def to_all(block, axes, count):
    copies = jnp.broadcast_to(block[None], (count,) + block.shape)
    return lax.all_to_all(copies, axes, 0, 0, tiled=True)


def core_swap(block):
    return lax.ppermute(block, "k", [(0, 1), (1, 0)])


def col_gather(block, col_index):
    count = 8
    height, width = block.shape
    whole = jnp.zeros((height, count * width), block.dtype)
    for step in range(count):
        if step == 0:
            piece = block
        else:
            piece = lax.ppermute(block, COL, [(i, i ^ step) for i in range(count)])
        whole = lax.dynamic_update_slice(whole, piece, (0, (col_index ^ step) * width))
    return whole


def on_device(
    tokens,
    attn_gain,
    mlp_gain,
    trainer_qkv,
    trainer_out,
    router,
    shared_gate,
    shared_up,
    shared_down,
    expert_gate_up,
    expert_down,
    lengths,
    order,
    routes,
):
    tok_rows = tokens.shape[0]
    row_count, col_count = 16, 8
    zh_index = lax.axis_index("zh")
    y_index = lax.axis_index("y")
    k_index = lax.axis_index("k")
    row_index = lax.axis_index(ROW)
    col_index = lax.axis_index(COL)
    first = row_index * tok_rows
    local = jnp.arange(tok_rows, dtype=jnp.int32)

    qkv_block = lax.all_to_all(
        server_columns(trainer_qkv, col_count).reshape(16, col_count, 512).transpose(1, 0, 2),
        COL, 0, 0, tiled=True,
    ).reshape(128, 512)
    full_tokens = col_gather(tokens, col_index)
    qkv_mine = to_all(qkv_block, ("zh", "y"), 8)
    qkv_other = core_swap(qkv_mine)

    out_block = lax.all_to_all(
        trainer_out.astype(jnp.bfloat16).reshape(col_count, 256, 16), COL, 0, 0, tiled=True
    ).transpose(1, 0, 2).reshape(256, 128)
    out_mine = to_all(out_block, ("zh", "y"), 8)
    out_other = core_swap(out_mine)

    seg_query, within_query, _ = prompt_tables(lengths, order, first + local)
    normed = rms_scale(full_tokens, attn_gain).astype(jnp.bfloat16)
    normed4 = normed.reshape(tok_rows, 8, 2, 128)
    mine_in = jnp.where(k_index == 0, normed4[:, :, 0], normed4[:, :, 1]).reshape(tok_rows, 1024)
    other_in = jnp.where(k_index == 0, normed4[:, :, 1], normed4[:, :, 0]).reshape(tok_rows, 1024)
    projected = jnp.dot(
        mine_in, qkv_mine.reshape(1024, 512), preferred_element_type=jnp.float32
    ) + jnp.dot(other_in, qkv_other.reshape(1024, 512), preferred_element_type=jnp.float32)
    queries = projected[:, : 2 * HEAD_DIM].reshape(tok_rows, 2, HEAD_DIM).transpose(1, 0, 2)
    queries = rotary(queries, within_query).astype(jnp.bfloat16)
    key_rows = rotary(projected[:, 2 * HEAD_DIM : 3 * HEAD_DIM], within_query).astype(jnp.bfloat16)
    value_rows = projected[:, 3 * HEAD_DIM :].astype(jnp.bfloat16)
    cache_out = jnp.where(col_index % 2 == 0, key_rows, value_rows)

    kv_rows = jnp.concatenate([key_rows, value_rows], axis=1)
    tail = kv_rows[128:]
    head_sent = sum(lax.ppermute(tail, ROW, [(7, to)]) for to in (9, 11, 13, 15))
    kv_mine = to_all(kv_rows, "y", 4)
    kv_other = core_swap(kv_mine)
    kv_head = head_sent + core_swap(head_sent)
    kv_all = jnp.concatenate(
        [kv_mine.reshape(1024, 256), kv_other.reshape(1024, 256), kv_head], axis=0
    )
    span = jnp.arange(1024, dtype=jnp.int32)
    base_pos = zh_index * 2048 + (span // 256) * 512 + span % 256
    head_pos = FIRST_LONG + jnp.arange(128, dtype=jnp.int32)
    key_pos = jnp.concatenate(
        [
            base_pos + k_index * 256,
            base_pos + (1 - k_index) * 256,
            jnp.where(zh_index == 1, head_pos, jnp.int32(1 << 20)),
        ]
    )
    seg_key, _, _ = prompt_tables(lengths, order, key_pos)
    query_pos = first + local
    allowed = (seg_key[None, :] == seg_query[:, None]) & (key_pos[None, :] <= query_pos[:, None])
    scale = HEAD_DIM ** (-0.5)
    scores = (
        jnp.einsum(
            "hqd,kd->hqk", queries, kv_all[:, :HEAD_DIM], preferred_element_type=jnp.float32
        )
        * scale
    )
    scores = jnp.where(allowed[None], scores, masked_score)
    peak = jnp.max(scores, axis=2)
    numerators = jnp.where(allowed[None], jnp.exp(scores - peak[..., None]), 0.0)
    denominator = jnp.sum(numerators, axis=2)
    summed = jnp.einsum(
        "hqk,kd->hqd",
        numerators.astype(jnp.bfloat16),
        kv_all[:, HEAD_DIM:],
        preferred_element_type=jnp.float32,
    )
    attended = (
        (summed / denominator[..., None])
        .transpose(1, 0, 2)
        .reshape(tok_rows, 2 * HEAD_DIM)
        .astype(jnp.bfloat16)
    )
    terms = jnp.concatenate(
        [
            jnp.einsum("th,fhn->ftn", attended, out_mine, preferred_element_type=jnp.float32),
            jnp.einsum("th,fhn->ftn", attended, out_other, preferred_element_type=jnp.float32),
        ],
        axis=2,
    ).astype(jnp.bfloat16)
    got = lax.all_to_all(terms, COL, 0, 0, tiled=True)
    attn_sum = jnp.sum(got.astype(jnp.float32), axis=0)
    attn_part = jnp.where(k_index == 0, attn_sum, jnp.roll(attn_sum, 128, axis=1))
    resid = (tokens.astype(jnp.float32) + attn_part).astype(jnp.bfloat16)

    full_resid = col_gather(resid, col_index)
    mlp_in = rms_scale(full_resid, mlp_gain).astype(jnp.bfloat16)
    logits = jnp.dot(mlp_in, router, preferred_element_type=jnp.float32)
    router_probs = jax.nn.softmax(logits, axis=-1)
    n_experts = row_count * col_count // 2
    expert_ids = jnp.arange(n_experts, dtype=jnp.int32)
    chosen = jnp.sum(
        jnp.where(routes[:, :, None] == expert_ids[None, None, :], router_probs[:, None, :], 0.0),
        axis=-1,
    )
    route_weight = (chosen / jnp.sum(chosen, axis=-1, keepdims=True)).astype(jnp.bfloat16)
    shared_hidden = (
        jax.nn.silu(jnp.dot(mlp_in, shared_gate, preferred_element_type=jnp.float32))
        * jnp.dot(mlp_in, shared_up, preferred_element_type=jnp.float32)
    ).astype(jnp.bfloat16)
    capacity = 40
    targets = jnp.arange(row_count, dtype=jnp.int32) * (col_count // 2) + col_index // 2
    matches = routes[:, :, None] == targets[None, None, :]
    member = jnp.any(matches, axis=1)
    slot_of = jnp.cumsum(member.astype(jnp.int32), axis=0) - 1
    chosen_weight = jnp.sum(
        jnp.where(matches, route_weight[:, :, None].astype(jnp.float32), 0.0), axis=1
    )
    placing = member[:, :, None] & (
        slot_of[:, :, None] == jnp.arange(capacity, dtype=jnp.int32)[None, None, :]
    )
    picker = placing.astype(jnp.bfloat16).reshape(tok_rows, row_count * capacity)
    combiner = (
        (placing.astype(jnp.float32) * chosen_weight[:, :, None])
        .astype(jnp.bfloat16)
        .reshape(tok_rows, row_count * capacity)
    )
    outgoing = jnp.einsum("ts,td->sd", picker, mlp_in, preferred_element_type=jnp.float32).astype(
        jnp.bfloat16
    )
    outgoing = outgoing.reshape(row_count, capacity, D)
    gate_up_slab = expert_gate_up[0]
    down_slab = expert_down[0]
    half_units = down_slab.shape[0]
    arrived = lax.all_to_all(outgoing, ROW, split_axis=0, concat_axis=0, tiled=True)
    flat = arrived.reshape(-1, D)
    gate_up = jnp.dot(flat, gate_up_slab, preferred_element_type=jnp.float32)
    hidden = (jax.nn.silu(gate_up[:, :half_units]) * gate_up[:, half_units:]).astype(jnp.bfloat16)
    result = (
        jnp.dot(hidden, down_slab, preferred_element_type=jnp.float32)
        .astype(jnp.bfloat16)
        .reshape(arrived.shape)
    )
    came_back = lax.all_to_all(result, ROW, split_axis=0, concat_axis=0, tiled=True)
    came_back = came_back.reshape(row_count * capacity, D)
    parts = jnp.stack(
        [
            jnp.dot(
                combiner, came_back[:, f * 256 : (f + 1) * 256], preferred_element_type=jnp.float32
            )
            + jnp.dot(
                shared_hidden,
                shared_down[:, f * 256 : (f + 1) * 256],
                preferred_element_type=jnp.float32,
            )
            for f in range(col_count)
        ]
    ).astype(jnp.bfloat16)
    layer_got = lax.all_to_all(parts, COL, 0, 0, tiled=True)
    layer_part = jnp.sum(layer_got.astype(jnp.float32), axis=0)
    layer_out = (resid.astype(jnp.float32) + layer_part).astype(jnp.bfloat16)

    received = []
    for step in range(4):
        pairs = [(s, 4 + (s + step) % 4) for s in range(4)]
        if step == 0:
            pairs += [(4 + s, s) for s in range(4)]
        received.append(lax.ppermute(layer_out, ("zh", "y"), pairs))
    late = lax.ppermute(
        layer_out[128:], ROW, [(7 + i, i) for i in range(0, 8, 2)] + [(15, 8)]
    )
    mine_rows = jnp.concatenate(received, axis=0)
    other_rows = core_swap(mine_rows)
    sources = jnp.concatenate([mine_rows, other_rows, late], axis=0)
    step_of = span // 256
    from_row = jnp.where(
        zh_index == 1,
        ((y_index - step_of) % 4) * 2,
        jnp.where(step_of == 0, 8 + y_index * 2, jnp.int32(1 << 12)),
    )
    late_from = jnp.where(
        k_index == 1, 1 << 12, jnp.where(zh_index == 0, row_index + 7, jnp.where(row_index == 8, 15, 1 << 12))
    )
    source_pos = jnp.concatenate(
        [
            (from_row + k_index) * 256 + span % 256,
            (from_row + 1 - k_index) * 256 + span % 256,
            late_from * 256 + 128 + jnp.arange(128, dtype=jnp.int32),
        ]
    )
    _, _, dest = prompt_tables(lengths, order, source_pos)
    dest = jnp.where(source_pos < row_count * tok_rows, dest, -1)
    mover = (dest[None, :] == (first + local)[:, None]).astype(jnp.bfloat16)
    hidden_states = jnp.dot(mover, sources, preferred_element_type=jnp.float32).astype(jnp.bfloat16)
    return (hidden_states, cache_out, qkv_block, out_block)


def solution(mesh):
    fine = Mesh(mesh.devices.reshape(2, 4, 2, 2, 4), ROW + COL)
    in_specs = (
        P(ROW, COL),
        P(),
        P(),
        P(ROW + COL, None),
        P(None, ROW + COL),
        P(),
        P(None, COL),
        P(None, COL),
        P(COL, None),
        P(ROW + COL, None, None),
        P(ROW + COL, None, None),
        P(),
        P(),
        P(ROW, None),
    )
    out_specs = (P(ROW, COL), P(ROW, COL), P(ROW, COL), P(COL, ROW))
    return jax.shard_map(
        on_device, mesh=fine, in_specs=in_specs, out_specs=out_specs, check_vma=False
    )
```

time: 531 us -> 329 us (0.62)
  waiting for transfers between devices: 374 us -> 89 us
  starting transfers between devices: 12.9 us -> 83.2 us
  local copies, waits for them, and re-layouts: 8 us -> 32.3 us
  between operations: 14.2 us -> 1.46 us
  blocking collectives: 52.8 us -> 40.1 us
  other arithmetic: 19 us -> 30.9 us
    all_gather x7 -> x0, waiting for transfers between devices: 274 us -> none  [the longest x1 53.1 us: on_device(): lax.all_gather(qkv_block, 'row', axis=0, tiled=True)]
    reduce_scatter x2 -> x0, waiting for transfers between devices: 68.5 us -> none  [the longest x1 34.9 us: on_device(): lax.psum_scatter((routed_part + shared_part).astype(jnp.bfloat16), 'col',...]
    ppermute x0 -> x28, starting transfers between devices: none -> 40.4 us  [the longest x14 19.4 us: col_gather(): piece = lax.ppermute(block, COL, [(i, i ^ step) for i in range(count)])]
    all_to_all x2 -> x8, waiting for transfers between devices: 30.2 us -> 61.6 us  [the longest x1 27.7 us: on_device(): lax.all_to_all(result, ROW, split_axis=0, concat_axis=0, tiled=True)]
    all_to_all x2 -> x8, starting transfers between devices: 12.6 us -> 42.8 us  [the longest x3 15.9 us: to_all(): return lax.all_to_all(copies, axes, 0, 0, tiled=True)]
    ppermute x0 -> x28, waiting for transfers between devices: none -> 27.4 us  [the longest x14 12.2 us: col_gather(): piece = lax.ppermute(block, COL, [(i, i ^ step) for i in range(count)])]
    dynamic_update_slice x0 -> x15, local copies, waits for them, and re-layouts: none -> 12.7 us  [col_gather(): lax.dynamic_update_slice(whole, piece, (0, (col_index ^ step) * width))]
    all_to_all x2 -> x1, blocking collectives: 52.8 us -> 40.1 us  [on_device(): lax.all_to_all(outgoing, ROW, split_axis=0, concat_axis=0, tiled=True)]
  transfers between devices with their start and end apart: 11 -> 36, of which waited for: 11 -> 11; matrix products, arithmetic and copies ran while one was open for 6% -> 20% of each run, Pallas kernels for 0% -> 0%
where the time goes in v1:
time: 329 us; the launch traced here: 325 us
  waiting for transfers between devices  89 us (27%)
  starting transfers between devices  83.2 us (25%)
  matrix products  47.6 us (14%)
  blocking collectives  40.1 us (12%)
  local copies, waits for them, and re-layouts  32.3 us (10%)
  other arithmetic  30.9 us (9%)
    all_to_all x1, blocking collectives, on_device(): lax.all_to_all(outgoing, ROW, split_axis=0, concat_axis=0, tiled=True)  40.1 us
    all_to_all x1, waiting for transfers between devices, on_device(): lax.all_to_all(result, ROW, split_axis=0, concat_axis=0, tiled=True)  27.7 us
    ppermute x14, starting transfers between devices, col_gather(): piece = lax.ppermute(block, COL, [(i, i ^ step) for i in range(count)])  19.4 us
    all_to_all x3, starting transfers between devices, to_all(): return lax.all_to_all(copies, axes, 0, 0, tiled=True)  15.9 us
    all_to_all x1, waiting for transfers between devices, on_device(): layer_got = lax.all_to_all(parts, COL, 0, 0, tiled=True)  14 us
    dynamic_update_slice x15, local copies, waits for them, and re-layouts, col_gather(): lax.dynamic_update_slice(whole, piece, (0, (col_index ^ step) * width))  12.7 us
    all_to_all x1, waiting for transfers between devices, on_device(): got = lax.all_to_all(terms, COL, 0, 0, tiled=True)  12.3 us
    ppermute x14, waiting for transfers between devices, col_gather(): piece = lax.ppermute(block, COL, [(i, i ^ step) for i in range(count)])  12.2 us
  transfers between devices with their start and end apart: 36, of which 11 were waited for; matrix products, arithmetic and copies ran while one was open for 20% of the time, Pallas kernels for 0%

profile of v1, /device:TPU:97, one launch (start us, length us, event | category | flops | bytes accessed | tf_op | source)
XLA Modules:
  0.0 324.7 jit_solution(10407899351055130443)
XLA Ops:
  1.8 2.4 collective-permute-start.6
  5.9 2.7 collective-permute-start.1
  11.3 4.6 %all-to-all-start = ((bf16[8,16,512]{2,1,0:T(8,128)(2,1)}), bf16[8,16,512]{2,1,0:T(8,128)(2,1)S(1)}, u32[]{:S(2)}, u32[]{:S(2)}) async-start(bf16[8,16,512]{2,1,0:T(8,128)(2,1)} %maximum_bitcast_fusion), calls=%async_computation | async-start | bytes 262144 | tf_op jit(solution)/shard_map/all_to_all | solution.py:123
  21.8 6.9 %all-to-all-start.1 = ((bf16[8,128,512]{2,1,0:T(8,128)(2,1)}), bf16[8,128,512]{2,1,0:T(8,128)(2,1)}, u32[]{:S(2)}, u32[]{:S(2)}) async-start(bf16[8,128,512]{2,1,0:T(8,128)(2,1)} %broadcast_in_dim.224), calls=%async_computation.1 | async-start | bytes 2097152 | tf_op jit(solution)/shard_map/all_to_all | solution.py:77
  29.8 2.4 collective-permute-start.2
  36.3 8.5 %collective-permute-done.3 = bf16[256,256]{0,1:T(8,128)(2,1)S(1)} collective-permute-done((bf16[256,256]{0,1:T(8,128)(2,1)S(1)}, bf16[256,256]{0,1:T(8,128)(2,1)S(1)}, u32[]{:S(2)}, u32[]{:S(2)}) %collective-permute-start.3) | collective-permute-done | bytes 131104 | tf_op jit(solution)/shard_map/ppermute | solution.py:92
  48.4 4.4 %all-to-all-start.3 = ((bf16[8,256,16]{1,2,0:T(8,128)(2,1)}), bf16[8,256,16]{1,2,0:T(8,128)(2,1)S(1)}, u32[]{:S(2)}, u32[]{:S(2)}) async-start(bf16[8,256,16]{1,2,0:T(8,128)(2,1)} %bitcast.184), calls=%async_computation.3 | async-start | bytes 131072 | tf_op jit(solution)/shard_map/all_to_all | solution.py:131
  52.8 2.2 collective-permute-start.7
  63.5 4.1 %all-to-all-start.2 = ((bf16[4,256,256]{2,1,0:T(8,128)(2,1)}), bf16[4,256,256]{2,1,0:T(8,128)(2,1)}, u32[]{:S(2)}, u32[]{:S(2)}) async-start(bf16[4,256,256]{2,1,0:T(8,128)(2,1)} %broadcast_in_dim.227), calls=%async_computation.2 | async-start | bytes 1048576 | tf_op jit(solution)/shard_map/all_to_all | solution.py:77
  69.7 7.6 %all-to-all-done.2 = bf16[4,256,256]{2,1,0:T(8,128)(2,1)} async-done(((bf16[4,256,256]{2,1,0:T(8,128)(2,1)}), bf16[4,256,256]{2,1,0:T(8,128)(2,1)}, u32[]{:S(2)}, u32[]{:S(2)}) %all-to-all-start.2) | async-done | bytes 524320 | tf_op jit(solution)/shard_map/all_to_all | solution.py:77
  78.2 4.9 %all-to-all-start.4 = ((bf16[8,256,128]{1,2,0:T(8,128)(2,1)}), bf16[8,256,128]{1,2,0:T(8,128)(2,1)}, u32[]{:S(2)}, u32[]{:S(2)}) async-start(bf16[8,256,128]{1,2,0:T(8,128)(2,1)} %broadcast_in_dim.231), calls=%async_computation.4 | async-start | bytes 1048576 | tf_op jit(solution)/shard_map/all_to_all | solution.py:77
  83.1 2.0 compare_and_fusion
  93.2 7.2 %collective-permute-done.9 = bf16[128,256]{1,0:T(8,128)(2,1)} collective-permute-done((bf16[128,256]{1,0:T(8,128)(2,1)}, bf16[128,256]{1,0:T(8,128)(2,1)}, u32[]{:S(2)}, u32[]{:S(2)}) %collective-permute-start.9) | collective-permute-done | bytes 65568 | tf_op jit(solution)/shard_map/ppermute | solution.py:153
  103.4 2.4 pad_maximum_fusion
  105.8 3.8 %fusion.144 = f32[2,256]{1,0:T(2,128)S(1)} fusion(pred[256,2176]{1,0:T(8,128)(4,1)} %compare_and_fusion, bf16[2176,256]{1,0:T(8,128)(2,1)} %pad_maximum_fusion, bf16[2,256,64]{2,1,0:T(8,128)(2,1)S(1)} %copy-done.12, bf16[2,256,64]{2,1,0:T(8,128)(2,1)S(1)} %copy-done.11), kind=kOutput, calls=%fused_computation.246 | convolution fusion | flops 291047552 | bytes 1804288 | tf_op jit(solution)/shard_map/sub | solution.py:182
  109.6 4.0 %fusion.34 = bf16[256,2,128]{0,2,1:T(8,128)(2,1)S(1)} fusion(bf16[2176,256]{1,0:T(8,128)(2,1)} %pad_maximum_fusion, f32[256,2]{0,1:T(2,128)S(1)} %bitcast.209, pred[256,2176]{1,0:T(8,128)(4,1)} %compare_and_fusion, bf16[2,256,64]{2,1,0:T(8,128)(2,1)S(1)} %copy-done.12, bf16[2,256,64]{2,1,0:T(8,128)(2,1)S(1)} %copy-done.11), kind=kOutput, calls=%fused_computation.51 | convolution fusion | flops 576391808 | bytes 2492416 | tf_op jit(solution)/shard_map/hqk,kd->hqd/dot_general | solution.py:184
  117.5 5.1 %all-to-all-start.5 = ((bf16[8,256,256]{1,2,0:T(8,128)(2,1)}), bf16[8,256,256]{1,2,0:T(8,128)(2,1)}, u32[]{:S(2)}, u32[]{:S(2)}) async-start(bf16[8,256,256]{1,2,0:T(8,128)(2,1)} %pad_maximum_fusion.1), calls=%async_computation.5 | async-start | bytes 2097152 | tf_op jit(solution)/shard_map/all_to_all | solution.py:203
  125.1 12.3 %all-to-all-done.5 = bf16[8,256,256]{1,2,0:T(8,128)(2,1)} async-done(((bf16[8,256,256]{1,2,0:T(8,128)(2,1)}), bf16[8,256,256]{1,2,0:T(8,128)(2,1)}, u32[]{:S(2)}, u32[]{:S(2)}) %all-to-all-start.5) | async-done | bytes 1048608 | tf_op jit(solution)/shard_map/all_to_all | solution.py:203
  142.8 3.1 collective-permute-start.20
  161.1 2.3 convolution_convert_fusion.1
  163.5 40.1 %all_to_all.45 = bf16[16,40,2048]{2,1,0:T(8,128)(2,1)S(1)} all-to-all(bf16[16,40,2048]{2,1,0:T(8,128)(2,1)S(1)} %bitcast.185), channel_id=1, replica_groups=mesh['zh'=2,'y'=4,'k'=2,'zl'=2,'x'=4] {'zh','y','k'}, dimensions={0} | all-to-all | bytes 5242880 | tf_op jit(solution)/shard_map/all_to_all | solution.py:247
  203.6 4.2 %fusion.1 = f32[640,1408]{1,0:T(8,128)S(1)} fusion(bf16[640,2048]{1,0:T(8,128)(2,1)S(1)} %bitcast.189, bf16[1,2048,1408]{2,1,0:T(8,128)(2,1)S(1)} %bitcast.206), kind=kOutput, calls=%fused_computation.1 | convolution fusion | flops 3690987520 | bytes 11993088 | tf_op jit(solution)/shard_map/dot_general | solution.py:249
  207.8 3.8 %convolution_convert_fusion = bf16[640,2048]{1,0:T(8,128)(2,1)} fusion(bf16[1,704,2048]{2,1,0:T(8,128)(2,1)S(1)} %copy-done, f32[640,1408]{1,0:T(8,128)S(1)} %fusion.1), kind=kOutput, calls=%fused_computation.8 | convolution fusion | flops 1849507840 | bytes 9437184 | tf_op jit(solution)/shard_map/dot_general | solution.py:252
  211.7 7.4 %all-to-all-start.7 = ((bf16[16,40,2048]{2,1,0:T(8,128)(2,1)}), bf16[16,40,2048]{2,1,0:T(8,128)(2,1)}, u32[]{:S(2)}, u32[]{:S(2)}) async-start(bf16[16,40,2048]{2,1,0:T(8,128)(2,1)} %bitcast.188), calls=%async_computation.7 | async-start | bytes 5242880 | tf_op jit(solution)/shard_map/all_to_all | solution.py:256
  221.5 2.0 fusion.135
  223.6 1.9 multiply_convert_fusion
  225.5 27.7 %all-to-all-done.7 = bf16[16,40,2048]{2,1,0:T(8,128)(2,1)} async-done(((bf16[16,40,2048]{2,1,0:T(8,128)(2,1)}), bf16[16,40,2048]{2,1,0:T(8,128)(2,1)}, u32[]{:S(2)}, u32[]{:S(2)}) %all-to-all-start.7) | async-done | bytes 2621472 | tf_op jit(solution)/shard_map/all_to_all | solution.py:256
  271.0 5.2 %all-to-all-start.8 = ((bf16[8,256,256]{2,1,0:T(8,128)(2,1)}), bf16[8,256,256]{2,1,0:T(8,128)(2,1)}, u32[]{:S(2)}, u32[]{:S(2)}) async-start(bf16[8,256,256]{2,1,0:T(8,128)(2,1)} %fusion.41), calls=%async_computation.8 | async-start | bytes 2097152 | tf_op jit(solution)/shard_map/all_to_all | solution.py:271
  276.9 14.0 %all-to-all-done.8 = bf16[8,256,256]{2,1,0:T(8,128)(2,1)} async-done(((bf16[8,256,256]{2,1,0:T(8,128)(2,1)}), bf16[8,256,256]{2,1,0:T(8,128)(2,1)}, u32[]{:S(2)}, u32[]{:S(2)}) %all-to-all-start.8) | async-done | bytes 1048608 | tf_op jit(solution)/shard_map/all_to_all | solution.py:271
  297.4 5.9 %collective-permute-start.22 = (bf16[256,256]{0,1:T(8,128)(2,1)S(1)}, bf16[256,256]{0,1:T(8,128)(2,1)S(1)}, u32[]{:S(2)}, u32[]{:S(2)}) collective-permute-start(bf16[256,256]{0,1:T(8,128)(2,1)S(1)} %add_convert_fusion), channel_id=1, source_target_pairs={{0,64},{16,80},{32,96},{48,112},{64,0},{80,16},{96,32},{112,48},{1... | collective-permute-start | bytes 393224 | tf_op jit(solution)/shard_map/ppermute | solution.py:280
  305.8 3.7 %collective-permute-done.23 = bf16[256,256]{0,1:T(8,128)(2,1)S(1)} collective-permute-done((bf16[256,256]{0,1:T(8,128)(2,1)S(1)}, bf16[256,256]{0,1:T(8,128)(2,1)S(1)}, u32[]{:S(2)}, u32[]{:S(2)}) %collective-permute-start.23) | collective-permute-done | bytes 131104 | tf_op jit(solution)/shard_map/ppermute | solution.py:280
  309.4 3.3 %collective-permute-done.22 = bf16[256,256]{0,1:T(8,128)(2,1)S(1)} collective-permute-done((bf16[256,256]{0,1:T(8,128)(2,1)S(1)}, bf16[256,256]{0,1:T(8,128)(2,1)S(1)}, u32[]{:S(2)}, u32[]{:S(2)}) %collective-permute-start.22) | collective-permute-done | bytes 131104 | tf_op jit(solution)/shard_map/ppermute | solution.py:280
  (254 shorter events, 110.9 us)
Async XLA Ops:
  1.8 45.9 %collective-permute-start.6 = (bf16[256,256]{0,1:T(8,128)(2,1)S(1)}, bf16[256,256]{0,1:T(8,128)(2,1)S(1)}, u32[]{:S(2)}, u32[]{:S(2)}) collective-permute-start(bf16[256,256]{0,1:T(8,128)(2,1)S(1)} %copy.137), channel_id=1, source_target_pairs={{0,7},{1,6},{2,5},{3,4},{4,3},{5,2},{6,1},{7,0},{8,15},{9,14},{10,... | collective-permute-start | bytes 393224 | tf_op jit(solution)/shard_map/ppermute | solution.py:92
  4.2 42.9 %collective-permute-start.5 = (bf16[256,256]{0,1:T(8,128)(2,1)S(1)}, bf16[256,256]{0,1:T(8,128)(2,1)S(1)}, u32[]{:S(2)}, u32[]{:S(2)}) collective-permute-start(bf16[256,256]{0,1:T(8,128)(2,1)S(1)} %copy.137), channel_id=1, source_target_pairs={{0,6},{1,7},{2,4},{3,5},{4,2},{5,3},{6,0},{7,1},{8,14},{9,15},{10,... | collective-permute-start | bytes 393224 | tf_op jit(solution)/shard_map/ppermute | solution.py:92
  5.8 39.7 %collective-permute-start.4 = (bf16[256,256]{0,1:T(8,128)(2,1)S(1)}, bf16[256,256]{0,1:T(8,128)(2,1)}, u32[]{:S(2)}, u32[]{:S(2)}) collective-permute-start(bf16[256,256]{0,1:T(8,128)(2,1)S(1)} %copy.137), channel_id=1, source_target_pairs={{0,5},{1,4},{2,7},{3,6},{4,1},{5,0},{6,3},{7,2},{8,13},{9,12},{10,... | collective-permute-start | bytes 393224 | tf_op jit(solution)/shard_map/ppermute | solution.py:92
  5.9 27.9 %collective-permute-start.1 = (bf16[256,256]{0,1:T(8,128)(2,1)S(1)}, bf16[256,256]{0,1:T(8,128)(2,1)}, u32[]{:S(2)}, u32[]{:S(2)}) collective-permute-start(bf16[256,256]{0,1:T(8,128)(2,1)S(1)} %copy.137), channel_id=1, source_target_pairs={{0,2},{1,3},{2,0},{3,1},{4,6},{5,7},{6,4},{7,5},{8,10},{9,11},{10,... | collective-permute-start | bytes 393224 | tf_op jit(solution)/shard_map/ppermute | solution.py:92
  8.6 21.2 %collective-permute-start = (bf16[256,256]{0,1:T(8,128)(2,1)S(1)}, bf16[256,256]{0,1:T(8,128)(2,1)}, u32[]{:S(2)}, u32[]{:S(2)}) collective-permute-start(bf16[256,256]{0,1:T(8,128)(2,1)S(1)} %copy.137), channel_id=1, source_target_pairs={{0,1},{1,0},{2,3},{3,2},{4,5},{5,4},{6,7},{7,6},{8,9},{9,8},{10,11... | collective-permute-start | bytes 393224 | tf_op jit(solution)/shard_map/ppermute | solution.py:92
  11.3 9.4 %all-to-all-start = ((bf16[8,16,512]{2,1,0:T(8,128)(2,1)}), bf16[8,16,512]{2,1,0:T(8,128)(2,1)S(1)}, u32[]{:S(2)}, u32[]{:S(2)}) async-start(bf16[8,16,512]{2,1,0:T(8,128)(2,1)} %maximum_bitcast_fusion), calls=%async_computation | async-start | bytes 262144 | tf_op jit(solution)/shard_map/all_to_all | solution.py:123
  21.8 26.6 %all-to-all-start.1 = ((bf16[8,128,512]{2,1,0:T(8,128)(2,1)}), bf16[8,128,512]{2,1,0:T(8,128)(2,1)}, u32[]{:S(2)}, u32[]{:S(2)}) async-start(bf16[8,128,512]{2,1,0:T(8,128)(2,1)} %broadcast_in_dim.224), calls=%async_computation.1 | async-start | bytes 2097152 | tf_op jit(solution)/shard_map/all_to_all | solution.py:77
  33.8 11.0 %collective-permute-start.3 = (bf16[256,256]{0,1:T(8,128)(2,1)S(1)}, bf16[256,256]{0,1:T(8,128)(2,1)S(1)}, u32[]{:S(2)}, u32[]{:S(2)}) collective-permute-start(bf16[256,256]{0,1:T(8,128)(2,1)S(1)} %copy.137), channel_id=1, source_target_pairs={{0,4},{1,5},{2,6},{3,7},{4,0},{5,1},{6,2},{7,3},{8,12},{9,13},{10,... | collective-permute-start | bytes 393224 | tf_op jit(solution)/shard_map/ppermute | solution.py:92
  48.4 14.2 %all-to-all-start.3 = ((bf16[8,256,16]{1,2,0:T(8,128)(2,1)}), bf16[8,256,16]{1,2,0:T(8,128)(2,1)S(1)}, u32[]{:S(2)}, u32[]{:S(2)}) async-start(bf16[8,256,16]{1,2,0:T(8,128)(2,1)} %bitcast.184), calls=%async_computation.3 | async-start | bytes 131072 | tf_op jit(solution)/shard_map/all_to_all | solution.py:131
  52.8 7.0 %collective-permute-start.7 = (bf16[8,128,512]{2,1,0:T(8,128)(2,1)}, bf16[8,128,512]{2,1,0:T(8,128)(2,1)S(1)}, u32[]{:S(2)}, u32[]{:S(2)}) collective-permute-start(bf16[8,128,512]{2,1,0:T(8,128)(2,1)} %all-to-all-done.1), channel_id=1, source_target_pairs={{0,8},{8,0},{1,9},{9,1},{2,10},{10,2},{3,11},{11,3},{4,12},{12,4},... | collective-permute-start | bytes 3145736 | tf_op jit(solution)/shard_map/ppermute | solution.py:81
  63.5 13.9 %all-to-all-start.2 = ((bf16[4,256,256]{2,1,0:T(8,128)(2,1)}), bf16[4,256,256]{2,1,0:T(8,128)(2,1)}, u32[]{:S(2)}, u32[]{:S(2)}) async-start(bf16[4,256,256]{2,1,0:T(8,128)(2,1)} %broadcast_in_dim.227), calls=%async_computation.2 | async-start | bytes 1048576 | tf_op jit(solution)/shard_map/all_to_all | solution.py:77
  78.2 14.9 %all-to-all-start.4 = ((bf16[8,256,128]{1,2,0:T(8,128)(2,1)}), bf16[8,256,128]{1,2,0:T(8,128)(2,1)}, u32[]{:S(2)}, u32[]{:S(2)}) async-start(bf16[8,256,128]{1,2,0:T(8,128)(2,1)} %broadcast_in_dim.231), calls=%async_computation.4 | async-start | bytes 1048576 | tf_op jit(solution)/shard_map/all_to_all | solution.py:77
  85.7 7.4 %collective-permute-start.12 = (bf16[128,256]{1,0:T(8,128)(2,1)}, bf16[128,256]{1,0:T(8,128)(2,1)}, u32[]{:S(2)}, u32[]{:S(2)}) collective-permute-start(bf16[128,256]{1,0:T(8,128)(2,1)} %slice.166), channel_id=1, source_target_pairs={{56,120},{57,121},{58,122},{59,123},{60,124},{61,125},{62,126},{63... | collective-permute-start | bytes 196616 | tf_op jit(solution)/shard_map/ppermute | solution.py:153
  87.0 6.2 %collective-permute-start.11 = (bf16[128,256]{1,0:T(8,128)(2,1)}, bf16[128,256]{1,0:T(8,128)(2,1)}, u32[]{:S(2)}, u32[]{:S(2)}) collective-permute-start(bf16[128,256]{1,0:T(8,128)(2,1)} %slice.166), channel_id=1, source_target_pairs={{56,104},{57,105},{58,106},{59,107},{60,108},{61,109},{62,110},{63... | collective-permute-start | bytes 196616 | tf_op jit(solution)/shard_map/ppermute | solution.py:153
  89.6 10.8 %collective-permute-start.9 = (bf16[128,256]{1,0:T(8,128)(2,1)}, bf16[128,256]{1,0:T(8,128)(2,1)}, u32[]{:S(2)}, u32[]{:S(2)}) collective-permute-start(bf16[128,256]{1,0:T(8,128)(2,1)} %slice.166), channel_id=1, source_target_pairs={{56,72},{57,73},{58,74},{59,75},{60,76},{61,77},{62,78},{63,79}} | collective-permute-start | bytes 196616 | tf_op jit(solution)/shard_map/ppermute | solution.py:153
  90.9 12.6 %collective-permute-start.8 = (bf16[4,256,256]{2,1,0:T(8,128)(2,1)}, bf16[4,256,256]{2,1,0:T(8,128)(2,1)}, u32[]{:S(2)}, u32[]{:S(2)}) collective-permute-start(bf16[4,256,256]{2,1,0:T(8,128)(2,1)} %all-to-all-done.2), channel_id=1, source_target_pairs={{0,8},{8,0},{1,9},{9,1},{2,10},{10,2},{3,11},{11,3},{4,12},{12,4},... | collective-permute-start | bytes 1572872 | tf_op jit(solution)/shard_map/ppermute | solution.py:81
  93.1 21.9 %collective-permute-start.14 = (bf16[8,256,128]{1,2,0:T(8,128)(2,1)}, bf16[8,256,128]{1,2,0:T(8,128)(2,1)}, u32[]{:S(2)}, u32[]{:S(2)}) collective-permute-start(bf16[8,256,128]{1,2,0:T(8,128)(2,1)} %all-to-all-done.4), channel_id=1, source_target_pairs={{0,8},{8,0},{1,9},{9,1},{2,10},{10,2},{3,11},{11,3},{4,12},{12,4},... | collective-permute-start | bytes 1572872 | tf_op jit(solution)/shard_map/ppermute | solution.py:81
  117.5 19.9 %all-to-all-start.5 = ((bf16[8,256,256]{1,2,0:T(8,128)(2,1)}), bf16[8,256,256]{1,2,0:T(8,128)(2,1)}, u32[]{:S(2)}, u32[]{:S(2)}) async-start(bf16[8,256,256]{1,2,0:T(8,128)(2,1)} %pad_maximum_fusion.1), calls=%async_computation.5 | async-start | bytes 2097152 | tf_op jit(solution)/shard_map/all_to_all | solution.py:203
  140.5 9.4 %collective-permute-start.16 = (bf16[256,256]{0,1:T(8,128)(2,1)S(1)}, bf16[256,256]{0,1:T(8,128)(2,1)S(1)}, u32[]{:S(2)}, u32[]{:S(2)}) collective-permute-start(bf16[256,256]{0,1:T(8,128)(2,1)S(1)} %get-tuple-element.33), channel_id=1, source_target_pairs={{0,2},{1,3},{2,0},{3,1},{4,6},{5,7},{6,4},{7,5},{8,10},{9,11},{10,... | collective-permute-start | bytes 393224 | tf_op jit(solution)/shard_map/ppermute | solution.py:92
  141.8 5.8 %collective-permute-start.15 = (bf16[256,256]{0,1:T(8,128)(2,1)S(1)}, bf16[256,256]{0,1:T(8,128)(2,1)S(1)}, u32[]{:S(2)}, u32[]{:S(2)}) collective-permute-start(bf16[256,256]{0,1:T(8,128)(2,1)S(1)} %get-tuple-element.33), channel_id=1, source_target_pairs={{0,1},{1,0},{2,3},{3,2},{4,5},{5,4},{6,7},{7,6},{8,9},{9,8},{10,11... | collective-permute-start | bytes 393224 | tf_op jit(solution)/shard_map/ppermute | solution.py:92
  142.8 15.4 %collective-permute-start.20 = (bf16[256,256]{0,1:T(8,128)(2,1)S(1)}, bf16[256,256]{0,1:T(8,128)(2,1)S(1)}, u32[]{:S(2)}, u32[]{:S(2)}) collective-permute-start(bf16[256,256]{0,1:T(8,128)(2,1)S(1)} %get-tuple-element.33), channel_id=1, source_target_pairs={{0,6},{1,7},{2,4},{3,5},{4,2},{5,3},{6,0},{7,1},{8,14},{9,15},{10,... | collective-permute-start | bytes 393224 | tf_op jit(solution)/shard_map/ppermute | solution.py:92
  145.9 11.7 %collective-permute-start.19 = (bf16[256,256]{0,1:T(8,128)(2,1)S(1)}, bf16[256,256]{0,1:T(8,128)(2,1)S(1)}, u32[]{:S(2)}, u32[]{:S(2)}) collective-permute-start(bf16[256,256]{0,1:T(8,128)(2,1)S(1)} %get-tuple-element.33), channel_id=1, source_target_pairs={{0,5},{1,4},{2,7},{3,6},{4,1},{5,0},{6,3},{7,2},{8,13},{9,12},{10,... | collective-permute-start | bytes 393224 | tf_op jit(solution)/shard_map/ppermute | solution.py:92
  146.4 10.5 %collective-permute-start.18 = (bf16[256,256]{0,1:T(8,128)(2,1)S(1)}, bf16[256,256]{0,1:T(8,128)(2,1)S(1)}, u32[]{:S(2)}, u32[]{:S(2)}) collective-permute-start(bf16[256,256]{0,1:T(8,128)(2,1)S(1)} %get-tuple-element.33), channel_id=1, source_target_pairs={{0,4},{1,5},{2,6},{3,7},{4,0},{5,1},{6,2},{7,3},{8,12},{9,13},{10,... | collective-permute-start | bytes 393224 | tf_op jit(solution)/shard_map/ppermute | solution.py:92
  147.6 6.9 %collective-permute-start.17 = (bf16[256,256]{0,1:T(8,128)(2,1)S(1)}, bf16[256,256]{0,1:T(8,128)(2,1)S(1)}, u32[]{:S(2)}, u32[]{:S(2)}) collective-permute-start(bf16[256,256]{0,1:T(8,128)(2,1)S(1)} %get-tuple-element.33), channel_id=1, source_target_pairs={{0,3},{1,2},{2,1},{3,0},{4,7},{5,6},{6,5},{7,4},{8,11},{9,10},{10,... | collective-permute-start | bytes 393224 | tf_op jit(solution)/shard_map/ppermute | solution.py:92
  150.0 8.9 %collective-permute-start.21 = (bf16[256,256]{0,1:T(8,128)(2,1)S(1)}, bf16[256,256]{0,1:T(8,128)(2,1)S(1)}, u32[]{:S(2)}, u32[]{:S(2)}) collective-permute-start(bf16[256,256]{0,1:T(8,128)(2,1)S(1)} %get-tuple-element.33), channel_id=1, source_target_pairs={{0,7},{1,6},{2,5},{3,4},{4,3},{5,2},{6,1},{7,0},{8,15},{9,14},{10,... | collective-permute-start | bytes 393224 | tf_op jit(solution)/shard_map/ppermute | solution.py:92
  211.7 41.6 %all-to-all-start.7 = ((bf16[16,40,2048]{2,1,0:T(8,128)(2,1)}), bf16[16,40,2048]{2,1,0:T(8,128)(2,1)}, u32[]{:S(2)}, u32[]{:S(2)}) async-start(bf16[16,40,2048]{2,1,0:T(8,128)(2,1)} %bitcast.188), calls=%async_computation.7 | async-start | bytes 5242880 | tf_op jit(solution)/shard_map/all_to_all | solution.py:256
  271.0 20.0 %all-to-all-start.8 = ((bf16[8,256,256]{2,1,0:T(8,128)(2,1)}), bf16[8,256,256]{2,1,0:T(8,128)(2,1)}, u32[]{:S(2)}, u32[]{:S(2)}) async-start(bf16[8,256,256]{2,1,0:T(8,128)(2,1)} %fusion.41), calls=%async_computation.8 | async-start | bytes 2097152 | tf_op jit(solution)/shard_map/all_to_all | solution.py:271
  293.5 11.3 %collective-permute-start.25 = (bf16[256,256]{0,1:T(8,128)(2,1)S(1)}, bf16[256,256]{0,1:T(8,128)(2,1)S(1)}, u32[]{:S(2)}, u32[]{:S(2)}) collective-permute-start(bf16[256,256]{0,1:T(8,128)(2,1)S(1)} %add_convert_fusion), channel_id=1, source_target_pairs={{0,112},{16,64},{32,80},{48,96},{1,113},{17,65},{33,81},{49,97},{2... | collective-permute-start | bytes 393224 | tf_op jit(solution)/shard_map/ppermute | solution.py:280
  294.8 11.0 %collective-permute-start.24 = (bf16[256,256]{0,1:T(8,128)(2,1)S(1)}, bf16[256,256]{0,1:T(8,128)(2,1)S(1)}, u32[]{:S(2)}, u32[]{:S(2)}) collective-permute-start(bf16[256,256]{0,1:T(8,128)(2,1)S(1)} %add_convert_fusion), channel_id=1, source_target_pairs={{0,96},{16,112},{32,64},{48,80},{1,97},{17,113},{33,65},{49,81},{2... | collective-permute-start | bytes 393224 | tf_op jit(solution)/shard_map/ppermute | solution.py:280
  296.1 13.4 %collective-permute-start.23 = (bf16[256,256]{0,1:T(8,128)(2,1)S(1)}, bf16[256,256]{0,1:T(8,128)(2,1)S(1)}, u32[]{:S(2)}, u32[]{:S(2)}) collective-permute-start(bf16[256,256]{0,1:T(8,128)(2,1)S(1)} %add_convert_fusion), channel_id=1, source_target_pairs={{0,80},{16,96},{32,112},{48,64},{1,81},{17,97},{33,113},{49,65},{2... | collective-permute-start | bytes 393224 | tf_op jit(solution)/shard_map/ppermute | solution.py:280
  297.4 15.4 %collective-permute-start.22 = (bf16[256,256]{0,1:T(8,128)(2,1)S(1)}, bf16[256,256]{0,1:T(8,128)(2,1)S(1)}, u32[]{:S(2)}, u32[]{:S(2)}) collective-permute-start(bf16[256,256]{0,1:T(8,128)(2,1)S(1)} %add_convert_fusion), channel_id=1, source_target_pairs={{0,64},{16,80},{32,96},{48,112},{64,0},{80,16},{96,32},{112,48},{1... | collective-permute-start | bytes 393224 | tf_op jit(solution)/shard_map/ppermute | solution.py:280
  313.7 9.1 %collective-permute-start.26 = (bf16[1024,256]{0,1:T(8,128)(2,1)}, bf16[1024,256]{0,1:T(8,128)(2,1)S(1)}, u32[]{:S(2)}, u32[]{:S(2)}) collective-permute-start(bf16[1024,256]{0,1:T(8,128)(2,1)} %pad_maximum_fusion.2), channel_id=1, source_target_pairs={{0,8},{8,0},{1,9},{9,1},{2,10},{10,2},{3,11},{11,3},{4,12},{12,4},... | collective-permute-start | bytes 1572872 | tf_op jit(solution)/shard_map/ppermute | solution.py:81
  (45 other events, 691.1 us)

commit v2 on v1

v2 whole, which is shorter than its diff:
```python
import jax
import jax.numpy as jnp
from jax import lax
from jax.experimental import pallas as pl
from jax.experimental.pallas import tpu as pltpu
from jax.sharding import Mesh
from jax.sharding import PartitionSpec as P

D = 2048
HEAD_DIM = 128
TOP = 6
FIRST_LONG = 1920

ROW = ("zh", "y", "k")
COL = ("zl", "x")

epsilon = 1e-06
rope_base = 600000.0
masked_score = -1e30


def prompt_tables(lengths, order, positions):
    prompt_ids = jnp.arange(lengths.shape[0], dtype=jnp.int32)
    picked = order[:, None] == prompt_ids[None, :]
    packed_len = jnp.sum(jnp.where(picked, lengths[None, :], 0), axis=1)
    packed_end = jnp.cumsum(packed_len)
    packed_start = packed_end - packed_len
    request_start = jnp.cumsum(lengths) - lengths
    segment = jnp.sum((positions[:, None] >= packed_end[None, :]).astype(jnp.int32), axis=1)
    onehot = segment[:, None] == prompt_ids[None, :]
    within = positions - jnp.sum(jnp.where(onehot, packed_start[None, :], 0), axis=1)
    request = jnp.sum(jnp.where(onehot, order[None, :], 0), axis=1)
    offset = jnp.sum(
        jnp.where(request[:, None] == prompt_ids[None, :], request_start[None, :], 0), axis=1
    )
    return (segment, within, within + offset)


def rms_scale(values, gain):
    wide = values.astype(jnp.float32)
    return wide * lax.rsqrt(jnp.mean(wide * wide, axis=-1, keepdims=True) + epsilon) * gain


def rotary_tables(within, size):
    half_dim = size // 2
    inverse = rope_base ** (-jnp.arange(half_dim, dtype=jnp.float32) * 2.0 / size)
    angles = within.astype(jnp.float32)[:, None] * inverse[None, :]
    cosine = jnp.cos(angles)
    sine_part = jnp.sin(angles)
    return (
        jnp.concatenate([cosine, cosine], axis=1),
        jnp.concatenate([-sine_part, sine_part], axis=1),
    )


def core_swap(block):
    return lax.ppermute(block, "k", [(0, 1), (1, 0)])


def col_gather(block):
    copies = jnp.broadcast_to(block[None], (8,) + block.shape)
    return lax.all_to_all(copies, COL, 0, 0, tiled=True)


def projection_kernel(came_ref, mine_ref, other_ref, gain_ref, cos_ref, sin_ref, q_ref, kv_ref):
    core = lax.axis_index("k")
    squares = jnp.zeros((256, HEAD_DIM), jnp.float32)
    for member in range(8):
        for part in range(2):
            x = came_ref[member, 64 + part * 256 : 320 + part * 256, :].astype(jnp.float32)
            squares += x * x
    mean = jnp.sum(squares, axis=1, keepdims=True) * (1.0 / D)
    level = lax.rsqrt(mean + epsilon)
    total = jnp.zeros((256, 4 * HEAD_DIM), jnp.float32)
    for member in range(8):
        inputs, weights = [], []
        for part, ref in ((core, mine_ref), (1 - core, other_ref)):
            at = pl.multiple_of(64 + part * 256, 64)
            x = came_ref[member, pl.ds(at, 256), :].astype(jnp.float32)
            gain = gain_ref[pl.ds(2 * member + part, 1), :]
            inputs.append((x * level * gain).astype(jnp.bfloat16))
            weights.append(
                jnp.concatenate(
                    [ref[member, h * HEAD_DIM : (h + 1) * HEAD_DIM, :] for h in range(4)], axis=1
                )
            )
        total += jnp.dot(
            jnp.concatenate(inputs, axis=1),
            jnp.concatenate(weights, axis=0),
            preferred_element_type=jnp.float32,
        )
    cosine = cos_ref[...]
    sine_part = sin_ref[...]
    for h in range(4):
        part = total[:, h * HEAD_DIM : (h + 1) * HEAD_DIM]
        if h < 3:
            part = part * cosine + pltpu.roll(part, HEAD_DIM // 2, 1) * sine_part
        part = part.astype(jnp.bfloat16)
        if h < 2:
            q_ref[h] = part
        else:
            kv_ref[:, (h - 2) * HEAD_DIM : (h - 1) * HEAD_DIM] = part


def in_vmem(count):
    return [pl.BlockSpec(memory_space=pltpu.VMEM)] * count


def projection(came, mine, other, gain, cosine, sine_part):
    return pl.pallas_call(
        projection_kernel,
        in_specs=in_vmem(6),
        out_shape=(
            jax.ShapeDtypeStruct((2, 256, HEAD_DIM), jnp.bfloat16),
            jax.ShapeDtypeStruct((256, 2 * HEAD_DIM), jnp.bfloat16),
        ),
        name="projection",
    )(came, mine, other, gain, cosine, sine_part)


def attention_kernel(
    q_ref, mine_ref, other_ref, head_ref, start_ref, out_mine_ref, out_other_ref, terms_ref, s_ref
):
    half, core = lax.axis_index("zh"), lax.axis_index("k")
    first = half * 2048 + lax.axis_index("y") * 512 + core * 256
    scale = HEAD_DIM ** (-0.5)
    query_pos = first + lax.broadcasted_iota(jnp.int32, (256, 1), 0)
    start = start_ref[...]
    blocks = []
    for y in range(4):
        blocks.append((mine_ref, y, half * 2048 + y * 512 + core * 256, 256))
        blocks.append((other_ref, y, half * 2048 + y * 512 + (1 - core) * 256, 256))
    blocks.append((head_ref, None, jnp.where(half == 1, FIRST_LONG, 1 << 20), 128))

    def piece(ref, index, lanes):
        return ref[:, lanes] if index is None else ref[index, :, lanes]

    heads = []
    for h in range(2):
        query = q_ref[h]
        top = jnp.full((256, 128), masked_score, jnp.float32)
        at = 0
        for ref, index, pos, height in blocks:
            keys = piece(ref, index, slice(0, HEAD_DIM))
            scores = lax.dot_general(
                query, keys, (((1,), (1,)), ((), ())), preferred_element_type=jnp.float32
            ) * scale
            key_pos = pos + lax.broadcasted_iota(jnp.int32, (1, height), 1)
            allowed = (key_pos >= start) & (key_pos <= query_pos)
            scores = jnp.where(allowed, scores, masked_score)
            s_ref[:, at : at + height] = scores
            for lane in range(0, height, 128):
                top = jnp.maximum(top, scores[:, lane : lane + 128])
            at += height
        peak = jnp.max(top, axis=1, keepdims=True)
        sums = jnp.zeros((256, 128), jnp.float32)
        total = jnp.zeros((256, HEAD_DIM), jnp.float32)
        at = 0
        for ref, index, pos, height in blocks:
            numerators = jnp.exp(s_ref[:, at : at + height] - peak)
            for lane in range(0, height, 128):
                sums += numerators[:, lane : lane + 128]
            total += jnp.dot(
                numerators.astype(jnp.bfloat16),
                piece(ref, index, slice(HEAD_DIM, 2 * HEAD_DIM)),
                preferred_element_type=jnp.float32,
            )
            at += height
        heads.append((total / jnp.sum(sums, axis=1, keepdims=True)).astype(jnp.bfloat16))
    attended = jnp.concatenate(heads, axis=1)
    for f in range(8):
        mine = out_mine_ref[f, 512:768, :]
        other = out_other_ref[f, 512:768, :]
        low = jnp.where(core == 0, mine, other)
        high = jnp.where(core == 0, other, mine)
        terms_ref[f] = jnp.dot(
            attended, jnp.concatenate([low, high], axis=1), preferred_element_type=jnp.float32
        ).astype(jnp.bfloat16)


def attention(queries, mine, other, head, start, out_mine, out_other):
    return pl.pallas_call(
        attention_kernel,
        in_specs=in_vmem(7),
        out_shape=jax.ShapeDtypeStruct((8, 256, 256), jnp.bfloat16),
        scratch_shapes=[pltpu.VMEM((256, 2176), jnp.float32)],
        name="attention",
    )(queries, mine, other, head, start, out_mine, out_other)


def dispatch_kernel(resid_ref, gain_ref, slots_ref, mlp_ref, out_ref):
    squares = jnp.zeros((256, 256), jnp.float32)
    for f in range(8):
        x = resid_ref[f].astype(jnp.float32)
        squares += x * x
    level = lax.rsqrt(jnp.sum(squares, axis=1, keepdims=True) * (1.0 / D) + epsilon)
    slot = lax.broadcasted_iota(jnp.int32, (40, 256), 0)
    picker = jnp.concatenate(
        [jnp.where(slots_ref[r : r + 1, :] == slot, 1.0, 0.0) for r in range(16)], axis=0
    ).astype(jnp.bfloat16)
    for f in range(8):
        lanes = slice(f * 256, (f + 1) * 256)
        rows = (resid_ref[f].astype(jnp.float32) * level * gain_ref[:, lanes]).astype(jnp.bfloat16)
        mlp_ref[:, lanes] = rows
        picked = jnp.dot(picker, rows, preferred_element_type=jnp.float32)
        for r in range(16):
            out_ref[r, :, lanes] = picked[r * 40 : (r + 1) * 40].astype(jnp.bfloat16)


def dispatch(full_resid, gain, slots):
    return pl.pallas_call(
        dispatch_kernel,
        out_shape=(
            jax.ShapeDtypeStruct((256, D), jnp.bfloat16),
            jax.ShapeDtypeStruct((16, 40, D), jnp.bfloat16),
        ),
        name="dispatch",
    )(full_resid, gain, slots)


def expert_kernel(rows_ref, gate_up_ref, down_ref, out_ref):
    units = down_ref.shape[0]
    for part in range(2):
        rows = rows_ref[part * 320 : (part + 1) * 320, :]
        gate_up = jnp.dot(rows, gate_up_ref[...], preferred_element_type=jnp.float32)
        hidden = (jax.nn.silu(gate_up[:, :units]) * gate_up[:, units:]).astype(jnp.bfloat16)
        for f in range(8):
            result = jnp.dot(
                hidden, down_ref[:, f * 256 : (f + 1) * 256], preferred_element_type=jnp.float32
            )
            for r in range(8):
                out_ref[part * 8 + r, f] = result[r * 40 : (r + 1) * 40].astype(jnp.bfloat16)


def expert(rows, gate_up, down):
    return pl.pallas_call(
        expert_kernel,
        in_specs=in_vmem(3),
        out_shape=jax.ShapeDtypeStruct((16, 8, 40, 256), jnp.bfloat16),
        name="expert",
    )(rows, gate_up, down)


def place_rows_kernel(dest_ref, *refs):
    out_ref = refs[-1]
    total = jnp.zeros(out_ref.shape, jnp.float32)
    at = 0
    for ref in refs[:-1]:
        height = ref.shape[0]
        dest = dest_ref[:, at : at + height]
        rows = lax.broadcasted_iota(jnp.int32, (out_ref.shape[0], height), 0)
        mover = jnp.where(rows == dest, 1.0, 0.0).astype(jnp.bfloat16)
        total += jnp.dot(mover, ref[...], preferred_element_type=jnp.float32)
        at += height
    out_ref[...] = total.astype(out_ref.dtype)


def place_rows(dest, sources):
    return pl.pallas_call(
        place_rows_kernel,
        out_shape=jax.ShapeDtypeStruct((256, sources[0].shape[1]), sources[0].dtype),
        name="place_rows",
    )(dest, *sources)


def on_device(
    tokens,
    attn_gain,
    mlp_gain,
    trainer_qkv,
    trainer_out,
    router,
    shared_gate,
    shared_up,
    shared_down,
    expert_gate_up,
    expert_down,
    lengths,
    order,
    routes,
):
    tok_rows = tokens.shape[0]
    row_count, col_count = 16, 8
    zh_index = lax.axis_index("zh")
    y_index = lax.axis_index("y")
    k_index = lax.axis_index("k")
    row_index = lax.axis_index(ROW)
    col_index = lax.axis_index(COL)
    first = row_index * tok_rows
    local = jnp.arange(tok_rows, dtype=jnp.int32)

    seg_query, within_query, _ = prompt_tables(lengths, order, first + local)
    cosine, sine_part = rotary_tables(within_query, HEAD_DIM)
    start = (first + local - within_query)[:, None]

    heads = trainer_qkv.astype(jnp.bfloat16).reshape(16, 24, HEAD_DIM).transpose(1, 0, 2)
    groups = jnp.stack(
        [jnp.stack([heads[2 * g], heads[2 * g + 1], heads[16 + g // 2], heads[20 + g // 2]]) for g in range(8)]
    ).reshape(8, 64, HEAD_DIM)
    token_parts = tokens.reshape(tok_rows, 2, HEAD_DIM).transpose(1, 0, 2).reshape(1, 512, HEAD_DIM)
    out_parts = (
        trainer_out.astype(jnp.bfloat16).T.reshape(16, 8, 2, HEAD_DIM).transpose(1, 2, 0, 3)
    ).reshape(8, 32, HEAD_DIM)
    came = lax.all_to_all(
        jnp.concatenate(
            [groups, jnp.broadcast_to(token_parts, (8, 512, HEAD_DIM)), out_parts], axis=1
        ),
        COL, 0, 0, tiled=True,
    )
    qkv_heads = came[:, :64].reshape(8, 4, 16, HEAD_DIM).transpose(1, 0, 2, 3).reshape(4, 128, HEAD_DIM)
    qkv_block = qkv_heads.transpose(1, 0, 2).reshape(128, 512)
    out_block = came[:, 576:].reshape(8, 2, 16, HEAD_DIM).transpose(1, 3, 0, 2).reshape(256, 128)

    block = jnp.concatenate([qkv_heads.reshape(512, HEAD_DIM), out_block], axis=0)
    mine = lax.all_to_all(
        jnp.broadcast_to(block[None], (8, 768, HEAD_DIM)), ("zh", "y"), 0, 0, tiled=True
    )
    other = core_swap(mine)

    queries, kv_rows = projection(
        came, mine, other, attn_gain.reshape(16, HEAD_DIM), cosine, sine_part
    )
    cache_out = jnp.where(col_index % 2 == 0, kv_rows[:, :HEAD_DIM], kv_rows[:, HEAD_DIM:])

    tail = kv_rows[128:]
    head_sent = sum(lax.ppermute(tail, ROW, [(7, to)]) for to in (9, 11, 13, 15))
    head_sent, kv_copies = lax.optimization_barrier(
        (head_sent, jnp.broadcast_to(kv_rows[None], (4, 256, 256)))
    )
    kv_mine = lax.all_to_all(kv_copies, "y", 0, 0, tiled=True)
    kv_other = core_swap(kv_mine)
    kv_head = head_sent + core_swap(head_sent)
    terms = attention(queries, kv_mine, kv_other, kv_head, start, mine, other)
    got = lax.all_to_all(terms, COL, 0, 0, tiled=True)
    attn_part = jnp.sum(got.astype(jnp.float32), axis=0)
    resid = (tokens.astype(jnp.float32) + attn_part).astype(jnp.bfloat16)
    full_resid = col_gather(resid)

    n_experts = row_count * col_count // 2
    capacity = 40
    expert_ids = jnp.arange(n_experts, dtype=jnp.int32)
    member = jnp.any(routes[:, :, None] == expert_ids[None, None, :], axis=1)
    slot_of = jnp.where(member, jnp.cumsum(member.astype(jnp.int32), axis=0) - 1, -1)
    slots = lax.dynamic_index_in_dim(
        slot_of.reshape(tok_rows, row_count, col_count // 2), col_index // 2, 2, keepdims=False
    ).T
    mlp_in, outgoing = dispatch(full_resid, mlp_gain[None, :], slots)
    arrived = lax.all_to_all(outgoing, ROW, 0, 0, tiled=True)

    logits = jnp.dot(mlp_in, router, preferred_element_type=jnp.float32)
    router_probs = jax.nn.softmax(logits, axis=-1)
    picked_probs = jnp.where(member, router_probs, 0.0)
    route_weight = (
        picked_probs / jnp.sum(picked_probs, axis=-1, keepdims=True)
    ).astype(jnp.bfloat16)
    twice = jnp.repeat(slot_of, 2, axis=1)[:, :, None]
    combiner = jnp.where(
        twice == jnp.arange(capacity, dtype=jnp.int32),
        jnp.repeat(route_weight, 2, axis=1)[:, :, None],
        jnp.bfloat16(0),
    ).reshape(tok_rows, 2 * n_experts * capacity)
    shared_hidden = (
        jax.nn.silu(jnp.dot(mlp_in, shared_gate, preferred_element_type=jnp.float32))
        * jnp.dot(mlp_in, shared_up, preferred_element_type=jnp.float32)
    ).astype(jnp.bfloat16)
    shared_part = jnp.dot(shared_hidden, shared_down, preferred_element_type=jnp.float32).astype(
        jnp.bfloat16
    )
    pieces = []
    for step in range(col_count):
        piece = lax.dynamic_slice(shared_part, (0, (col_index ^ step) * 256), (tok_rows, 256))
        if step:
            piece = lax.ppermute(piece, COL, [(i, i ^ step) for i in range(col_count)])
        pieces.append(piece)
    arrived, combiner, pieces = lax.optimization_barrier((arrived, combiner, pieces))
    shared_sum = sum(piece.astype(jnp.float32) for piece in pieces)

    result = expert(arrived.reshape(row_count * capacity, D), expert_gate_up[0], expert_down[0])
    came_back = lax.all_to_all(
        result.reshape(2 * n_experts, capacity, 256), ROW + COL, 0, 0, tiled=True
    )
    routed_part = jnp.dot(
        combiner,
        came_back.reshape(2 * n_experts * capacity, 256),
        preferred_element_type=jnp.float32,
    )
    layer_out = (
        resid.astype(jnp.float32) + shared_sum + routed_part
    ).astype(jnp.bfloat16)

    received = []
    for step in range(4):
        pairs = [(s, 4 + (s + step) % 4) for s in range(4)]
        if step == 0:
            pairs += [(4 + s, s) for s in range(4)]
        received.append(lax.ppermute(layer_out, ("zh", "y"), pairs))
    late = lax.ppermute(
        layer_out[128:], ROW, [(7 + i, i) for i in range(0, 8, 2)] + [(15, 8)]
    )
    swapped = [core_swap(rows) for rows in received]
    span = jnp.arange(1024, dtype=jnp.int32)
    step_of = span // 256
    from_row = jnp.where(
        zh_index == 1,
        ((y_index - step_of) % 4) * 2,
        jnp.where(step_of == 0, 8 + y_index * 2, jnp.int32(1 << 12)),
    )
    late_from = jnp.where(
        k_index == 1, 1 << 12, jnp.where(zh_index == 0, row_index + 7, jnp.where(row_index == 8, 15, 1 << 12))
    )
    source_pos = jnp.concatenate(
        [
            (from_row + k_index) * 256 + span % 256,
            (from_row + 1 - k_index) * 256 + span % 256,
            late_from * 256 + 128 + jnp.arange(128, dtype=jnp.int32),
        ]
    )
    _, _, dest = prompt_tables(lengths, order, source_pos)
    dest = jnp.where(source_pos < row_count * tok_rows, dest, -1)
    hidden_states = place_rows((dest - first)[None, :], received + swapped + [late])
    return (hidden_states, cache_out, qkv_block, out_block)


def solution(mesh):
    fine = Mesh(mesh.devices.reshape(2, 4, 2, 2, 4), ROW + COL)
    in_specs = (
        P(ROW, COL),
        P(),
        P(),
        P(ROW + COL, None),
        P(None, ROW + COL),
        P(),
        P(None, COL),
        P(None, COL),
        P(COL, None),
        P(ROW + COL, None, None),
        P(ROW + COL, None, None),
        P(),
        P(),
        P(ROW, None),
    )
    out_specs = (P(ROW, COL), P(ROW, COL), P(ROW, COL), P(COL, ROW))
    return jax.shard_map(
        on_device, mesh=fine, in_specs=in_specs, out_specs=out_specs, check_vma=False
    )
```

time: 329 us -> 268 us (0.81); the launches traced: 325 us -> 267 us
  matrix products: 47.6 us -> 10.3 us
  starting transfers between devices: 83.2 us -> 46.5 us
  blocking collectives: 40.1 us -> 74.9 us
  Pallas kernels: 0 us -> 28.6 us
  other arithmetic: 30.9 us -> 10.5 us
  local copies, waits for them, and re-layouts: 32.3 us -> 14.3 us
  waiting for transfers between devices: 89 us -> 80.9 us
    all_to_all x1 -> x4, blocking collectives: 40.1 us -> 74.9 us  [the longest x1 25.2 us: on_device(): lax.all_to_all(jnp.broadcast_to(block[None], (8, 768, HEAD_DIM)), ('zh',...]
    dot_general x24 -> x2, matrix products: 37.3 us -> 7.94 us  [the longest x1 4.42 us: on_device(): jnp.dot(shared_hidden, shared_down, preferred_element_type=jnp.float32)]
    pallas_call x0 -> x5, Pallas kernels: none -> 28.6 us  [the longest x1 12.1 us: expert(): pl.pallas_call(expert_kernel, in_specs=in_vmem(3), out_shape=jax.ShapeDty...]
    all_to_all x8 -> x3, starting transfers between devices: 42.8 us -> 19.6 us  [the longest x1 8.97 us: on_device(): lax.all_to_all(result.reshape(2 * n_experts, capacity, 256), ROW + COL, 0...]
    all_to_all x8 -> x3, waiting for transfers between devices: 61.6 us -> 45.2 us  [the longest x1 32.2 us: on_device(): lax.all_to_all(result.reshape(2 * n_experts, capacity, 256), ROW + COL, 0...]
    ppermute x14 -> x7, starting transfers between devices: 19.4 us -> 6.62 us  [on_device(): piece = lax.ppermute(piece, COL, [(i, i ^ step) for i in range(col_count)])]
    dynamic_update_slice x15 -> x0, local copies, waits for them, and re-layouts: 12.7 us -> none  [col_gather(): lax.dynamic_update_slice(whole, piece, (0, (col_index ^ step) * width))]
    ppermute x14 -> x7, waiting for transfers between devices: 12.2 us -> 21.5 us  [on_device(): piece = lax.ppermute(piece, COL, [(i, i ^ step) for i in range(col_count)])]
  transfers between devices with their start and end apart: 36 -> 26, of which waited for: 11 -> 11; matrix products, arithmetic and copies ran while one was open for 20% -> 8% of each run, Pallas kernels for 0% -> 0%
where the time goes in v2:
time: 268 us; the launch traced here: 267 us
  waiting for transfers between devices  80.9 us (30%)
  blocking collectives  74.9 us (28%)
  starting transfers between devices  46.5 us (17%)
  Pallas kernels  28.6 us (11%)
  local copies, waits for them, and re-layouts  14.3 us (5%)
  other arithmetic  10.5 us (4%)
  matrix products  10.3 us (4%)
    all_to_all x1, waiting for transfers between devices, on_device(): lax.all_to_all(result.reshape(2 * n_experts, capacity, 256), ROW + COL, 0...  32.2 us
    all_to_all x1, blocking collectives, on_device(): lax.all_to_all(jnp.broadcast_to(block[None], (8, 768, HEAD_DIM)), ('zh',...  25.2 us
    ppermute x7, waiting for transfers between devices, on_device(): piece = lax.ppermute(piece, COL, [(i, i ^ step) for i in range(col_count)])  21.5 us
    all_to_all x1, blocking collectives, on_device(): lax.all_to_all(jnp.concatenate([groups, jnp.broadcast_to(token_parts, (8,...  20.9 us
    all_to_all x1, blocking collectives, on_device(): got = lax.all_to_all(terms, COL, 0, 0, tiled=True)  19.5 us
    all_to_all x1, waiting for transfers between devices, col_gather(): return lax.all_to_all(copies, COL, 0, 0, tiled=True)  13 us
    pallas_call x1, Pallas kernels, expert(): pl.pallas_call(expert_kernel, in_specs=in_vmem(3), out_shape=jax.ShapeDty...  12.1 us
    all_to_all x1, blocking collectives, on_device(): kv_mine = lax.all_to_all(kv_copies, 'y', 0, 0, tiled=True)  9.33 us
  transfers between devices with their start and end apart: 26, of which 11 were waited for; matrix products, arithmetic and copies ran while one was open for 8% of the time, Pallas kernels for 0%

profile of v2, /device:TPU:97, one launch (start us, length us, event | category | flops | bytes accessed | tf_op | source)
XLA Modules:
  0.0 267.2 jit_solution(10823903710023040472)
XLA Ops:
  4.1 20.9 %all_to_all.35.came_ref = bf16[8,608,128]{2,1,0:T(8,128)(2,1)S(1)} all-to-all(bf16[8,608,128]{2,1,0:T(8,128)(2,1)S(1)} %pad_maximum_fusion), channel_id=1, replica_groups=mesh['zh'=2,'y'=4,'k'=2,'zl'=2,'x'=4] {'zl','x'}, dimensions={0} | all-to-all | bytes 2490368 | tf_op jit(solution)/shard_map/all_to_all | solution.py:304
  26.2 25.2 %all_to_all.36.mine_ref.out_mine_ref = bf16[8,768,128]{2,1,0:T(8,128)(2,1)S(1)} all-to-all(bf16[8,768,128]{2,1,0:T(8,128)(2,1)S(1)} %broadcast_in_dim.161), channel_id=1, replica_groups=mesh['zh'=2,'y'=4,'k'=2,'zl'=2,'x'=4] {'zh','y'}, dimensions={0} | all-to-all | bytes 3145728 | tf_op jit(solution)/shard_map/all_to_all | solution.py:315
  51.4 2.6 collective-permute-start
  57.1 4.0 %projection.1 = (bf16[2,256,128]{2,1,0:T(8,128)(2,1)}, bf16[256,256]{1,0:T(8,128)(2,1)}) custom-call(bf16[8,608,128]{2,1,0:T(8,128)(2,1)} %copy-done.2, bf16[8,768,128]{2,1,0:T(8,128)(2,1)} %copy-done.1, bf16[8,768,128]{2,1,0:T(8,128)(2,1)} %collective-permute-done.other_ref.out_other_ref, f32[16,128]{1,0:T(8,128)} %bitcast.142, ...), custom_call_target="tpu_custom_call" | custom-call | tf_op jit(solution)/shard_map/projection/pallas_call | solution.py:110
  64.0 1.3 collective-permute-start.1
  65.3 8.2 %collective-permute-done.1 = bf16[128,256]{1,0:T(8,128)(2,1)S(1)} collective-permute-done((bf16[128,256]{1,0:T(8,128)(2,1)S(1)}, bf16[128,256]{1,0:T(8,128)(2,1)S(1)}, u32[]{:S(2)}, u32[]{:S(2)}) %collective-permute-start.1) | collective-permute-done | bytes 65568 | tf_op jit(solution)/shard_map/ppermute | solution.py:326
  74.5 9.3 %all_to_all.37.mine_ref = bf16[4,256,256]{2,1,0:T(8,128)(2,1)S(1)} all-to-all(bf16[4,256,256]{2,1,0:T(8,128)(2,1)S(1)} %broadcast_in_dim.164), channel_id=1, replica_groups=mesh['zh'=2,'y'=4,'k'=2,'zl'=2,'x'=4] {'y'}, dimensions={0} | all-to-all | bytes 1048576 | tf_op jit(solution)/shard_map/all_to_all | solution.py:330
  87.3 6.1 %attention.1 = bf16[8,256,256]{2,1,0:T(8,128)(2,1)} custom-call(bf16[2,256,128]{2,1,0:T(8,128)(2,1)} %get-tuple-element.20.q_ref, bf16[4,256,256]{2,1,0:T(8,128)(2,1)} %copy-done.5, bf16[4,256,256]{2,1,0:T(8,128)(2,1)} %copy-done.8, bf16[128,256]{1,0:T(8,128)(2,1)} %add.281.head_ref, s32[256,1]{1,0:T(8,128)} %copy.73.start_ref, ...), custom_call_target="tpu_custom_call" | custom-call | tf_op jit(solution)/shard_map/attention/pallas_call | solution.py:182
  93.5 19.5 %all_to_all.38 = bf16[8,256,256]{2,1,0:T(8,128)(2,1)S(1)} all-to-all(bf16[8,256,256]{2,1,0:T(8,128)(2,1)} %attention.1), channel_id=1, replica_groups=mesh['zh'=2,'y'=4,'k'=2,'zl'=2,'x'=4] {'zl','x'}, dimensions={0} | all-to-all | bytes 2097152 | tf_op jit(solution)/shard_map/all_to_all | solution.py:334
  114.2 4.7 %all-to-all-start.4 = ((bf16[8,256,256]{2,1,0:T(8,128)(2,1)}), bf16[8,256,256]{2,1,0:T(8,128)(2,1)S(1)}, u32[]{:S(2)}, u32[]{:S(2)}) async-start(bf16[8,256,256]{2,1,0:T(8,128)(2,1)} %broadcast_in_dim.165), calls=%async_computation.4 | async-start | bytes 2097152 | tf_op jit(solution)/shard_map/all_to_all | solution.py:62
  120.6 13.0 %all-to-all-done.4.resid_ref = bf16[8,256,256]{2,1,0:T(8,128)(2,1)S(1)} async-done(((bf16[8,256,256]{2,1,0:T(8,128)(2,1)}), bf16[8,256,256]{2,1,0:T(8,128)(2,1)S(1)}, u32[]{:S(2)}, u32[]{:S(2)}) %all-to-all-start.4) | async-done | bytes 1048608 | tf_op jit(solution)/shard_map/all_to_all | solution.py:62
  134.5 3.9 %dispatch.1 = (bf16[256,2048]{1,0:T(8,128)(2,1)}, bf16[16,40,2048]{2,1,0:T(8,128)(2,1)}) custom-call(bf16[8,256,256]{2,1,0:T(8,128)(2,1)} %copy-done.3, f32[1,2048]{1,0:T(1,128)} %bitcast.143, s32[16,256]{1,0:T(8,128)} %bitcast.130), custom_call_target="tpu_custom_call" | custom-call | tf_op jit(solution)/shard_map/dispatch/pallas_call | solution.py:211
  138.4 6.0 %all-to-all-start.5 = ((bf16[16,40,2048]{2,1,0:T(8,128)(2,1)}), bf16[16,40,2048]{2,1,0:T(8,128)(2,1)}, u32[]{:S(2)}, u32[]{:S(2)}) async-start(bf16[16,40,2048]{2,1,0:T(8,128)(2,1)} %get-tuple-element.24), calls=%async_computation.5 | async-start | bytes 5242880 | tf_op jit(solution)/shard_map/all_to_all | solution.py:348
  145.3 1.9 fusion.34
  147.3 4.4 %convolution_convert_fusion = bf16[256,2048]{1,0:T(8,128)(2,1)} fusion(bf16[352,2048]{1,0:T(8,128)(2,1)S(1)} %copy-done, bf16[256,2048]{1,0:T(8,128)(2,1)S(1)} %copy-done.4, bf16[2048,352]{0,1:T(8,128)(2,1)} %param.21, f32[256,352]{0,1:T(8,128)S(1)} %fusion.34), kind=kOutput, calls=%fused_computation.2 | convolution fusion | flops 739262464 | bytes 5341184 | tf_op jit(solution)/shard_map/dot_general | solution.py:366
  151.7 2.1 constant_dynamic-slice_fusion
  155.0 2.1 collective-permute-start.12
  157.0 1.8 collective-permute-start.11
  160.9 6.2 %collective-permute-done.13 = bf16[256,256]{1,0:T(8,128)(2,1)S(1)} collective-permute-done((bf16[256,256]{1,0:T(8,128)(2,1)S(1)}, bf16[256,256]{1,0:T(8,128)(2,1)S(1)}, u32[]{:S(2)}, u32[]{:S(2)}) %collective-permute-start.13) | collective-permute-done | bytes 131104 | tf_op jit(solution)/shard_map/ppermute | solution.py:373
  167.8 2.9 %fusion = bf16[256,5120]{0,1:T(8,128)(2,1)} fusion(s32[5120]{0:T(1024)} %eq.161, s32[256,128]{0,1:T(8,128)S(1)} %eq.157, bf16[256,128]{0,1:T(8,128)(2,1)S(1)} %broadcast_in_dim.170), kind=kLoop, calls=%fused_computation.1 | loop fusion | flops 2621440 | bytes 2838528 | tf_op jit(solution)/shard_map/jit(_where)/select_n | solution.py:357
  170.7 1.3 collective-permute-done.11
  172.0 14.0 %collective-permute-done.10 = bf16[256,256]{1,0:T(8,128)(2,1)} collective-permute-done((bf16[256,256]{1,0:T(8,128)(2,1)}, bf16[256,256]{1,0:T(8,128)(2,1)}, u32[]{:S(2)}, u32[]{:S(2)}) %collective-permute-start.10) | collective-permute-done | bytes 131104 | tf_op jit(solution)/shard_map/ppermute | solution.py:373
  186.1 12.1 %expert.1 = bf16[16,8,40,256]{3,2,1,0:T(8,128)(2,1)} custom-call(bf16[640,2048]{1,0:T(8,128)(2,1)} %bitcast.35.rows_ref, bf16[2048,1408]{1,0:T(8,128)(2,1)} %bitcast.118, bf16[704,2048]{1,0:T(8,128)(2,1)} %bitcast.119), custom_call_target="tpu_custom_call" | custom-call | tf_op jit(solution)/shard_map/expert/pallas_call | solution.py:236
  198.2 9.0 %all-to-all-start.6 = ((bf16[128,40,256]{2,1,0:T(8,128)(2,1)}), bf16[128,40,256]{2,1,0:T(8,128)(2,1)}, u32[]{:S(2)}, u32[]{:S(2)}) async-start(bf16[128,40,256]{2,1,0:T(8,128)(2,1)} %bitcast.117), calls=%async_computation.6 | async-start | bytes 5242880 | tf_op jit(solution)/shard_map/all_to_all | solution.py:379
  207.8 32.2 %all-to-all-done.6 = bf16[128,40,256]{2,1,0:T(8,128)(2,1)} async-done(((bf16[128,40,256]{2,1,0:T(8,128)(2,1)}), bf16[128,40,256]{2,1,0:T(8,128)(2,1)}, u32[]{:S(2)}, u32[]{:S(2)}) %all-to-all-start.6) | async-done | bytes 2621472 | tf_op jit(solution)/shard_map/all_to_all | solution.py:379
  240.0 3.5 %fusion.2 = bf16[256,256]{1,0:T(8,128)(2,1)S(1)} fusion(bf16[256,5120]{0,1:T(8,128)(2,1)} %fusion, bf16[5120,256]{1,0:T(8,128)(2,1)} %bitcast.39, bf16[256,256]{1,0:T(8,128)(2,1)S(1)} %copy-done.23, bf16[256,256]{1,0:T(8,128)(2,1)S(1)} %copy-done.25, bf16[256,256]{1,0:T(8,128)(2,1)} %collective-permute-done.11, ...), kind=kOutput, calls=%fused_computation.8 | convolution fusion | flops 672333824 | bytes 6553600 | tf_op jit(solution)/shard_map/dot_general | solution.py:382
  247.4 4.8 %collective-permute-start.14 = (bf16[256,256]{1,0:T(8,128)(2,1)S(1)}, bf16[256,256]{1,0:T(8,128)(2,1)S(1)}, u32[]{:S(2)}, u32[]{:S(2)}) collective-permute-start(bf16[256,256]{1,0:T(8,128)(2,1)S(1)} %fusion.2), channel_id=1, source_target_pairs={{0,64},{16,80},{32,96},{48,112},{64,0},{80,16},{96,32},{112,48},{1... | collective-permute-start | bytes 393224 | tf_op jit(solution)/shard_map/ppermute | solution.py:396
  253.7 2.5 collective-permute-start.22
  256.4 1.3 collective-permute-start.20
  257.7 1.6 collective-permute-done.15.refs_1_
  260.2 2.1 collective-permute-done.14.refs_0_
  264.8 2.4 place_rows.1
  (168 shorter events, 32.9 us)
Async XLA Ops:
  0.6 146.6 %copy-start = (bf16[352,2048]{1,0:T(8,128)(2,1)S(1)}, bf16[352,2048]{1,0:T(8,128)(2,1)}, u32[]{:S(2)}) copy-start(bf16[352,2048]{1,0:T(8,128)(2,1)} %param.22) | copy-start | bytes 4325380
  26.0 28.0 %copy-start.21 = (s32[8]{0:T(128)S(1)}, s32[8]{0:T(128)}, u32[]{:S(2)}) copy-start(s32[8]{0:T(128)} %param.26) | copy-start | bytes 100
  26.0 28.0 %copy-start.26 = (s32[8]{0:T(128)S(1)}, s32[8]{0:T(128)}, u32[]{:S(2)}) copy-start(s32[8]{0:T(128)} %param.25) | copy-start | bytes 100
  51.4 5.8 %collective-permute-start = (bf16[8,768,128]{2,1,0:T(8,128)(2,1)S(1)}, bf16[8,768,128]{2,1,0:T(8,128)(2,1)}, u32[]{:S(2)}, u32[]{:S(2)}) collective-permute-start(bf16[8,768,128]{2,1,0:T(8,128)(2,1)S(1)} %all_to_all.36.mine_ref.out_mine_ref), channel_id=1, source_target_pairs={{0,8},{8,0},{1,9},{9,1},{2,10},{10,2},{3,11},{11,3},{4,12},{12,4},... | collective-permute-start | bytes 4718600 | tf_op jit(solution)/shard_map/ppermute | solution.py:57
  62.0 3.3 %collective-permute-start.4 = (bf16[128,256]{1,0:T(8,128)(2,1)S(1)}, bf16[128,256]{1,0:T(8,128)(2,1)S(1)}, u32[]{:S(2)}, u32[]{:S(2)}) collective-permute-start(bf16[128,256]{1,0:T(8,128)(2,1)S(1)} %slice.114), channel_id=1, source_target_pairs={{56,120},{57,121},{58,122},{59,123},{60,124},{61,125},{62,126},{63... | collective-permute-start | bytes 196616 | tf_op jit(solution)/shard_map/ppermute | solution.py:326
  62.7 2.7 collective-permute-start.3
  63.3 2.0 collective-permute-start.2
  64.0 9.5 %collective-permute-start.1 = (bf16[128,256]{1,0:T(8,128)(2,1)S(1)}, bf16[128,256]{1,0:T(8,128)(2,1)S(1)}, u32[]{:S(2)}, u32[]{:S(2)}) collective-permute-start(bf16[128,256]{1,0:T(8,128)(2,1)S(1)} %slice.114), channel_id=1, source_target_pairs={{56,72},{57,73},{58,74},{59,75},{60,76},{61,77},{62,78},{63,79}} | collective-permute-start | bytes 196616 | tf_op jit(solution)/shard_map/ppermute | solution.py:326
  83.8 2.7 collective-permute-start.5
  83.8 2.0 collective-permute-start.6
  114.2 19.3 %all-to-all-start.4 = ((bf16[8,256,256]{2,1,0:T(8,128)(2,1)}), bf16[8,256,256]{2,1,0:T(8,128)(2,1)S(1)}, u32[]{:S(2)}, u32[]{:S(2)}) async-start(bf16[8,256,256]{2,1,0:T(8,128)(2,1)} %broadcast_in_dim.165), calls=%async_computation.4 | async-start | bytes 2097152 | tf_op jit(solution)/shard_map/all_to_all | solution.py:62
  138.4 47.6 %all-to-all-start.5 = ((bf16[16,40,2048]{2,1,0:T(8,128)(2,1)}), bf16[16,40,2048]{2,1,0:T(8,128)(2,1)}, u32[]{:S(2)}, u32[]{:S(2)}) async-start(bf16[16,40,2048]{2,1,0:T(8,128)(2,1)} %get-tuple-element.24), calls=%async_computation.5 | async-start | bytes 5242880 | tf_op jit(solution)/shard_map/all_to_all | solution.py:348
  153.8 13.3 %collective-permute-start.13 = (bf16[256,256]{1,0:T(8,128)(2,1)S(1)}, bf16[256,256]{1,0:T(8,128)(2,1)S(1)}, u32[]{:S(2)}, u32[]{:S(2)}) collective-permute-start(bf16[256,256]{1,0:T(8,128)(2,1)S(1)} %get-tuple-element.54), channel_id=1, source_target_pairs={{0,7},{1,6},{2,5},{3,4},{4,3},{5,2},{6,1},{7,0},{8,15},{9,14},{10,... | collective-permute-start | bytes 393224 | tf_op jit(solution)/shard_map/ppermute | solution.py:373
  155.0 12.1 %collective-permute-start.12 = (bf16[256,256]{1,0:T(8,128)(2,1)S(1)}, bf16[256,256]{1,0:T(8,128)(2,1)S(1)}, u32[]{:S(2)}, u32[]{:S(2)}) collective-permute-start(bf16[256,256]{1,0:T(8,128)(2,1)S(1)} %get-tuple-element.55), channel_id=1, source_target_pairs={{0,6},{1,7},{2,4},{3,5},{4,2},{5,3},{6,0},{7,1},{8,14},{9,15},{10,... | collective-permute-start | bytes 393224 | tf_op jit(solution)/shard_map/ppermute | solution.py:373
  157.0 15.0 %collective-permute-start.11 = (bf16[256,256]{1,0:T(8,128)(2,1)}, bf16[256,256]{1,0:T(8,128)(2,1)}, u32[]{:S(2)}, u32[]{:S(2)}) collective-permute-start(bf16[256,256]{1,0:T(8,128)(2,1)} %get-tuple-element.56), channel_id=1, source_target_pairs={{0,5},{1,4},{2,7},{3,6},{4,1},{5,0},{6,3},{7,2},{8,13},{9,12},{10,... | collective-permute-start | bytes 393224 | tf_op jit(solution)/shard_map/ppermute | solution.py:373
  158.9 27.2 %collective-permute-start.10 = (bf16[256,256]{1,0:T(8,128)(2,1)}, bf16[256,256]{1,0:T(8,128)(2,1)}, u32[]{:S(2)}, u32[]{:S(2)}) collective-permute-start(bf16[256,256]{1,0:T(8,128)(2,1)} %get-tuple-element.57), channel_id=1, source_target_pairs={{0,4},{1,5},{2,6},{3,7},{4,0},{5,1},{6,2},{7,3},{8,12},{9,13},{10,... | collective-permute-start | bytes 393224 | tf_op jit(solution)/shard_map/ppermute | solution.py:373
  159.1 26.9 %collective-permute-start.9 = (bf16[256,256]{1,0:T(8,128)(2,1)}, bf16[256,256]{1,0:T(8,128)(2,1)}, u32[]{:S(2)}, u32[]{:S(2)}) collective-permute-start(bf16[256,256]{1,0:T(8,128)(2,1)} %get-tuple-element.58), channel_id=1, source_target_pairs={{0,3},{1,2},{2,1},{3,0},{4,7},{5,6},{6,5},{7,4},{8,11},{9,10},{10,... | collective-permute-start | bytes 393224 | tf_op jit(solution)/shard_map/ppermute | solution.py:373
  167.0 19.0 %collective-permute-start.8 = (bf16[256,256]{1,0:T(8,128)(2,1)S(1)}, bf16[256,256]{1,0:T(8,128)(2,1)S(1)}, u32[]{:S(2)}, u32[]{:S(2)}) collective-permute-start(bf16[256,256]{1,0:T(8,128)(2,1)S(1)} %get-tuple-element.59), channel_id=1, source_target_pairs={{0,2},{1,3},{2,0},{3,1},{4,6},{5,7},{6,4},{7,5},{8,10},{9,11},{10,... | collective-permute-start | bytes 393224 | tf_op jit(solution)/shard_map/ppermute | solution.py:373
  167.1 19.0 %collective-permute-start.7 = (bf16[256,256]{1,0:T(8,128)(2,1)S(1)}, bf16[256,256]{1,0:T(8,128)(2,1)S(1)}, u32[]{:S(2)}, u32[]{:S(2)}) collective-permute-start(bf16[256,256]{1,0:T(8,128)(2,1)S(1)} %get-tuple-element.60), channel_id=1, source_target_pairs={{0,1},{1,0},{2,3},{3,2},{4,5},{5,4},{6,7},{7,6},{8,9},{9,8},{10,11... | collective-permute-start | bytes 393224 | tf_op jit(solution)/shard_map/ppermute | solution.py:373
  198.2 41.8 %copy-start.23 = (bf16[256,256]{1,0:T(8,128)(2,1)S(1)}, bf16[256,256]{1,0:T(8,128)(2,1)}, u32[]{:S(2)}) copy-start(bf16[256,256]{1,0:T(8,128)(2,1)} %copy-done.22) | copy-start | bytes 393220
  198.2 41.8 %copy-start.25 = (bf16[256,256]{1,0:T(8,128)(2,1)S(1)}, bf16[256,256]{1,0:T(8,128)(2,1)}, u32[]{:S(2)}) copy-start(bf16[256,256]{1,0:T(8,128)(2,1)} %copy-done.24) | copy-start | bytes 393220
  198.2 41.8 %all-to-all-start.6 = ((bf16[128,40,256]{2,1,0:T(8,128)(2,1)}), bf16[128,40,256]{2,1,0:T(8,128)(2,1)}, u32[]{:S(2)}, u32[]{:S(2)}) async-start(bf16[128,40,256]{2,1,0:T(8,128)(2,1)} %bitcast.117), calls=%async_computation.6 | async-start | bytes 5242880 | tf_op jit(solution)/shard_map/all_to_all | solution.py:379
  240.0 22.7 %copy-start.6 = (bf16[256,256]{1,0:T(8,128)(2,1)S(1)}, bf16[256,256]{1,0:T(8,128)(2,1)}, u32[]{:S(2)}) copy-start(bf16[256,256]{1,0:T(8,128)(2,1)} %get-tuple-element.21) | copy-start | bytes 393220
  243.5 12.7 %collective-permute-start.17 = (bf16[256,256]{1,0:T(8,128)(2,1)S(1)}, bf16[256,256]{1,0:T(8,128)(2,1)S(1)}, u32[]{:S(2)}, u32[]{:S(2)}) collective-permute-start(bf16[256,256]{1,0:T(8,128)(2,1)S(1)} %fusion.2), channel_id=1, source_target_pairs={{0,112},{16,64},{32,80},{48,96},{1,113},{17,65},{33,81},{49,97},{2... | collective-permute-start | bytes 393224 | tf_op jit(solution)/shard_map/ppermute | solution.py:396
  244.8 11.5 %collective-permute-start.16 = (bf16[256,256]{1,0:T(8,128)(2,1)S(1)}, bf16[256,256]{1,0:T(8,128)(2,1)S(1)}, u32[]{:S(2)}, u32[]{:S(2)}) collective-permute-start(bf16[256,256]{1,0:T(8,128)(2,1)S(1)} %fusion.2), channel_id=1, source_target_pairs={{0,96},{16,112},{32,64},{48,80},{1,97},{17,113},{33,65},{49,81},{2... | collective-permute-start | bytes 393224 | tf_op jit(solution)/shard_map/ppermute | solution.py:396
  246.1 13.2 %collective-permute-start.15 = (bf16[256,256]{1,0:T(8,128)(2,1)S(1)}, bf16[256,256]{1,0:T(8,128)(2,1)S(1)}, u32[]{:S(2)}, u32[]{:S(2)}) collective-permute-start(bf16[256,256]{1,0:T(8,128)(2,1)S(1)} %fusion.2), channel_id=1, source_target_pairs={{0,80},{16,96},{32,112},{48,64},{1,81},{17,97},{33,113},{49,65},{2... | collective-permute-start | bytes 393224 | tf_op jit(solution)/shard_map/ppermute | solution.py:396
  247.4 14.8 %collective-permute-start.14 = (bf16[256,256]{1,0:T(8,128)(2,1)S(1)}, bf16[256,256]{1,0:T(8,128)(2,1)S(1)}, u32[]{:S(2)}, u32[]{:S(2)}) collective-permute-start(bf16[256,256]{1,0:T(8,128)(2,1)S(1)} %fusion.2), channel_id=1, source_target_pairs={{0,64},{16,80},{32,96},{48,112},{64,0},{80,16},{96,32},{112,48},{1... | collective-permute-start | bytes 393224 | tf_op jit(solution)/shard_map/ppermute | solution.py:396
  253.7 9.6 %collective-permute-start.22 = (bf16[128,256]{1,0:T(8,128)(2,1)S(1)}, bf16[128,256]{1,0:T(8,128)(2,1)S(1)}, u32[]{:S(2)}, u32[]{:S(2)}) collective-permute-start(bf16[128,256]{1,0:T(8,128)(2,1)S(1)} %slice.139), channel_id=1, source_target_pairs={{56,0},{72,16},{88,32},{104,48},{120,64},{57,1},{73,17},{89,33},{1... | collective-permute-start | bytes 196616 | tf_op jit(solution)/shard_map/ppermute | solution.py:397
  256.3 7.1 %collective-permute-start.21 = (bf16[256,256]{1,0:T(8,128)(2,1)S(1)}, bf16[256,256]{1,0:T(8,128)(2,1)S(1)}, u32[]{:S(2)}, u32[]{:S(2)}) collective-permute-start(bf16[256,256]{1,0:T(8,128)(2,1)S(1)} %collective-permute-done.17.refs_3_), channel_id=1, source_target_pairs={{0,8},{8,0},{1,9},{9,1},{2,10},{10,2},{3,11},{11,3},{4,12},{12,4},... | collective-permute-start | bytes 393224 | tf_op jit(solution)/shard_map/ppermute | solution.py:57
  256.4 7.0 %collective-permute-start.20 = (bf16[256,256]{1,0:T(8,128)(2,1)S(1)}, bf16[256,256]{1,0:T(8,128)(2,1)S(1)}, u32[]{:S(2)}, u32[]{:S(2)}) collective-permute-start(bf16[256,256]{1,0:T(8,128)(2,1)S(1)} %collective-permute-done.16.refs_2_), channel_id=1, source_target_pairs={{0,8},{8,0},{1,9},{9,1},{2,10},{10,2},{3,11},{11,3},{4,12},{12,4},... | collective-permute-start | bytes 393224 | tf_op jit(solution)/shard_map/ppermute | solution.py:57
  259.3 4.1 %collective-permute-start.19 = (bf16[256,256]{1,0:T(8,128)(2,1)S(1)}, bf16[256,256]{1,0:T(8,128)(2,1)S(1)}, u32[]{:S(2)}, u32[]{:S(2)}) collective-permute-start(bf16[256,256]{1,0:T(8,128)(2,1)S(1)} %collective-permute-done.15.refs_1_), channel_id=1, source_target_pairs={{0,8},{8,0},{1,9},{9,1},{2,10},{10,2},{3,11},{11,3},{4,12},{12,4},... | collective-permute-start | bytes 393224 | tf_op jit(solution)/shard_map/ppermute | solution.py:57
  262.3 1.4 collective-permute-start.18
  (21 other events, 78.4 us)

commit v3 on v2

--- a/solution.py
+++ b/solution.py
@@ -62,7 +62,17 @@
     return lax.all_to_all(copies, COL, 0, 0, tiled=True)
 
 
-def projection_kernel(came_ref, mine_ref, other_ref, gain_ref, cos_ref, sin_ref, q_ref, kv_ref):
+def in_vmem(count):
+    return [pl.BlockSpec(memory_space=pltpu.VMEM)] * count
+
+
+def in_hbm(count):
+    return [pl.BlockSpec(memory_space=pltpu.HBM)] * count
+
+
+def projection_kernel(
+    came_ref, mine_ref, other_ref, gain_ref, cos_ref, sin_ref, q_hbm, kv_ref, q_ref, sems
+):
     core = lax.axis_index("k")
     squares = jnp.zeros((256, HEAD_DIM), jnp.float32)
     for member in range(8):
@@ -100,40 +110,55 @@
             q_ref[h] = part
         else:
             kv_ref[:, (h - 2) * HEAD_DIM : (h - 1) * HEAD_DIM] = part
-
-
-def in_vmem(count):
-    return [pl.BlockSpec(memory_space=pltpu.VMEM)] * count
+        if h == 1:
+            keep = pltpu.make_async_copy(q_ref, q_hbm, sems.at[0])
+            keep.start()
+    keep.wait()
 
 
 def projection(came, mine, other, gain, cosine, sine_part):
     return pl.pallas_call(
         projection_kernel,
         in_specs=in_vmem(6),
+        out_specs=in_hbm(1) + in_vmem(1),
+        scratch_shapes=[
+            pltpu.VMEM((2, 256, HEAD_DIM), jnp.bfloat16),
+            pltpu.SemaphoreType.DMA((1,)),
+        ],
         out_shape=(
             jax.ShapeDtypeStruct((2, 256, HEAD_DIM), jnp.bfloat16),
             jax.ShapeDtypeStruct((256, 2 * HEAD_DIM), jnp.bfloat16),
         ),
+        compiler_params=pltpu.CompilerParams(vmem_limit_bytes=16 << 20),
         name="projection",
     )(came, mine, other, gain, cosine, sine_part)
 
 
 def attention_kernel(
-    q_ref, mine_ref, other_ref, head_ref, start_ref, out_mine_ref, out_other_ref, terms_ref, s_ref
+    q_hbm, mine_ref, other_ref, start_ref, out_mine_ref, out_other_ref, terms_ref, s_ref, q_ref, sems
 ):
     half, core = lax.axis_index("zh"), lax.axis_index("k")
     first = half * 2048 + lax.axis_index("y") * 512 + core * 256
     scale = HEAD_DIM ** (-0.5)
     query_pos = first + lax.broadcasted_iota(jnp.int32, (256, 1), 0)
-    start = start_ref[...]
+    fetch = pltpu.make_async_copy(q_hbm, q_ref, sems.at[0])
+    fetch.start()
+    start = jnp.zeros((256, 1), jnp.int32)
+    for slot in range(8):
+        start = jnp.where(query_pos >= start_ref[slot], start_ref[slot], start)
+    fetch.wait()
     blocks = []
     for y in range(4):
         blocks.append((mine_ref, y, half * 2048 + y * 512 + core * 256, 256))
         blocks.append((other_ref, y, half * 2048 + y * 512 + (1 - core) * 256, 256))
-    blocks.append((head_ref, None, jnp.where(half == 1, FIRST_LONG, 1 << 20), 128))
+    blocks.append((None, 3, jnp.where(half == 1, FIRST_LONG, 1 << 20), 128))
 
     def piece(ref, index, lanes):
-        return ref[:, lanes] if index is None else ref[index, :, lanes]
+        if ref is None:
+            return jnp.where(
+                core == 1, mine_ref[index, 256:384, lanes], other_ref[index, 256:384, lanes]
+            )
+        return ref[index, :256, lanes]
 
     heads = []
     for h in range(2):
@@ -178,14 +203,22 @@
         ).astype(jnp.bfloat16)
 
 
-def attention(queries, mine, other, head, start, out_mine, out_other):
+def attention(queries, mine, other, start, out_mine, out_other):
     return pl.pallas_call(
         attention_kernel,
-        in_specs=in_vmem(7),
+        in_specs=in_hbm(1)
+        + in_vmem(2)
+        + [pl.BlockSpec(memory_space=pltpu.SMEM)]
+        + in_vmem(2),
         out_shape=jax.ShapeDtypeStruct((8, 256, 256), jnp.bfloat16),
-        scratch_shapes=[pltpu.VMEM((256, 2176), jnp.float32)],
+        scratch_shapes=[
+            pltpu.VMEM((256, 2176), jnp.float32),
+            pltpu.VMEM((2, 256, HEAD_DIM), jnp.bfloat16),
+            pltpu.SemaphoreType.DMA((1,)),
+        ],
+        compiler_params=pltpu.CompilerParams(vmem_limit_bytes=24 << 20),
         name="attention",
-    )(queries, mine, other, head, start, out_mine, out_other)
+    )(queries, mine, other, start, out_mine, out_other)
 
 
 def dispatch_kernel(resid_ref, gain_ref, slots_ref, mlp_ref, out_ref):
@@ -214,15 +247,73 @@
             jax.ShapeDtypeStruct((256, D), jnp.bfloat16),
             jax.ShapeDtypeStruct((16, 40, D), jnp.bfloat16),
         ),
+        compiler_params=pltpu.CompilerParams(vmem_limit_bytes=16 << 20),
         name="dispatch",
     )(full_resid, gain, slots)
 
 
-def expert_kernel(rows_ref, gate_up_ref, down_ref, out_ref):
+def shared_kernel(
+    rows_hbm, gate_hbm, up_hbm, down_hbm, out_ref, rows_ref, gate_ref, up_ref, down_ref, sems
+):
+    pairs = ((rows_hbm, rows_ref), (gate_hbm, gate_ref), (up_hbm, up_ref), (down_hbm, down_ref))
+    fetches = [
+        pltpu.make_async_copy(source, target, sems.at[i]) for i, (source, target) in enumerate(pairs)
+    ]
+    for fetch in fetches:
+        fetch.start()
+    fetches[0].wait()
+    fetches[1].wait()
+    col = lax.axis_index("zl") * 4 + lax.axis_index("x")
+    rows = rows_ref[...]
+    across = (((1,), (1,)), ((), ()))
+    gate = lax.dot_general(rows, gate_ref[...], across, preferred_element_type=jnp.float32)
+    fetches[2].wait()
+    up = lax.dot_general(rows, up_ref[...], across, preferred_element_type=jnp.float32)
+    hidden = (jax.nn.silu(gate) * up).astype(jnp.bfloat16)
+    fetches[3].wait()
+    for f in range(8):
+        out_ref[jnp.bitwise_xor(col, f)] = jnp.dot(
+            hidden, down_ref[:, f * 256 : (f + 1) * 256], preferred_element_type=jnp.float32
+        ).astype(jnp.bfloat16)
+
+
+def shared(rows, gate, up, down):
+    return pl.pallas_call(
+        shared_kernel,
+        in_specs=in_hbm(4),
+        out_specs=in_vmem(1)[0],
+        out_shape=jax.ShapeDtypeStruct((8, 256, 256), jnp.bfloat16),
+        scratch_shapes=[
+            pltpu.VMEM((256, D), jnp.bfloat16),
+            pltpu.VMEM(gate.shape, jnp.bfloat16),
+            pltpu.VMEM(up.shape, jnp.bfloat16),
+            pltpu.VMEM(down.shape, jnp.bfloat16),
+            pltpu.SemaphoreType.DMA((4,)),
+        ],
+        compiler_params=pltpu.CompilerParams(vmem_limit_bytes=60 << 20),
+        name="shared",
+    )(rows, gate, up, down)
+
+
+def expert_kernel(
+    rows_hbm, gate_up_hbm, down_hbm, out_hbm, rows_ref, gate_up_ref, down_ref, out_ref, fetch_sems, sems
+):
     units = down_ref.shape[0]
+    pairs = ((gate_up_hbm, gate_up_ref), (rows_hbm, rows_ref), (down_hbm, down_ref))
+    fetches = [
+        pltpu.make_async_copy(source, target, fetch_sems.at[i])
+        for i, (source, target) in enumerate(pairs)
+    ]
+    for fetch in fetches:
+        fetch.start()
+    fetches[0].wait()
+    fetches[1].wait()
+    copies = []
     for part in range(2):
-        rows = rows_ref[part * 320 : (part + 1) * 320, :]
-        gate_up = jnp.dot(rows, gate_up_ref[...], preferred_element_type=jnp.float32)
+        rows = slice(part * 320, (part + 1) * 320)
+        gate_up = jnp.dot(rows_ref[rows, :], gate_up_ref[...], preferred_element_type=jnp.float32)
+        if part == 0:
+            fetches[2].wait()
         hidden = (jax.nn.silu(gate_up[:, :units]) * gate_up[:, units:]).astype(jnp.bfloat16)
         for f in range(8):
             result = jnp.dot(
@@ -230,13 +321,30 @@
             )
             for r in range(8):
                 out_ref[part * 8 + r, f] = result[r * 40 : (r + 1) * 40].astype(jnp.bfloat16)
+            there = (pl.ds(part * 8, 8), f)
+            copies.append(
+                pltpu.make_async_copy(out_ref.at[there], out_hbm.at[there], sems.at[part * 8 + f])
+            )
+            copies[-1].start()
+    for copy in copies:
+        copy.wait()
 
 
 def expert(rows, gate_up, down):
     return pl.pallas_call(
         expert_kernel,
-        in_specs=in_vmem(3),
+        in_specs=in_hbm(3),
+        out_specs=in_hbm(1)[0],
         out_shape=jax.ShapeDtypeStruct((16, 8, 40, 256), jnp.bfloat16),
+        scratch_shapes=[
+            pltpu.VMEM(rows.shape, jnp.bfloat16),
+            pltpu.VMEM(gate_up.shape, jnp.bfloat16),
+            pltpu.VMEM(down.shape, jnp.bfloat16),
+            pltpu.VMEM((16, 8, 40, 256), jnp.bfloat16),
+            pltpu.SemaphoreType.DMA((3,)),
+            pltpu.SemaphoreType.DMA((16,)),
+        ],
+        compiler_params=pltpu.CompilerParams(vmem_limit_bytes=60 << 20),
         name="expert",
     )(rows, gate_up, down)
 
@@ -259,6 +367,7 @@
     return pl.pallas_call(
         place_rows_kernel,
         out_shape=jax.ShapeDtypeStruct((256, sources[0].shape[1]), sources[0].dtype),
+        compiler_params=pltpu.CompilerParams(vmem_limit_bytes=8 << 20),
         name="place_rows",
     )(dest, *sources)
 
@@ -291,7 +400,10 @@
 
     seg_query, within_query, _ = prompt_tables(lengths, order, first + local)
     cosine, sine_part = rotary_tables(within_query, HEAD_DIM)
-    start = (first + local - within_query)[:, None]
+    packed = jnp.sum(
+        jnp.where(order[:, None] == jnp.arange(8, dtype=jnp.int32)[None, :], lengths[None, :], 0), axis=1
+    )
+    start = jnp.cumsum(packed) - packed
 
     heads = trainer_qkv.astype(jnp.bfloat16).reshape(16, 24, HEAD_DIM).transpose(1, 0, 2)
     groups = jnp.stack(
@@ -322,15 +434,13 @@
     )
     cache_out = jnp.where(col_index % 2 == 0, kv_rows[:, :HEAD_DIM], kv_rows[:, HEAD_DIM:])
 
-    tail = kv_rows[128:]
-    head_sent = sum(lax.ppermute(tail, ROW, [(7, to)]) for to in (9, 11, 13, 15))
-    head_sent, kv_copies = lax.optimization_barrier(
-        (head_sent, jnp.broadcast_to(kv_rows[None], (4, 256, 256)))
-    )
-    kv_mine = lax.all_to_all(kv_copies, "y", 0, 0, tiled=True)
+    head_sent = lax.ppermute(kv_rows[128:], ROW, [(7, 15)])
+    block = jnp.concatenate([kv_rows, head_sent], axis=0)
+    kv_mine = lax.all_to_all(
+        jnp.broadcast_to(block[None], (4, 384, 256)), "y", 0, 0, tiled=True
+    )
     kv_other = core_swap(kv_mine)
-    kv_head = head_sent + core_swap(head_sent)
-    terms = attention(queries, kv_mine, kv_other, kv_head, start, mine, other)
+    terms = attention(queries, kv_mine, kv_other, start, mine, other)
     got = lax.all_to_all(terms, COL, 0, 0, tiled=True)
     attn_part = jnp.sum(got.astype(jnp.float32), axis=0)
     resid = (tokens.astype(jnp.float32) + attn_part).astype(jnp.bfloat16)
@@ -359,23 +469,21 @@
         jnp.repeat(route_weight, 2, axis=1)[:, :, None],
         jnp.bfloat16(0),
     ).reshape(tok_rows, 2 * n_experts * capacity)
-    shared_hidden = (
-        jax.nn.silu(jnp.dot(mlp_in, shared_gate, preferred_element_type=jnp.float32))
-        * jnp.dot(mlp_in, shared_up, preferred_element_type=jnp.float32)
-    ).astype(jnp.bfloat16)
-    shared_part = jnp.dot(shared_hidden, shared_down, preferred_element_type=jnp.float32).astype(
-        jnp.bfloat16
-    )
+    shared_part = shared(mlp_in, shared_gate.T, shared_up.T, shared_down)
     pieces = []
     for step in range(col_count):
-        piece = lax.dynamic_slice(shared_part, (0, (col_index ^ step) * 256), (tok_rows, 256))
+        piece = shared_part[step]
         if step:
             piece = lax.ppermute(piece, COL, [(i, i ^ step) for i in range(col_count)])
         pieces.append(piece)
-    arrived, combiner, pieces = lax.optimization_barrier((arrived, combiner, pieces))
+    arrived, combiner, pieces, qkv_block, out_block, cache_out = lax.optimization_barrier(
+        (arrived, combiner, pieces, qkv_block, out_block, cache_out)
+    )
     shared_sum = sum(piece.astype(jnp.float32) for piece in pieces)
 
-    result = expert(arrived.reshape(row_count * capacity, D), expert_gate_up[0], expert_down[0])
+    result = expert(
+        arrived.reshape(row_count * capacity, D), expert_gate_up[0], expert_down[0]
+    )
     came_back = lax.all_to_all(
         result.reshape(2 * n_experts, capacity, 256), ROW + COL, 0, 0, tiled=True
     )

time: 268 us -> 254 us (0.948)
  waiting for transfers between devices: 80.9 us -> 73.3 us
  matrix products: 10.3 us -> 3.4 us
  blocking collectives: 74.9 us -> 80.9 us
  Pallas kernels: 28.6 us -> 23 us
  local copies, waits for them, and re-layouts: 14.3 us -> 17 us
    ppermute x4 -> x1, waiting for transfers between devices: 8.22 us -> 0.01 us  [on_device(): head_sent = lax.ppermute(kv_rows[128:], ROW, [(7, 15)])]
    all_to_all x1, blocking collectives: 9.33 us -> 16.4 us  [on_device(): lax.all_to_all(jnp.broadcast_to(block[None], (4, 384, 256)), 'y', 0, 0, t...]
    dot_general x2 -> x0, matrix products: 6.35 us -> none  [the longest x1 4.42 us: on_device(): jnp.dot(shared_hidden, shared_down, preferred_element_type=jnp.float32)]
    unnamed x64 -> x77, local copies, waits for them, and re-layouts: 5.71 us -> 8.74 us
    pallas_call x1, Pallas kernels: 3.9 us -> 1.14 us  [dispatch(): pl.pallas_call(dispatch_kernel, out_shape=(jax.ShapeDtypeStruct((256, D),...]
    pallas_call x3 -> x4, Pallas kernels: 22.3 us -> 20.7 us  [the longest x1 10.9 us: expert(): pl.pallas_call(expert_kernel, in_specs=in_hbm(3), out_specs=in_hbm(1)[0],...]
    ppermute x7 -> x6, starting transfers between devices: 5.8 us -> 6.69 us  [core_swap(): return lax.ppermute(block, 'k', [(0, 1), (1, 0)])]
  transfers between devices with their start and end apart: 26 -> 22, of which waited for: 11 -> 9; matrix products, arithmetic and copies ran while one was open for 8% -> 6% of each run, Pallas kernels for 0% -> 2%
where the time goes in v3:
time: 254 us
  blocking collectives  80.9 us (32%)
  waiting for transfers between devices  73.3 us (29%)
  starting transfers between devices  46.1 us (18%)
  Pallas kernels  23 us (9%)
  local copies, waits for them, and re-layouts  17 us (7%)
  other arithmetic  8.69 us (3%)
  matrix products  3.4 us (1%)
    all_to_all x1, waiting for transfers between devices, on_device(): lax.all_to_all(result.reshape(2 * n_experts, capacity, 256), ROW + COL, 0...  32.3 us
    all_to_all x1, blocking collectives, on_device(): lax.all_to_all(jnp.broadcast_to(block[None], (8, 768, HEAD_DIM)), ('zh',...  25.2 us
    all_to_all x1, blocking collectives, on_device(): lax.all_to_all(jnp.concatenate([groups, jnp.broadcast_to(token_parts, (8,...  20.9 us
    ppermute x7, waiting for transfers between devices, on_device(): piece = lax.ppermute(piece, COL, [(i, i ^ step) for i in range(col_count)])  19 us
    all_to_all x1, blocking collectives, on_device(): got = lax.all_to_all(terms, COL, 0, 0, tiled=True)  18.4 us
    all_to_all x1, blocking collectives, on_device(): lax.all_to_all(jnp.broadcast_to(block[None], (4, 384, 256)), 'y', 0, 0, t...  16.4 us
    all_to_all x1, waiting for transfers between devices, col_gather(): return lax.all_to_all(copies, COL, 0, 0, tiled=True)  13.5 us
    pallas_call x1, Pallas kernels, expert(): pl.pallas_call(expert_kernel, in_specs=in_hbm(3), out_specs=in_hbm(1)[0],...  10.9 us
  transfers between devices with their start and end apart: 22, of which 9 were waited for; matrix products, arithmetic and copies ran while one was open for 6% of the time, Pallas kernels for 2%

profile of v3, /device:TPU:97, one launch (start us, length us, event | category | flops | bytes accessed | tf_op | source)
XLA Modules:
  0.0 253.8 jit_solution(15415918200863146022)
XLA Ops:
  4.0 20.9 %all_to_all.35.came_ref = bf16[8,608,128]{2,1,0:T(8,128)(2,1)S(1)} all-to-all(bf16[8,608,128]{2,1,0:T(8,128)(2,1)S(1)} %pad_maximum_fusion), channel_id=1, replica_groups=mesh['zh'=2,'y'=4,'k'=2,'zl'=2,'x'=4] {'zl','x'}, dimensions={0} | all-to-all | bytes 2490368 | tf_op jit(solution)/shard_map/all_to_all | solution.py:416
  26.6 25.2 %all_to_all.36.mine_ref.out_mine_ref = bf16[8,768,128]{2,1,0:T(8,128)(2,1)S(1)} all-to-all(bf16[8,768,128]{2,1,0:T(8,128)(2,1)S(1)} %broadcast_in_dim.167), channel_id=1, replica_groups=mesh['zh'=2,'y'=4,'k'=2,'zl'=2,'x'=4] {'zh','y'}, dimensions={0} | all-to-all | bytes 3145728 | tf_op jit(solution)/shard_map/all_to_all | solution.py:427
  51.8 2.6 %collective-permute-start = (bf16[8,768,128]{2,1,0:T(8,128)(2,1)S(1)}, bf16[8,768,128]{2,1,0:T(8,128)(2,1)S(1)}, u32[]{:S(2)}, u32[]{:S(2)}) collective-permute-start(bf16[8,768,128]{2,1,0:T(8,128)(2,1)S(1)} %all_to_all.36.mine_ref.out_mine_ref), channel_id=1, source_target_pairs={{0,8},{8,0},{1,9},{9,1},{2,10},{10,2},{3,11},{11,3},{4,12},{12,4},... | collective-permute-start | bytes 4718600 | tf_op jit(solution)/shard_map/ppermute | solution.py:57
  55.7 1.8 collective-permute-done.other_ref.out_other_ref
  57.4 1.3 copy-done.2
  60.7 16.4 %all_to_all.37.mine_ref = bf16[4,384,256]{2,1,0:T(8,128)(2,1)S(1)} all-to-all(bf16[4,384,256]{2,1,0:T(8,128)(2,1)S(1)} %broadcast_in_dim.170), channel_id=1, replica_groups=mesh['zh'=2,'y'=4,'k'=2,'zl'=2,'x'=4] {'y'}, dimensions={0} | all-to-all | bytes 1572864 | tf_op jit(solution)/shard_map/all_to_all | solution.py:439
  77.2 2.3 collective-permute-done.2.other_ref
  79.5 3.6 %attention.1 = bf16[8,256,256]{2,1,0:T(8,128)(2,1)S(1)} custom-call(bf16[2,256,128]{2,1,0:T(8,128)(2,1)S(1)} %get-tuple-element.21.q_hbm, bf16[4,384,256]{2,1,0:T(8,128)(2,1)S(1)} %all_to_all.37.mine_ref, bf16[4,384,256]{2,1,0:T(8,128)(2,1)S(1)} %collective-permute-done.2.other_ref, s32[8]{0:T(128)S(1)} %bitcast_subtract_fusion.1.start_ref, ...), custom_call_target="tpu_custom_call" | custom-call | tf_op jit(solution)/shard_map/attention/pallas_call | solution.py:207
  83.1 18.4 %all_to_all.38 = bf16[8,256,256]{2,1,0:T(8,128)(2,1)S(1)} all-to-all(bf16[8,256,256]{2,1,0:T(8,128)(2,1)S(1)} %attention.1), channel_id=1, replica_groups=mesh['zh'=2,'y'=4,'k'=2,'zl'=2,'x'=4] {'zl','x'}, dimensions={0} | all-to-all | bytes 2097152 | tf_op jit(solution)/shard_map/all_to_all | solution.py:444
  102.7 4.7 %all-to-all-start.4 = ((bf16[8,256,256]{2,1,0:T(8,128)(2,1)}), bf16[8,256,256]{2,1,0:T(8,128)(2,1)S(1)}, u32[]{:S(2)}, u32[]{:S(2)}) async-start(bf16[8,256,256]{2,1,0:T(8,128)(2,1)} %broadcast_in_dim.171), calls=%async_computation.4 | async-start | bytes 2097152 | tf_op jit(solution)/shard_map/all_to_all | solution.py:62
  108.5 13.5 %all-to-all-done.4.resid_ref = bf16[8,256,256]{2,1,0:T(8,128)(2,1)S(1)} async-done(((bf16[8,256,256]{2,1,0:T(8,128)(2,1)}), bf16[8,256,256]{2,1,0:T(8,128)(2,1)S(1)}, u32[]{:S(2)}, u32[]{:S(2)}) %all-to-all-start.4) | async-done | bytes 1048608 | tf_op jit(solution)/shard_map/all_to_all | solution.py:62
  124.2 1.5 copy-done.5
  125.7 7.2 %all-to-all-start.5 = ((bf16[16,40,2048]{2,1,0:T(8,128)(2,1)}), bf16[16,40,2048]{2,1,0:T(8,128)(2,1)S(1)}, u32[]{:S(2)}, u32[]{:S(2)}) async-start(bf16[16,40,2048]{2,1,0:T(8,128)(2,1)} %copy-done.5), calls=%async_computation.5 | async-start | bytes 5242880 | tf_op jit(solution)/shard_map/all_to_all | solution.py:458
  136.6 5.0 %shared.1 = bf16[8,256,256]{2,1,0:T(8,128)(2,1)} custom-call(bf16[256,2048]{1,0:T(8,128)(2,1)} %copy-done.3, bf16[352,2048]{1,0:T(8,128)(2,1)} %bitcast.136, bf16[352,2048]{1,0:T(8,128)(2,1)} %bitcast.137, bf16[352,2048]{1,0:T(8,128)(2,1)} %down_hbm.1), custom_call_target="tpu_custom_call" | custom-call | tf_op jit(solution)/shard_map/shared/pallas_call | solution.py:281
  141.6 2.2 slice_bitcast_fusion
  144.4 2.7 %collective-permute-start.8 = (bf16[256,256]{1,0:T(8,128)(2,1)S(1)}, bf16[256,256]{1,0:T(8,128)(2,1)S(1)}, u32[]{:S(2)}, u32[]{:S(2)}) collective-permute-start(bf16[256,256]{1,0:T(8,128)(2,1)S(1)} %get-tuple-element.57), channel_id=1, source_target_pairs={{0,6},{1,7},{2,4},{3,5},{4,2},{5,3},{6,0},{7,1},{8,14},{9,15},{10,... | collective-permute-start | bytes 393224 | tf_op jit(solution)/shard_map/ppermute | solution.py:477
  150.9 9.2 %collective-permute-done.9 = bf16[256,256]{1,0:T(8,128)(2,1)S(1)} collective-permute-done((bf16[256,256]{1,0:T(8,128)(2,1)S(1)}, bf16[256,256]{1,0:T(8,128)(2,1)S(1)}, u32[]{:S(2)}, u32[]{:S(2)}) %collective-permute-start.9) | collective-permute-done | bytes 131104 | tf_op jit(solution)/shard_map/ppermute | solution.py:477
  160.9 3.2 %fusion = bf16[256,5120]{0,1:T(8,128)(2,1)} fusion(s32[5120]{0:T(1024)S(1)} %copy-done.22, s32[256,128]{0,1:T(8,128)} %eq.164, bf16[256,128]{0,1:T(8,128)(2,1)S(1)} %broadcast_in_dim.176), kind=kLoop, calls=%fused_computation.1 | loop fusion | flops 2621440 | bytes 2838528 | tf_op jit(solution)/shard_map/jit(_where)/select_n | solution.py:467
  164.0 9.8 %collective-permute-done.6 = bf16[256,256]{1,0:T(8,128)(2,1)} collective-permute-done((bf16[256,256]{1,0:T(8,128)(2,1)}, bf16[256,256]{1,0:T(8,128)(2,1)}, u32[]{:S(2)}, u32[]{:S(2)}) %collective-permute-start.6) | collective-permute-done | bytes 131104 | tf_op jit(solution)/shard_map/ppermute | solution.py:477
  174.4 1.5 copy-done.8
  175.9 10.9 %expert.1 = bf16[16,8,40,256]{3,2,1,0:T(8,128)(2,1)} custom-call(bf16[640,2048]{1,0:T(8,128)(2,1)} %bitcast.132, bf16[2048,1408]{1,0:T(8,128)(2,1)} %bitcast.134, bf16[704,2048]{1,0:T(8,128)(2,1)} %bitcast.135), custom_call_target="tpu_custom_call" | custom-call | tf_op jit(solution)/shard_map/expert/pallas_call | solution.py:334
  186.9 9.1 %all-to-all-start.6 = ((bf16[128,40,256]{2,1,0:T(8,128)(2,1)}), bf16[128,40,256]{2,1,0:T(8,128)(2,1)}, u32[]{:S(2)}, u32[]{:S(2)}) async-start(bf16[128,40,256]{2,1,0:T(8,128)(2,1)} %bitcast.133), calls=%async_computation.6 | async-start | bytes 5242880 | tf_op jit(solution)/shard_map/all_to_all | solution.py:487
  196.6 32.3 %all-to-all-done.6 = bf16[128,40,256]{2,1,0:T(8,128)(2,1)} async-done(((bf16[128,40,256]{2,1,0:T(8,128)(2,1)}), bf16[128,40,256]{2,1,0:T(8,128)(2,1)}, u32[]{:S(2)}, u32[]{:S(2)}) %all-to-all-start.6) | async-done | bytes 2621472 | tf_op jit(solution)/shard_map/all_to_all | solution.py:487
  228.9 2.9 %fusion.1 = bf16[256,256]{1,0:T(8,128)(2,1)S(1)} fusion(bf16[256,5120]{0,1:T(8,128)(2,1)S(1)} %copy-done.9, bf16[5120,256]{1,0:T(8,128)(2,1)} %bitcast.51, bf16[256,256]{1,0:T(8,128)(2,1)S(1)} %copy-done.27, bf16[256,256]{1,0:T(8,128)(2,1)} %copy-done.28, bf16[256,256]{1,0:T(8,128)(2,1)} %collective-permute-done.7, ...), kind=kOutput, calls=%fused_computation.5 | convolution fusion | flops 672333824 | bytes 6553600 | tf_op jit(solution)/shard_map/dot_general | solution.py:490
  231.9 1.3 collective-permute-start.13
  233.2 1.3 collective-permute-start.12
  234.5 1.3 collective-permute-start.11
  235.8 4.8 %collective-permute-start.10 = (bf16[256,256]{1,0:T(8,128)(2,1)S(1)}, bf16[256,256]{1,0:T(8,128)(2,1)S(1)}, u32[]{:S(2)}, u32[]{:S(2)}) collective-permute-start(bf16[256,256]{1,0:T(8,128)(2,1)S(1)} %fusion.1), channel_id=1, source_target_pairs={{0,64},{16,80},{32,96},{48,112},{64,0},{80,16},{96,32},{112,48},{1... | collective-permute-start | bytes 393224 | tf_op jit(solution)/shard_map/ppermute | solution.py:504
  240.7 2.5 collective-permute-start.18
  243.9 2.2 collective-permute-start.16
  246.0 1.6 collective-permute-done.11.refs_1_
  248.5 2.1 collective-permute-done.10.refs_0_
  (170 shorter events, 27.1 us)
Async XLA Ops:
  0.6 149.7 %copy-start = (bf16[2048,64]{0,1:T(8,128)(2,1)S(1)}, bf16[2048,64]{0,1:T(8,128)(2,1)}, u32[]{:S(2)}) copy-start(bf16[2048,64]{0,1:T(8,128)(2,1)} %param.19) | copy-start | bytes 786436
  26.4 28.0 %copy-start.24 = (s32[8]{0:T(128)S(1)}, s32[8]{0:T(128)}, u32[]{:S(2)}) copy-start(s32[8]{0:T(128)} %param.26) | copy-start | bytes 100
  26.4 28.0 %copy-start.31 = (s32[8]{0:T(128)S(1)}, s32[8]{0:T(128)}, u32[]{:S(2)}) copy-start(s32[8]{0:T(128)} %param.25) | copy-start | bytes 100
  26.6 30.8 %copy-start.6 = (f32[2048]{0:T(1024)S(1)}, f32[2048]{0:T(1024)}, u32[]{:S(2)}) copy-start(f32[2048]{0:T(1024)} %param.15) | copy-start | bytes 24580
  51.8 5.6 %collective-permute-start = (bf16[8,768,128]{2,1,0:T(8,128)(2,1)S(1)}, bf16[8,768,128]{2,1,0:T(8,128)(2,1)S(1)}, u32[]{:S(2)}, u32[]{:S(2)}) collective-permute-start(bf16[8,768,128]{2,1,0:T(8,128)(2,1)S(1)} %all_to_all.36.mine_ref.out_mine_ref), channel_id=1, source_target_pairs={{0,8},{8,0},{1,9},{9,1},{2,10},{10,2},{3,11},{11,3},{4,12},{12,4},... | collective-permute-start | bytes 4718600 | tf_op jit(solution)/shard_map/ppermute | solution.py:57
  60.0 0.7 collective-permute-start.1
  77.2 2.3 collective-permute-start.2
  102.7 19.3 %all-to-all-start.4 = ((bf16[8,256,256]{2,1,0:T(8,128)(2,1)}), bf16[8,256,256]{2,1,0:T(8,128)(2,1)S(1)}, u32[]{:S(2)}, u32[]{:S(2)}) async-start(bf16[8,256,256]{2,1,0:T(8,128)(2,1)} %broadcast_in_dim.171), calls=%async_computation.4 | async-start | bytes 2097152 | tf_op jit(solution)/shard_map/all_to_all | solution.py:62
  125.7 48.7 %all-to-all-start.5 = ((bf16[16,40,2048]{2,1,0:T(8,128)(2,1)}), bf16[16,40,2048]{2,1,0:T(8,128)(2,1)S(1)}, u32[]{:S(2)}, u32[]{:S(2)}) async-start(bf16[16,40,2048]{2,1,0:T(8,128)(2,1)} %copy-done.5), calls=%async_computation.5 | async-start | bytes 5242880 | tf_op jit(solution)/shard_map/all_to_all | solution.py:458
  143.8 16.3 %collective-permute-start.9 = (bf16[256,256]{1,0:T(8,128)(2,1)S(1)}, bf16[256,256]{1,0:T(8,128)(2,1)S(1)}, u32[]{:S(2)}, u32[]{:S(2)}) collective-permute-start(bf16[256,256]{1,0:T(8,128)(2,1)S(1)} %get-tuple-element.56), channel_id=1, source_target_pairs={{0,7},{1,6},{2,5},{3,4},{4,3},{5,2},{6,1},{7,0},{8,15},{9,14},{10,... | collective-permute-start | bytes 393224 | tf_op jit(solution)/shard_map/ppermute | solution.py:477
  144.4 15.7 %collective-permute-start.8 = (bf16[256,256]{1,0:T(8,128)(2,1)S(1)}, bf16[256,256]{1,0:T(8,128)(2,1)S(1)}, u32[]{:S(2)}, u32[]{:S(2)}) collective-permute-start(bf16[256,256]{1,0:T(8,128)(2,1)S(1)} %get-tuple-element.57), channel_id=1, source_target_pairs={{0,6},{1,7},{2,4},{3,5},{4,2},{5,3},{6,0},{7,1},{8,14},{9,15},{10,... | collective-permute-start | bytes 393224 | tf_op jit(solution)/shard_map/ppermute | solution.py:477
  147.0 17.0 %collective-permute-start.7 = (bf16[256,256]{1,0:T(8,128)(2,1)}, bf16[256,256]{1,0:T(8,128)(2,1)}, u32[]{:S(2)}, u32[]{:S(2)}) collective-permute-start(bf16[256,256]{1,0:T(8,128)(2,1)} %get-tuple-element.58), channel_id=1, source_target_pairs={{0,5},{1,4},{2,7},{3,6},{4,1},{5,0},{6,3},{7,2},{8,13},{9,12},{10,... | collective-permute-start | bytes 393224 | tf_op jit(solution)/shard_map/ppermute | solution.py:477
  148.3 25.6 %collective-permute-start.6 = (bf16[256,256]{1,0:T(8,128)(2,1)}, bf16[256,256]{1,0:T(8,128)(2,1)}, u32[]{:S(2)}, u32[]{:S(2)}) collective-permute-start(bf16[256,256]{1,0:T(8,128)(2,1)} %get-tuple-element.59), channel_id=1, source_target_pairs={{0,4},{1,5},{2,6},{3,7},{4,0},{5,1},{6,2},{7,3},{8,12},{9,13},{10,... | collective-permute-start | bytes 393224 | tf_op jit(solution)/shard_map/ppermute | solution.py:477
  149.1 24.8 %collective-permute-start.5 = (bf16[256,256]{1,0:T(8,128)(2,1)}, bf16[256,256]{1,0:T(8,128)(2,1)}, u32[]{:S(2)}, u32[]{:S(2)}) collective-permute-start(bf16[256,256]{1,0:T(8,128)(2,1)} %get-tuple-element.60), channel_id=1, source_target_pairs={{0,3},{1,2},{2,1},{3,0},{4,7},{5,6},{6,5},{7,4},{8,11},{9,10},{10,... | collective-permute-start | bytes 393224 | tf_op jit(solution)/shard_map/ppermute | solution.py:477
  160.1 13.8 %collective-permute-start.4 = (bf16[256,256]{1,0:T(8,128)(2,1)}, bf16[256,256]{1,0:T(8,128)(2,1)S(1)}, u32[]{:S(2)}, u32[]{:S(2)}) collective-permute-start(bf16[256,256]{1,0:T(8,128)(2,1)} %get-tuple-element.61), channel_id=1, source_target_pairs={{0,2},{1,3},{2,0},{3,1},{4,6},{5,7},{6,4},{7,5},{8,10},{9,11},{10,... | collective-permute-start | bytes 393224 | tf_op jit(solution)/shard_map/ppermute | solution.py:477
  160.1 13.8 %collective-permute-start.3 = (bf16[256,256]{1,0:T(8,128)(2,1)}, bf16[256,256]{1,0:T(8,128)(2,1)S(1)}, u32[]{:S(2)}, u32[]{:S(2)}) collective-permute-start(bf16[256,256]{1,0:T(8,128)(2,1)} %get-tuple-element.62), channel_id=1, source_target_pairs={{0,1},{1,0},{2,3},{3,2},{4,5},{5,4},{6,7},{7,6},{8,9},{9,8},{10,11... | collective-permute-start | bytes 393224 | tf_op jit(solution)/shard_map/ppermute | solution.py:477
  186.9 42.0 %copy-start.9 = (bf16[256,5120]{0,1:T(8,128)(2,1)S(1)}, bf16[256,5120]{0,1:T(8,128)(2,1)}, u32[]{:S(2)}) copy-start(bf16[256,5120]{0,1:T(8,128)(2,1)} %fusion) | copy-start | bytes 7864324
  186.9 42.0 %copy-start.16 = (bf16[256,256]{1,0:T(8,128)(2,1)S(1)}, bf16[256,256]{1,0:T(8,128)(2,1)}, u32[]{:S(2)}) copy-start(bf16[256,256]{1,0:T(8,128)(2,1)} %copy-done.15) | copy-start | bytes 393220
  186.9 42.0 %copy-start.21 = (bf16[256,256]{1,0:T(8,128)(2,1)S(1)}, bf16[256,256]{1,0:T(8,128)(2,1)}, u32[]{:S(2)}) copy-start(bf16[256,256]{1,0:T(8,128)(2,1)} %get-tuple-element.25) | copy-start | bytes 393220
  186.9 42.0 %copy-start.27 = (bf16[256,256]{1,0:T(8,128)(2,1)S(1)}, bf16[256,256]{1,0:T(8,128)(2,1)}, u32[]{:S(2)}) copy-start(bf16[256,256]{1,0:T(8,128)(2,1)} %copy-done.26) | copy-start | bytes 393220
  186.9 42.0 %all-to-all-start.6 = ((bf16[128,40,256]{2,1,0:T(8,128)(2,1)}), bf16[128,40,256]{2,1,0:T(8,128)(2,1)}, u32[]{:S(2)}, u32[]{:S(2)}) async-start(bf16[128,40,256]{2,1,0:T(8,128)(2,1)} %bitcast.133), calls=%async_computation.6 | async-start | bytes 5242880 | tf_op jit(solution)/shard_map/all_to_all | solution.py:487
  228.9 22.2 %copy-start.14 = (bf16[16,8,2,128]{3,1,2,0:T(8,128)(2,1)S(1)}, bf16[16,8,2,128]{3,1,2,0:T(8,128)(2,1)}, u32[]{:S(2)}) copy-start(bf16[16,8,2,128]{3,1,2,0:T(8,128)(2,1)} %copy-done.13) | copy-start | bytes 196612
  228.9 22.9 %copy-start.17 = (bf16[128,4,128]{0,2,1:T(8,128)(2,1)S(1)}, bf16[128,4,128]{0,2,1:T(8,128)(2,1)}, u32[]{:S(2)}) copy-start(bf16[128,4,128]{0,2,1:T(8,128)(2,1)} %copy.73) | copy-start | bytes 393220
  231.9 11.3 %collective-permute-start.13 = (bf16[256,256]{1,0:T(8,128)(2,1)S(1)}, bf16[256,256]{1,0:T(8,128)(2,1)S(1)}, u32[]{:S(2)}, u32[]{:S(2)}) collective-permute-start(bf16[256,256]{1,0:T(8,128)(2,1)S(1)} %fusion.1), channel_id=1, source_target_pairs={{0,112},{16,64},{32,80},{48,96},{1,113},{17,65},{33,81},{49,97},{2... | collective-permute-start | bytes 393224 | tf_op jit(solution)/shard_map/ppermute | solution.py:504
  233.2 10.7 %collective-permute-start.12 = (bf16[256,256]{1,0:T(8,128)(2,1)S(1)}, bf16[256,256]{1,0:T(8,128)(2,1)S(1)}, u32[]{:S(2)}, u32[]{:S(2)}) collective-permute-start(bf16[256,256]{1,0:T(8,128)(2,1)S(1)} %fusion.1), channel_id=1, source_target_pairs={{0,96},{16,112},{32,64},{48,80},{1,97},{17,113},{33,65},{49,81},{2... | collective-permute-start | bytes 393224 | tf_op jit(solution)/shard_map/ppermute | solution.py:504
  234.5 13.2 %collective-permute-start.11 = (bf16[256,256]{1,0:T(8,128)(2,1)S(1)}, bf16[256,256]{1,0:T(8,128)(2,1)S(1)}, u32[]{:S(2)}, u32[]{:S(2)}) collective-permute-start(bf16[256,256]{1,0:T(8,128)(2,1)S(1)} %fusion.1), channel_id=1, source_target_pairs={{0,80},{16,96},{32,112},{48,64},{1,81},{17,97},{33,113},{49,65},{2... | collective-permute-start | bytes 393224 | tf_op jit(solution)/shard_map/ppermute | solution.py:504
  235.8 14.8 %collective-permute-start.10 = (bf16[256,256]{1,0:T(8,128)(2,1)S(1)}, bf16[256,256]{1,0:T(8,128)(2,1)S(1)}, u32[]{:S(2)}, u32[]{:S(2)}) collective-permute-start(bf16[256,256]{1,0:T(8,128)(2,1)S(1)} %fusion.1), channel_id=1, source_target_pairs={{0,64},{16,80},{32,96},{48,112},{64,0},{80,16},{96,32},{112,48},{1... | collective-permute-start | bytes 393224 | tf_op jit(solution)/shard_map/ppermute | solution.py:504
  240.7 12.0 %collective-permute-start.18 = (bf16[128,256]{1,0:T(8,128)(2,1)S(1)}, bf16[128,256]{1,0:T(8,128)(2,1)S(1)}, u32[]{:S(2)}, u32[]{:S(2)}) collective-permute-start(bf16[128,256]{1,0:T(8,128)(2,1)S(1)} %slice.179), channel_id=1, source_target_pairs={{56,0},{72,16},{88,32},{104,48},{120,64},{57,1},{73,17},{89,33},{1... | collective-permute-start | bytes 196616 | tf_op jit(solution)/shard_map/ppermute | solution.py:505
  243.2 9.4 %collective-permute-start.17 = (bf16[256,256]{1,0:T(8,128)(2,1)S(1)}, bf16[256,256]{1,0:T(8,128)(2,1)S(1)}, u32[]{:S(2)}, u32[]{:S(2)}) collective-permute-start(bf16[256,256]{1,0:T(8,128)(2,1)S(1)} %collective-permute-done.13.refs_3_), channel_id=1, source_target_pairs={{0,8},{8,0},{1,9},{9,1},{2,10},{10,2},{3,11},{11,3},{4,12},{12,4},... | collective-permute-start | bytes 393224 | tf_op jit(solution)/shard_map/ppermute | solution.py:57
  243.9 8.8 %collective-permute-start.16 = (bf16[256,256]{1,0:T(8,128)(2,1)S(1)}, bf16[256,256]{1,0:T(8,128)(2,1)S(1)}, u32[]{:S(2)}, u32[]{:S(2)}) collective-permute-start(bf16[256,256]{1,0:T(8,128)(2,1)S(1)} %collective-permute-done.12.refs_2_), channel_id=1, source_target_pairs={{0,8},{8,0},{1,9},{9,1},{2,10},{10,2},{3,11},{11,3},{4,12},{12,4},... | collective-permute-start | bytes 393224 | tf_op jit(solution)/shard_map/ppermute | solution.py:57
  247.7 5.0 %collective-permute-start.15 = (bf16[256,256]{1,0:T(8,128)(2,1)S(1)}, bf16[256,256]{1,0:T(8,128)(2,1)S(1)}, u32[]{:S(2)}, u32[]{:S(2)}) collective-permute-start(bf16[256,256]{1,0:T(8,128)(2,1)S(1)} %collective-permute-done.11.refs_1_), channel_id=1, source_target_pairs={{0,8},{8,0},{1,9},{9,1},{2,10},{10,2},{3,11},{11,3},{4,12},{12,4},... | collective-permute-start | bytes 393224 | tf_op jit(solution)/shard_map/ppermute | solution.py:57
  250.6 2.0 collective-permute-start.14
  (23 other events, 190.6 us)

commit v4 on v3

--- a/solution.py
+++ b/solution.py
@@ -13,6 +13,9 @@
 
 ROW = ("zh", "y", "k")
 COL = ("zl", "x")
+DIAGONALS = [
+    [row * 8 + (low ^ (row // 8)) * 4 + x for row in range(16)] for low in range(2) for x in range(4)
+]
 
 epsilon = 1e-06
 rope_base = 600000.0
@@ -296,24 +299,52 @@
 
 
 def expert_kernel(
-    rows_hbm, gate_up_hbm, down_hbm, out_hbm, rows_ref, gate_up_ref, down_ref, out_ref, fetch_sems, sems
+    rows_hbm,
+    gate_up_hbm,
+    down_hbm,
+    out_hbm,
+    rows_ref,
+    gate_up_ref,
+    down_ref,
+    out_ref,
+    product_ref,
+    fetch_sems,
+    sems,
 ):
     units = down_ref.shape[0]
-    pairs = ((gate_up_hbm, gate_up_ref), (rows_hbm, rows_ref), (down_hbm, down_ref))
+    widths = (0, 512, 1024, 2 * units)
     fetches = [
-        pltpu.make_async_copy(source, target, fetch_sems.at[i])
-        for i, (source, target) in enumerate(pairs)
+        pltpu.make_async_copy(rows_hbm.at[:320], rows_ref.at[:320], fetch_sems.at[3])
     ]
+    for i in range(3):
+        lanes = slice(widths[i], widths[i + 1])
+        fetches.append(
+            pltpu.make_async_copy(
+                gate_up_hbm.at[:, lanes], gate_up_ref.at[:, lanes], fetch_sems.at[i]
+            )
+        )
+    fetches.append(pltpu.make_async_copy(rows_hbm.at[320:], rows_ref.at[320:], fetch_sems.at[4]))
+    fetches.append(pltpu.make_async_copy(down_hbm, down_ref, fetch_sems.at[5]))
     for fetch in fetches:
         fetch.start()
     fetches[0].wait()
-    fetches[1].wait()
     copies = []
     for part in range(2):
         rows = slice(part * 320, (part + 1) * 320)
-        gate_up = jnp.dot(rows_ref[rows, :], gate_up_ref[...], preferred_element_type=jnp.float32)
         if part == 0:
-            fetches[2].wait()
+            for i in range(3):
+                lanes = slice(widths[i], widths[i + 1])
+                fetches[1 + i].wait()
+                product_ref[:, lanes] = jnp.dot(
+                    rows_ref[rows, :], gate_up_ref[:, lanes], preferred_element_type=jnp.float32
+                )
+            gate_up = product_ref[...]
+            fetches[4].wait()
+            fetches[5].wait()
+        else:
+            gate_up = jnp.dot(
+                rows_ref[rows, :], gate_up_ref[...], preferred_element_type=jnp.float32
+            )
         hidden = (jax.nn.silu(gate_up[:, :units]) * gate_up[:, units:]).astype(jnp.bfloat16)
         for f in range(8):
             result = jnp.dot(
@@ -341,7 +372,8 @@
             pltpu.VMEM(gate_up.shape, jnp.bfloat16),
             pltpu.VMEM(down.shape, jnp.bfloat16),
             pltpu.VMEM((16, 8, 40, 256), jnp.bfloat16),
-            pltpu.SemaphoreType.DMA((3,)),
+            pltpu.VMEM((320, gate_up.shape[1]), jnp.float32),
+            pltpu.SemaphoreType.DMA((6,)),
             pltpu.SemaphoreType.DMA((16,)),
         ],
         compiler_params=pltpu.CompilerParams(vmem_limit_bytes=60 << 20),
@@ -451,11 +483,16 @@
     expert_ids = jnp.arange(n_experts, dtype=jnp.int32)
     member = jnp.any(routes[:, :, None] == expert_ids[None, None, :], axis=1)
     slot_of = jnp.where(member, jnp.cumsum(member.astype(jnp.int32), axis=0) - 1, -1)
-    slots = lax.dynamic_index_in_dim(
-        slot_of.reshape(tok_rows, row_count, col_count // 2), col_index // 2, 2, keepdims=False
-    ).T
+    by_quarter = slot_of.reshape(tok_rows, row_count, col_count // 2)
+    quarter = col_index // 2
+    straight = lax.dynamic_index_in_dim(by_quarter, quarter, 2, keepdims=False)
+    crossed = lax.dynamic_index_in_dim(by_quarter, quarter ^ 2, 2, keepdims=False)
+    same_half = (jnp.arange(row_count) // 8 == zh_index)[None, :]
+    slots = jnp.where(same_half, straight, crossed).T
     mlp_in, outgoing = dispatch(full_resid, mlp_gain[None, :], slots)
-    arrived = lax.all_to_all(outgoing, ROW, 0, 0, tiled=True)
+    arrived = lax.all_to_all(
+        outgoing, ROW + COL, 0, 0, axis_index_groups=DIAGONALS, tiled=True
+    )
 
     logits = jnp.dot(mlp_in, router, preferred_element_type=jnp.float32)
     router_probs = jax.nn.softmax(logits, axis=-1)

time: 254 us -> 247 us (0.972)
  blocking collectives: 80.9 us -> 62.4 us
  waiting for transfers between devices: 73.3 us -> 81.5 us
    all_to_all x1 -> x2, waiting for transfers between devices: 0.52 us -> 21.1 us  [the longest x1 14.7 us: on_device(): got = lax.all_to_all(terms, COL, 0, 0, tiled=True)]
    all_to_all x1 -> x0, blocking collectives: 18.4 us -> none  [on_device(): got = lax.all_to_all(terms, COL, 0, 0, tiled=True)]
    ppermute x7, waiting for transfers between devices: 19 us -> 6.71 us  [on_device(): piece = lax.ppermute(piece, COL, [(i, i ^ step) for i in range(col_count)])]
    all_to_all x1 -> x2, starting transfers between devices: 7.19 us -> 11.9 us  [the longest x1 6.84 us: on_device(): lax.all_to_all(outgoing, ROW + COL, 0, 0, axis_index_groups=DIAGONALS, ti...]
    unnamed x77 -> x78, local copies, waits for them, and re-layouts: 8.74 us -> 9.76 us
  transfers between devices with their start and end apart: 22 -> 23, of which waited for: 9 -> 11; matrix products, arithmetic and copies ran while one was open for 6% -> 6% of each run, Pallas kernels for 2% -> 2%
where the time goes in v4:
time: 247 us; the launch traced here: 246 us
  waiting for transfers between devices  81.5 us (33%)
  blocking collectives  62.4 us (25%)
  starting transfers between devices  48.6 us (20%)
  Pallas kernels  22 us (9%)
  local copies, waits for them, and re-layouts  18 us (7%)
  other arithmetic  8.79 us (4%)
  matrix products  3.39 us (1%)
    all_to_all x1, waiting for transfers between devices, on_device(): lax.all_to_all(result.reshape(2 * n_experts, capacity, 256), ROW + COL, 0...  32.3 us
    all_to_all x1, blocking collectives, on_device(): lax.all_to_all(jnp.broadcast_to(block[None], (8, 768, HEAD_DIM)), ('zh',...  25.2 us
    all_to_all x1, blocking collectives, on_device(): lax.all_to_all(jnp.concatenate([groups, jnp.broadcast_to(token_parts, (8,...  20.9 us
    all_to_all x1, blocking collectives, on_device(): lax.all_to_all(jnp.broadcast_to(block[None], (4, 384, 256)), 'y', 0, 0, t...  16.4 us
    all_to_all x1, waiting for transfers between devices, on_device(): got = lax.all_to_all(terms, COL, 0, 0, tiled=True)  14.7 us
    all_to_all x1, waiting for transfers between devices, col_gather(): return lax.all_to_all(copies, COL, 0, 0, tiled=True)  13.5 us
    pallas_call x1, Pallas kernels, expert(): pl.pallas_call(expert_kernel, in_specs=in_hbm(3), out_specs=in_hbm(1)[0],...  9.85 us
    unnamed x78, local copies, waits for them, and re-layouts  9.76 us
  transfers between devices with their start and end apart: 23, of which 11 were waited for; matrix products, arithmetic and copies ran while one was open for 6% of the time, Pallas kernels for 2%

profile of v4, /device:TPU:97, one launch (start us, length us, event | category | flops | bytes accessed | tf_op | source)
XLA Modules:
  0.0 246.1 jit_solution(9181734901173618329)
XLA Ops:
  4.0 20.9 %all_to_all.35.came_ref = bf16[8,608,128]{2,1,0:T(8,128)(2,1)S(1)} all-to-all(bf16[8,608,128]{2,1,0:T(8,128)(2,1)S(1)} %pad_maximum_fusion), channel_id=1, replica_groups=mesh['zh'=2,'y'=4,'k'=2,'zl'=2,'x'=4] {'zl','x'}, dimensions={0} | all-to-all | bytes 2490368 | tf_op jit(solution)/shard_map/all_to_all | solution.py:448
  26.7 25.2 %all_to_all.36.mine_ref.out_mine_ref = bf16[8,768,128]{2,1,0:T(8,128)(2,1)S(1)} all-to-all(bf16[8,768,128]{2,1,0:T(8,128)(2,1)S(1)} %broadcast_in_dim.176), channel_id=1, replica_groups=mesh['zh'=2,'y'=4,'k'=2,'zl'=2,'x'=4] {'zh','y'}, dimensions={0} | all-to-all | bytes 3145728 | tf_op jit(solution)/shard_map/all_to_all | solution.py:459
  51.8 2.6 %collective-permute-start = (bf16[8,768,128]{2,1,0:T(8,128)(2,1)S(1)}, bf16[8,768,128]{2,1,0:T(8,128)(2,1)S(1)}, u32[]{:S(2)}, u32[]{:S(2)}) collective-permute-start(bf16[8,768,128]{2,1,0:T(8,128)(2,1)S(1)} %all_to_all.36.mine_ref.out_mine_ref), channel_id=1, source_target_pairs={{0,8},{8,0},{1,9},{9,1},{2,10},{10,2},{3,11},{11,3},{4,12},{12,4},... | collective-permute-start | bytes 4718600 | tf_op jit(solution)/shard_map/ppermute | solution.py:60
  55.7 1.8 collective-permute-done.other_ref.out_other_ref
  60.8 16.4 %all_to_all.37.mine_ref = bf16[4,384,256]{2,1,0:T(8,128)(2,1)S(1)} all-to-all(bf16[4,384,256]{2,1,0:T(8,128)(2,1)S(1)} %broadcast_in_dim.179), channel_id=1, replica_groups=mesh['zh'=2,'y'=4,'k'=2,'zl'=2,'x'=4] {'y'}, dimensions={0} | all-to-all | bytes 1572864 | tf_op jit(solution)/shard_map/all_to_all | solution.py:471
  77.2 2.3 collective-permute-done.2.other_ref
  79.5 3.6 %attention.1 = bf16[8,256,256]{2,1,0:T(8,128)(2,1)S(1)} custom-call(bf16[2,256,128]{2,1,0:T(8,128)(2,1)S(1)} %get-tuple-element.21.q_hbm, bf16[4,384,256]{2,1,0:T(8,128)(2,1)S(1)} %all_to_all.37.mine_ref, bf16[4,384,256]{2,1,0:T(8,128)(2,1)S(1)} %collective-permute-done.2.other_ref, s32[8]{0:T(128)S(1)} %bitcast_subtract_fusion.1.start_ref, ...), custom_call_target="tpu_custom_call" | custom-call | tf_op jit(solution)/shard_map/attention/pallas_call | solution.py:210
  84.1 5.1 %all-to-all-start.3 = ((bf16[8,256,256]{2,1,0:T(8,128)(2,1)}), bf16[8,256,256]{2,1,0:T(8,128)(2,1)S(1)}, u32[]{:S(2)}, u32[]{:S(2)}) async-start(bf16[8,256,256]{2,1,0:T(8,128)(2,1)} %copy-done.5), calls=%async_computation.3 | async-start | bytes 2097152 | tf_op jit(solution)/shard_map/all_to_all | solution.py:476
  89.2 14.7 %all-to-all-done.3 = bf16[8,256,256]{2,1,0:T(8,128)(2,1)S(1)} async-done(((bf16[8,256,256]{2,1,0:T(8,128)(2,1)}), bf16[8,256,256]{2,1,0:T(8,128)(2,1)S(1)}, u32[]{:S(2)}, u32[]{:S(2)}) %all-to-all-start.3) | async-done | bytes 1048608 | tf_op jit(solution)/shard_map/all_to_all | solution.py:476
  105.2 4.7 %all-to-all-start.4 = ((bf16[8,256,256]{2,1,0:T(8,128)(2,1)}), bf16[8,256,256]{2,1,0:T(8,128)(2,1)S(1)}, u32[]{:S(2)}, u32[]{:S(2)}) async-start(bf16[8,256,256]{2,1,0:T(8,128)(2,1)} %broadcast_in_dim.180), calls=%async_computation.4 | async-start | bytes 2097152 | tf_op jit(solution)/shard_map/all_to_all | solution.py:65
  111.0 13.5 %all-to-all-done.4.resid_ref = bf16[8,256,256]{2,1,0:T(8,128)(2,1)S(1)} async-done(((bf16[8,256,256]{2,1,0:T(8,128)(2,1)}), bf16[8,256,256]{2,1,0:T(8,128)(2,1)S(1)}, u32[]{:S(2)}, u32[]{:S(2)}) %all-to-all-start.4) | async-done | bytes 1048608 | tf_op jit(solution)/shard_map/all_to_all | solution.py:65
  126.7 1.5 copy-done.6
  128.2 6.8 %all-to-all-start.5 = ((bf16[16,40,2048]{2,1,0:T(8,128)(2,1)}), bf16[16,40,2048]{2,1,0:T(8,128)(2,1)S(1)}, u32[]{:S(2)}, u32[]{:S(2)}) async-start(bf16[16,40,2048]{2,1,0:T(8,128)(2,1)} %copy-done.6), calls=%async_computation.5 | async-start | bytes 5242880 | tf_op jit(solution)/shard_map/all_to_all | solution.py:493
  138.8 5.0 %shared.1 = bf16[8,256,256]{2,1,0:T(8,128)(2,1)} custom-call(bf16[256,2048]{1,0:T(8,128)(2,1)} %copy-done.3, bf16[352,2048]{1,0:T(8,128)(2,1)} %bitcast.142, bf16[352,2048]{1,0:T(8,128)(2,1)} %bitcast.143, bf16[352,2048]{1,0:T(8,128)(2,1)} %down_hbm.1), custom_call_target="tpu_custom_call" | custom-call | tf_op jit(solution)/shard_map/shared/pallas_call | solution.py:284
  143.8 2.2 slice_bitcast_fusion
  146.5 2.7 %collective-permute-start.8 = (bf16[256,256]{1,0:T(8,128)(2,1)S(1)}, bf16[256,256]{1,0:T(8,128)(2,1)S(1)}, u32[]{:S(2)}, u32[]{:S(2)}) collective-permute-start(bf16[256,256]{1,0:T(8,128)(2,1)S(1)} %get-tuple-element.57), channel_id=1, source_target_pairs={{0,6},{1,7},{2,4},{3,5},{4,2},{5,3},{6,0},{7,1},{8,14},{9,15},{10,... | collective-permute-start | bytes 393224 | tf_op jit(solution)/shard_map/ppermute | solution.py:514
  149.5 1.8 collective-permute-start.6
  152.1 4.9 %collective-permute-done.9 = bf16[256,256]{1,0:T(8,128)(2,1)S(1)} collective-permute-done((bf16[256,256]{1,0:T(8,128)(2,1)S(1)}, bf16[256,256]{1,0:T(8,128)(2,1)S(1)}, u32[]{:S(2)}, u32[]{:S(2)}) %collective-permute-start.9) | collective-permute-done | bytes 131104 | tf_op jit(solution)/shard_map/ppermute | solution.py:514
  157.8 3.2 %fusion = bf16[256,5120]{0,1:T(8,128)(2,1)} fusion(s32[5120]{0:T(1024)S(1)} %copy-done.23, s32[256,128]{0,1:T(8,128)} %eq.176, bf16[256,128]{0,1:T(8,128)(2,1)S(1)} %broadcast_in_dim.186), kind=kLoop, calls=%fused_computation.1 | loop fusion | flops 2621440 | bytes 2838528 | tf_op jit(solution)/shard_map/jit(_where)/select_n | solution.py:504
  162.8 6.4 %all-to-all-done.5 = bf16[16,40,2048]{2,1,0:T(8,128)(2,1)S(1)} async-done(((bf16[16,40,2048]{2,1,0:T(8,128)(2,1)}), bf16[16,40,2048]{2,1,0:T(8,128)(2,1)S(1)}, u32[]{:S(2)}, u32[]{:S(2)}) %all-to-all-start.5) | async-done | bytes 2621472 | tf_op jit(solution)/shard_map/all_to_all | solution.py:493
  169.2 1.5 copy-done.9
  170.7 9.9 %expert.1 = bf16[16,8,40,256]{3,2,1,0:T(8,128)(2,1)} custom-call(bf16[640,2048]{1,0:T(8,128)(2,1)} %bitcast.138, bf16[2048,1408]{1,0:T(8,128)(2,1)} %bitcast.140, bf16[704,2048]{1,0:T(8,128)(2,1)} %bitcast.141), custom_call_target="tpu_custom_call" | custom-call | tf_op jit(solution)/shard_map/expert/pallas_call | solution.py:365
  180.6 7.8 %all-to-all-start.6 = ((bf16[128,40,256]{2,1,0:T(8,128)(2,1)}), bf16[128,40,256]{2,1,0:T(8,128)(2,1)}, u32[]{:S(2)}, u32[]{:S(2)}) async-start(bf16[128,40,256]{2,1,0:T(8,128)(2,1)} %bitcast.139), calls=%async_computation.6 | async-start | bytes 5242880 | tf_op jit(solution)/shard_map/all_to_all | solution.py:524
  188.9 32.3 %all-to-all-done.6 = bf16[128,40,256]{2,1,0:T(8,128)(2,1)} async-done(((bf16[128,40,256]{2,1,0:T(8,128)(2,1)}), bf16[128,40,256]{2,1,0:T(8,128)(2,1)}, u32[]{:S(2)}, u32[]{:S(2)}) %all-to-all-start.6) | async-done | bytes 2621472 | tf_op jit(solution)/shard_map/all_to_all | solution.py:524
  221.3 2.9 %fusion.1 = bf16[256,256]{1,0:T(8,128)(2,1)S(1)} fusion(bf16[256,5120]{0,1:T(8,128)(2,1)S(1)} %copy-done.10, bf16[5120,256]{1,0:T(8,128)(2,1)} %bitcast.52, bf16[256,256]{1,0:T(8,128)(2,1)S(1)} %copy-done.28, bf16[256,256]{1,0:T(8,128)(2,1)} %copy-done.29, bf16[256,256]{1,0:T(8,128)(2,1)} %collective-permute-done.7, ...), kind=kOutput, calls=%fused_computation.5 | convolution fusion | flops 672333824 | bytes 6553600 | tf_op jit(solution)/shard_map/dot_general | solution.py:527
  224.2 1.3 collective-permute-start.13
  225.5 1.3 collective-permute-start.12
  228.1 4.8 %collective-permute-start.10 = (bf16[256,256]{1,0:T(8,128)(2,1)S(1)}, bf16[256,256]{1,0:T(8,128)(2,1)S(1)}, u32[]{:S(2)}, u32[]{:S(2)}) collective-permute-start(bf16[256,256]{1,0:T(8,128)(2,1)S(1)} %fusion.1), channel_id=1, source_target_pairs={{0,64},{16,80},{32,96},{48,112},{64,0},{80,16},{96,32},{112,48},{1... | collective-permute-start | bytes 393224 | tf_op jit(solution)/shard_map/ppermute | solution.py:541
  233.0 2.5 %collective-permute-start.18 = (bf16[128,256]{1,0:T(8,128)(2,1)S(1)}, bf16[128,256]{1,0:T(8,128)(2,1)S(1)}, u32[]{:S(2)}, u32[]{:S(2)}) collective-permute-start(bf16[128,256]{1,0:T(8,128)(2,1)S(1)} %slice.179), channel_id=1, source_target_pairs={{56,0},{72,16},{88,32},{104,48},{120,64},{57,1},{73,17},{89,33},{1... | collective-permute-start | bytes 196616 | tf_op jit(solution)/shard_map/ppermute | solution.py:542
  236.2 2.2 collective-permute-start.16
  238.4 1.6 collective-permute-done.11.refs_1_
  240.9 2.1 collective-permute-done.10.refs_0_
  (174 shorter events, 29.4 us)
Async XLA Ops:
  0.6 150.9 %copy-start = (bf16[2048,64]{0,1:T(8,128)(2,1)S(1)}, bf16[2048,64]{0,1:T(8,128)(2,1)}, u32[]{:S(2)}) copy-start(bf16[2048,64]{0,1:T(8,128)(2,1)} %param.19) | copy-start | bytes 786436
  26.4 28.0 %copy-start.25 = (s32[8]{0:T(128)S(1)}, s32[8]{0:T(128)}, u32[]{:S(2)}) copy-start(s32[8]{0:T(128)} %param.26) | copy-start | bytes 100
  26.4 28.0 %copy-start.32 = (s32[8]{0:T(128)S(1)}, s32[8]{0:T(128)}, u32[]{:S(2)}) copy-start(s32[8]{0:T(128)} %param.25) | copy-start | bytes 100
  26.6 30.8 %copy-start.7 = (f32[2048]{0:T(1024)S(1)}, f32[2048]{0:T(1024)}, u32[]{:S(2)}) copy-start(f32[2048]{0:T(1024)} %param.15) | copy-start | bytes 24580
  51.8 5.6 %collective-permute-start = (bf16[8,768,128]{2,1,0:T(8,128)(2,1)S(1)}, bf16[8,768,128]{2,1,0:T(8,128)(2,1)S(1)}, u32[]{:S(2)}, u32[]{:S(2)}) collective-permute-start(bf16[8,768,128]{2,1,0:T(8,128)(2,1)S(1)} %all_to_all.36.mine_ref.out_mine_ref), channel_id=1, source_target_pairs={{0,8},{8,0},{1,9},{9,1},{2,10},{10,2},{3,11},{11,3},{4,12},{12,4},... | collective-permute-start | bytes 4718600 | tf_op jit(solution)/shard_map/ppermute | solution.py:60
  60.0 0.7 collective-permute-start.1
  77.2 2.3 collective-permute-start.2
  84.1 19.8 %all-to-all-start.3 = ((bf16[8,256,256]{2,1,0:T(8,128)(2,1)}), bf16[8,256,256]{2,1,0:T(8,128)(2,1)S(1)}, u32[]{:S(2)}, u32[]{:S(2)}) async-start(bf16[8,256,256]{2,1,0:T(8,128)(2,1)} %copy-done.5), calls=%async_computation.3 | async-start | bytes 2097152 | tf_op jit(solution)/shard_map/all_to_all | solution.py:476
  105.2 19.4 %all-to-all-start.4 = ((bf16[8,256,256]{2,1,0:T(8,128)(2,1)}), bf16[8,256,256]{2,1,0:T(8,128)(2,1)S(1)}, u32[]{:S(2)}, u32[]{:S(2)}) async-start(bf16[8,256,256]{2,1,0:T(8,128)(2,1)} %broadcast_in_dim.180), calls=%async_computation.4 | async-start | bytes 2097152 | tf_op jit(solution)/shard_map/all_to_all | solution.py:65
  128.2 41.0 %all-to-all-start.5 = ((bf16[16,40,2048]{2,1,0:T(8,128)(2,1)}), bf16[16,40,2048]{2,1,0:T(8,128)(2,1)S(1)}, u32[]{:S(2)}, u32[]{:S(2)}) async-start(bf16[16,40,2048]{2,1,0:T(8,128)(2,1)} %copy-done.6), calls=%async_computation.5 | async-start | bytes 5242880 | tf_op jit(solution)/shard_map/all_to_all | solution.py:493
  146.0 11.0 %collective-permute-start.9 = (bf16[256,256]{1,0:T(8,128)(2,1)S(1)}, bf16[256,256]{1,0:T(8,128)(2,1)S(1)}, u32[]{:S(2)}, u32[]{:S(2)}) collective-permute-start(bf16[256,256]{1,0:T(8,128)(2,1)S(1)} %get-tuple-element.56), channel_id=1, source_target_pairs={{0,7},{1,6},{2,5},{3,4},{4,3},{5,2},{6,1},{7,0},{8,15},{9,14},{10,... | collective-permute-start | bytes 393224 | tf_op jit(solution)/shard_map/ppermute | solution.py:514
  146.5 10.5 %collective-permute-start.8 = (bf16[256,256]{1,0:T(8,128)(2,1)S(1)}, bf16[256,256]{1,0:T(8,128)(2,1)S(1)}, u32[]{:S(2)}, u32[]{:S(2)}) collective-permute-start(bf16[256,256]{1,0:T(8,128)(2,1)S(1)} %get-tuple-element.57), channel_id=1, source_target_pairs={{0,6},{1,7},{2,4},{3,5},{4,2},{5,3},{6,0},{7,1},{8,14},{9,15},{10,... | collective-permute-start | bytes 393224 | tf_op jit(solution)/shard_map/ppermute | solution.py:514
  149.2 11.8 %collective-permute-start.7 = (bf16[256,256]{1,0:T(8,128)(2,1)}, bf16[256,256]{1,0:T(8,128)(2,1)}, u32[]{:S(2)}, u32[]{:S(2)}) collective-permute-start(bf16[256,256]{1,0:T(8,128)(2,1)} %get-tuple-element.58), channel_id=1, source_target_pairs={{0,5},{1,4},{2,7},{3,6},{4,1},{5,0},{6,3},{7,2},{8,13},{9,12},{10,... | collective-permute-start | bytes 393224 | tf_op jit(solution)/shard_map/ppermute | solution.py:514
  149.5 12.5 %collective-permute-start.6 = (bf16[256,256]{1,0:T(8,128)(2,1)}, bf16[256,256]{1,0:T(8,128)(2,1)}, u32[]{:S(2)}, u32[]{:S(2)}) collective-permute-start(bf16[256,256]{1,0:T(8,128)(2,1)} %get-tuple-element.59), channel_id=1, source_target_pairs={{0,4},{1,5},{2,6},{3,7},{4,0},{5,1},{6,2},{7,3},{8,12},{9,13},{10,... | collective-permute-start | bytes 393224 | tf_op jit(solution)/shard_map/ppermute | solution.py:514
  151.3 10.7 %collective-permute-start.5 = (bf16[256,256]{1,0:T(8,128)(2,1)}, bf16[256,256]{1,0:T(8,128)(2,1)}, u32[]{:S(2)}, u32[]{:S(2)}) collective-permute-start(bf16[256,256]{1,0:T(8,128)(2,1)} %get-tuple-element.60), channel_id=1, source_target_pairs={{0,3},{1,2},{2,1},{3,0},{4,7},{5,6},{6,5},{7,4},{8,11},{9,10},{10,... | collective-permute-start | bytes 393224 | tf_op jit(solution)/shard_map/ppermute | solution.py:514
  157.0 5.8 %collective-permute-start.4 = (bf16[256,256]{1,0:T(8,128)(2,1)}, bf16[256,256]{1,0:T(8,128)(2,1)S(1)}, u32[]{:S(2)}, u32[]{:S(2)}) collective-permute-start(bf16[256,256]{1,0:T(8,128)(2,1)} %get-tuple-element.61), channel_id=1, source_target_pairs={{0,2},{1,3},{2,0},{3,1},{4,6},{5,7},{6,4},{7,5},{8,10},{9,11},{10,... | collective-permute-start | bytes 393224 | tf_op jit(solution)/shard_map/ppermute | solution.py:514
  157.0 5.8 %collective-permute-start.3 = (bf16[256,256]{1,0:T(8,128)(2,1)}, bf16[256,256]{1,0:T(8,128)(2,1)S(1)}, u32[]{:S(2)}, u32[]{:S(2)}) collective-permute-start(bf16[256,256]{1,0:T(8,128)(2,1)} %get-tuple-element.62), channel_id=1, source_target_pairs={{0,1},{1,0},{2,3},{3,2},{4,5},{5,4},{6,7},{7,6},{8,9},{9,8},{10,11... | collective-permute-start | bytes 393224 | tf_op jit(solution)/shard_map/ppermute | solution.py:514
  180.6 40.7 %copy-start.10 = (bf16[256,5120]{0,1:T(8,128)(2,1)S(1)}, bf16[256,5120]{0,1:T(8,128)(2,1)}, u32[]{:S(2)}) copy-start(bf16[256,5120]{0,1:T(8,128)(2,1)} %fusion) | copy-start | bytes 7864324
  180.6 40.7 %copy-start.18 = (bf16[256,256]{1,0:T(8,128)(2,1)S(1)}, bf16[256,256]{1,0:T(8,128)(2,1)}, u32[]{:S(2)}) copy-start(bf16[256,256]{1,0:T(8,128)(2,1)} %copy-done.17) | copy-start | bytes 393220
  180.6 40.6 %copy-start.22 = (bf16[256,256]{1,0:T(8,128)(2,1)S(1)}, bf16[256,256]{1,0:T(8,128)(2,1)}, u32[]{:S(2)}) copy-start(bf16[256,256]{1,0:T(8,128)(2,1)} %get-tuple-element.25) | copy-start | bytes 393220
  180.6 40.6 %copy-start.28 = (bf16[256,256]{1,0:T(8,128)(2,1)S(1)}, bf16[256,256]{1,0:T(8,128)(2,1)}, u32[]{:S(2)}) copy-start(bf16[256,256]{1,0:T(8,128)(2,1)} %copy-done.27) | copy-start | bytes 393220
  180.6 40.6 %all-to-all-start.6 = ((bf16[128,40,256]{2,1,0:T(8,128)(2,1)}), bf16[128,40,256]{2,1,0:T(8,128)(2,1)}, u32[]{:S(2)}, u32[]{:S(2)}) async-start(bf16[128,40,256]{2,1,0:T(8,128)(2,1)} %bitcast.139), calls=%async_computation.6 | async-start | bytes 5242880 | tf_op jit(solution)/shard_map/all_to_all | solution.py:524
  221.3 22.9 %copy-start.16 = (bf16[128,4,128]{0,2,1:T(8,128)(2,1)S(1)}, bf16[128,4,128]{0,2,1:T(8,128)(2,1)}, u32[]{:S(2)}) copy-start(bf16[128,4,128]{0,2,1:T(8,128)(2,1)} %copy.78) | copy-start | bytes 393220
  224.2 11.3 %collective-permute-start.13 = (bf16[256,256]{1,0:T(8,128)(2,1)S(1)}, bf16[256,256]{1,0:T(8,128)(2,1)S(1)}, u32[]{:S(2)}, u32[]{:S(2)}) collective-permute-start(bf16[256,256]{1,0:T(8,128)(2,1)S(1)} %fusion.1), channel_id=1, source_target_pairs={{0,112},{16,64},{32,80},{48,96},{1,113},{17,65},{33,81},{49,97},{2... | collective-permute-start | bytes 393224 | tf_op jit(solution)/shard_map/ppermute | solution.py:541
  225.5 10.7 %collective-permute-start.12 = (bf16[256,256]{1,0:T(8,128)(2,1)S(1)}, bf16[256,256]{1,0:T(8,128)(2,1)S(1)}, u32[]{:S(2)}, u32[]{:S(2)}) collective-permute-start(bf16[256,256]{1,0:T(8,128)(2,1)S(1)} %fusion.1), channel_id=1, source_target_pairs={{0,96},{16,112},{32,64},{48,80},{1,97},{17,113},{33,65},{49,81},{2... | collective-permute-start | bytes 393224 | tf_op jit(solution)/shard_map/ppermute | solution.py:541
  226.8 13.2 %collective-permute-start.11 = (bf16[256,256]{1,0:T(8,128)(2,1)S(1)}, bf16[256,256]{1,0:T(8,128)(2,1)S(1)}, u32[]{:S(2)}, u32[]{:S(2)}) collective-permute-start(bf16[256,256]{1,0:T(8,128)(2,1)S(1)} %fusion.1), channel_id=1, source_target_pairs={{0,80},{16,96},{32,112},{48,64},{1,81},{17,97},{33,113},{49,65},{2... | collective-permute-start | bytes 393224 | tf_op jit(solution)/shard_map/ppermute | solution.py:541
  228.1 14.8 %collective-permute-start.10 = (bf16[256,256]{1,0:T(8,128)(2,1)S(1)}, bf16[256,256]{1,0:T(8,128)(2,1)S(1)}, u32[]{:S(2)}, u32[]{:S(2)}) collective-permute-start(bf16[256,256]{1,0:T(8,128)(2,1)S(1)} %fusion.1), channel_id=1, source_target_pairs={{0,64},{16,80},{32,96},{48,112},{64,0},{80,16},{96,32},{112,48},{1... | collective-permute-start | bytes 393224 | tf_op jit(solution)/shard_map/ppermute | solution.py:541
  233.0 11.9 %collective-permute-start.18 = (bf16[128,256]{1,0:T(8,128)(2,1)S(1)}, bf16[128,256]{1,0:T(8,128)(2,1)S(1)}, u32[]{:S(2)}, u32[]{:S(2)}) collective-permute-start(bf16[128,256]{1,0:T(8,128)(2,1)S(1)} %slice.179), channel_id=1, source_target_pairs={{56,0},{72,16},{88,32},{104,48},{120,64},{57,1},{73,17},{89,33},{1... | collective-permute-start | bytes 196616 | tf_op jit(solution)/shard_map/ppermute | solution.py:542
  235.6 9.4 %collective-permute-start.17 = (bf16[256,256]{1,0:T(8,128)(2,1)S(1)}, bf16[256,256]{1,0:T(8,128)(2,1)S(1)}, u32[]{:S(2)}, u32[]{:S(2)}) collective-permute-start(bf16[256,256]{1,0:T(8,128)(2,1)S(1)} %collective-permute-done.13.refs_3_), channel_id=1, source_target_pairs={{0,8},{8,0},{1,9},{9,1},{2,10},{10,2},{3,11},{11,3},{4,12},{12,4},... | collective-permute-start | bytes 393224 | tf_op jit(solution)/shard_map/ppermute | solution.py:60
  236.2 8.8 %collective-permute-start.16 = (bf16[256,256]{1,0:T(8,128)(2,1)S(1)}, bf16[256,256]{1,0:T(8,128)(2,1)S(1)}, u32[]{:S(2)}, u32[]{:S(2)}) collective-permute-start(bf16[256,256]{1,0:T(8,128)(2,1)S(1)} %collective-permute-done.12.refs_2_), channel_id=1, source_target_pairs={{0,8},{8,0},{1,9},{9,1},{2,10},{10,2},{3,11},{11,3},{4,12},{12,4},... | collective-permute-start | bytes 393224 | tf_op jit(solution)/shard_map/ppermute | solution.py:60
  240.0 5.0 %collective-permute-start.15 = (bf16[256,256]{1,0:T(8,128)(2,1)S(1)}, bf16[256,256]{1,0:T(8,128)(2,1)S(1)}, u32[]{:S(2)}, u32[]{:S(2)}) collective-permute-start(bf16[256,256]{1,0:T(8,128)(2,1)S(1)} %collective-permute-done.11.refs_1_), channel_id=1, source_target_pairs={{0,8},{8,0},{1,9},{9,1},{2,10},{10,2},{3,11},{11,3},{4,12},{12,4},... | collective-permute-start | bytes 393224 | tf_op jit(solution)/shard_map/ppermute | solution.py:60
  243.0 2.0 collective-permute-start.14
  (25 other events, 239.1 us)

commit v5 on v4

--- a/solution.py
+++ b/solution.py
@@ -138,7 +138,7 @@
 
 
 def attention_kernel(
-    q_hbm, mine_ref, other_ref, start_ref, out_mine_ref, out_other_ref, terms_ref, s_ref, q_ref, sems
+    q_hbm, mine_ref, other_ref, start_ref, out_mine_ref, out_other_ref, terms_ref, qkv_ref, out_ref, s_ref, q_ref, sems
 ):
     half, core = lax.axis_index("zh"), lax.axis_index("k")
     first = half * 2048 + lax.axis_index("y") * 512 + core * 256
@@ -196,6 +196,11 @@
             at += height
         heads.append((total / jnp.sum(sums, axis=1, keepdims=True)).astype(jnp.bfloat16))
     attended = jnp.concatenate(heads, axis=1)
+    own = half * 4 + lax.axis_index("y")
+    for h in range(4):
+        lanes = slice(h * HEAD_DIM, (h + 1) * HEAD_DIM)
+        qkv_ref[:, lanes] = out_mine_ref[own, lanes, :]
+    out_ref[...] = out_mine_ref[own, 512:768, :]
     for f in range(8):
         mine = out_mine_ref[f, 512:768, :]
         other = out_other_ref[f, 512:768, :]
@@ -213,7 +218,11 @@
         + in_vmem(2)
         + [pl.BlockSpec(memory_space=pltpu.SMEM)]
         + in_vmem(2),
-        out_shape=jax.ShapeDtypeStruct((8, 256, 256), jnp.bfloat16),
+        out_shape=(
+            jax.ShapeDtypeStruct((8, 256, 256), jnp.bfloat16),
+            jax.ShapeDtypeStruct((128, 512), jnp.bfloat16),
+            jax.ShapeDtypeStruct((256, 128), jnp.bfloat16),
+        ),
         scratch_shapes=[
             pltpu.VMEM((256, 2176), jnp.float32),
             pltpu.VMEM((2, 256, HEAD_DIM), jnp.bfloat16),
@@ -224,7 +233,7 @@
     )(queries, mine, other, start, out_mine, out_other)
 
 
-def dispatch_kernel(resid_ref, gain_ref, slots_ref, mlp_ref, out_ref):
+def dispatch_kernel(resid_ref, gain_ref, slots_ref, out_ref):
     squares = jnp.zeros((256, 256), jnp.float32)
     for f in range(8):
         x = resid_ref[f].astype(jnp.float32)
@@ -237,7 +246,6 @@
     for f in range(8):
         lanes = slice(f * 256, (f + 1) * 256)
         rows = (resid_ref[f].astype(jnp.float32) * level * gain_ref[:, lanes]).astype(jnp.bfloat16)
-        mlp_ref[:, lanes] = rows
         picked = jnp.dot(picker, rows, preferred_element_type=jnp.float32)
         for r in range(16):
             out_ref[r, :, lanes] = picked[r * 40 : (r + 1) * 40].astype(jnp.bfloat16)
@@ -246,29 +254,52 @@
 def dispatch(full_resid, gain, slots):
     return pl.pallas_call(
         dispatch_kernel,
-        out_shape=(
-            jax.ShapeDtypeStruct((256, D), jnp.bfloat16),
-            jax.ShapeDtypeStruct((16, 40, D), jnp.bfloat16),
-        ),
+        out_shape=jax.ShapeDtypeStruct((16, 40, D), jnp.bfloat16),
         compiler_params=pltpu.CompilerParams(vmem_limit_bytes=16 << 20),
         name="dispatch",
     )(full_resid, gain, slots)
 
 
 def shared_kernel(
-    rows_hbm, gate_hbm, up_hbm, down_hbm, out_ref, rows_ref, gate_ref, up_ref, down_ref, sems
+    resid_hbm,
+    gain_ref,
+    router_ref,
+    gate_hbm,
+    up_hbm,
+    down_hbm,
+    out_ref,
+    logits_ref,
+    resid_ref,
+    rows_ref,
+    gate_ref,
+    up_ref,
+    down_ref,
+    sems,
 ):
-    pairs = ((rows_hbm, rows_ref), (gate_hbm, gate_ref), (up_hbm, up_ref), (down_hbm, down_ref))
+    pairs = ((resid_hbm, resid_ref), (gate_hbm, gate_ref), (up_hbm, up_ref), (down_hbm, down_ref))
     fetches = [
         pltpu.make_async_copy(source, target, sems.at[i]) for i, (source, target) in enumerate(pairs)
     ]
     for fetch in fetches:
         fetch.start()
+    col = lax.axis_index("zl") * 4 + lax.axis_index("x")
     fetches[0].wait()
+    squares = jnp.zeros((256, 256), jnp.float32)
+    for f in range(8):
+        x = resid_ref[f].astype(jnp.float32)
+        squares += x * x
+    level = lax.rsqrt(jnp.sum(squares, axis=1, keepdims=True) * (1.0 / D) + epsilon)
+    for f in range(8):
+        lanes = slice(f * 256, (f + 1) * 256)
+        rows_ref[:, lanes] = (
+            resid_ref[f].astype(jnp.float32) * level * gain_ref[:, lanes]
+        ).astype(jnp.bfloat16)
+    rows = rows_ref[...]
     fetches[1].wait()
-    col = lax.axis_index("zl") * 4 + lax.axis_index("x")
-    rows = rows_ref[...]
     across = (((1,), (1,)), ((), ()))
+    logits_ref[...] = lax.dot_general(
+        rows, router_ref[...], across, preferred_element_type=jnp.float32
+    )
     gate = lax.dot_general(rows, gate_ref[...], across, preferred_element_type=jnp.float32)
     fetches[2].wait()
     up = lax.dot_general(rows, up_ref[...], across, preferred_element_type=jnp.float32)
@@ -280,13 +311,17 @@
         ).astype(jnp.bfloat16)
 
 
-def shared(rows, gate, up, down):
+def shared(resid, gain, router, gate, up, down):
     return pl.pallas_call(
         shared_kernel,
-        in_specs=in_hbm(4),
-        out_specs=in_vmem(1)[0],
-        out_shape=jax.ShapeDtypeStruct((8, 256, 256), jnp.bfloat16),
+        in_specs=in_hbm(1) + in_vmem(2) + in_hbm(3),
+        out_specs=in_vmem(2),
+        out_shape=(
+            jax.ShapeDtypeStruct((8, 256, 256), jnp.bfloat16),
+            jax.ShapeDtypeStruct((256, 64), jnp.float32),
+        ),
         scratch_shapes=[
+            pltpu.VMEM((8, 256, 256), jnp.bfloat16),
             pltpu.VMEM((256, D), jnp.bfloat16),
             pltpu.VMEM(gate.shape, jnp.bfloat16),
             pltpu.VMEM(up.shape, jnp.bfloat16),
@@ -295,7 +330,7 @@
         ],
         compiler_params=pltpu.CompilerParams(vmem_limit_bytes=60 << 20),
         name="shared",
-    )(rows, gate, up, down)
+    )(resid, gain, router, gate, up, down)
 
 
 def expert_kernel(
@@ -452,10 +487,9 @@
         COL, 0, 0, tiled=True,
     )
     qkv_heads = came[:, :64].reshape(8, 4, 16, HEAD_DIM).transpose(1, 0, 2, 3).reshape(4, 128, HEAD_DIM)
-    qkv_block = qkv_heads.transpose(1, 0, 2).reshape(128, 512)
-    out_block = came[:, 576:].reshape(8, 2, 16, HEAD_DIM).transpose(1, 3, 0, 2).reshape(256, 128)
-
-    block = jnp.concatenate([qkv_heads.reshape(512, HEAD_DIM), out_block], axis=0)
+    out_rows = came[:, 576:].reshape(8, 2, 16, HEAD_DIM).transpose(1, 3, 0, 2).reshape(256, 128)
+
+    block = jnp.concatenate([qkv_heads.reshape(512, HEAD_DIM), out_rows], axis=0)
     mine = lax.all_to_all(
         jnp.broadcast_to(block[None], (8, 768, HEAD_DIM)), ("zh", "y"), 0, 0, tiled=True
     )
@@ -472,7 +506,7 @@
         jnp.broadcast_to(block[None], (4, 384, 256)), "y", 0, 0, tiled=True
     )
     kv_other = core_swap(kv_mine)
-    terms = attention(queries, kv_mine, kv_other, start, mine, other)
+    terms, qkv_block, out_block = attention(queries, kv_mine, kv_other, start, mine, other)
     got = lax.all_to_all(terms, COL, 0, 0, tiled=True)
     attn_part = jnp.sum(got.astype(jnp.float32), axis=0)
     resid = (tokens.astype(jnp.float32) + attn_part).astype(jnp.bfloat16)
@@ -489,12 +523,14 @@
     crossed = lax.dynamic_index_in_dim(by_quarter, quarter ^ 2, 2, keepdims=False)
     same_half = (jnp.arange(row_count) // 8 == zh_index)[None, :]
     slots = jnp.where(same_half, straight, crossed).T
-    mlp_in, outgoing = dispatch(full_resid, mlp_gain[None, :], slots)
+    outgoing = dispatch(full_resid, mlp_gain[None, :], slots)
     arrived = lax.all_to_all(
         outgoing, ROW + COL, 0, 0, axis_index_groups=DIAGONALS, tiled=True
     )
 
-    logits = jnp.dot(mlp_in, router, preferred_element_type=jnp.float32)
+    shared_part, logits = shared(
+        full_resid, mlp_gain[None, :], router.T, shared_gate.T, shared_up.T, shared_down
+    )
     router_probs = jax.nn.softmax(logits, axis=-1)
     picked_probs = jnp.where(member, router_probs, 0.0)
     route_weight = (
@@ -506,15 +542,14 @@
         jnp.repeat(route_weight, 2, axis=1)[:, :, None],
         jnp.bfloat16(0),
     ).reshape(tok_rows, 2 * n_experts * capacity)
-    shared_part = shared(mlp_in, shared_gate.T, shared_up.T, shared_down)
     pieces = []
     for step in range(col_count):
         piece = shared_part[step]
         if step:
             piece = lax.ppermute(piece, COL, [(i, i ^ step) for i in range(col_count)])
         pieces.append(piece)
-    arrived, combiner, pieces, qkv_block, out_block, cache_out = lax.optimization_barrier(
-        (arrived, combiner, pieces, qkv_block, out_block, cache_out)
+    arrived, combiner, pieces, cache_out = lax.optimization_barrier(
+        (arrived, combiner, pieces, cache_out)
     )
     shared_sum = sum(piece.astype(jnp.float32) for piece in pieces)
 

time: 247 us -> 244 us (0.988)
  local copies, waits for them, and re-layouts: 18 us -> 8.65 us
  Pallas kernels: 22 us -> 25.7 us
    unnamed x78 -> x36, local copies, waits for them, and re-layouts: 9.76 us -> 3.16 us
    pallas_call x2, Pallas kernels: 6.12 us -> 9.26 us  [the longest x1 6.63 us: shared(): pl.pallas_call(shared_kernel, in_specs=in_hbm(1) + in_vmem(2) + in_hbm(3)...]
  transfers between devices with their start and end apart: 23 -> 23, of which waited for: 11 -> 12; matrix products, arithmetic and copies ran while one was open for 6% -> 4% of each run, Pallas kernels for 2% -> 3%
where the time goes in v5:
time: 244 us
  waiting for transfers between devices  83 us (34%)
  blocking collectives  62.5 us (26%)
  starting transfers between devices  50.1 us (21%)
  Pallas kernels  25.7 us (11%)
  other arithmetic  9.54 us (4%)
  local copies, waits for them, and re-layouts  8.65 us (4%)
  matrix products  2.84 us (1%)
    all_to_all x1, waiting for transfers between devices, on_device(): lax.all_to_all(result.reshape(2 * n_experts, capacity, 256), ROW + COL, 0...  32.4 us
    all_to_all x1, blocking collectives, on_device(): lax.all_to_all(jnp.broadcast_to(block[None], (8, 768, HEAD_DIM)), ('zh',...  25.2 us
    all_to_all x1, blocking collectives, on_device(): lax.all_to_all(jnp.concatenate([groups, jnp.broadcast_to(token_parts, (8,...  20.9 us
    all_to_all x1, blocking collectives, on_device(): lax.all_to_all(jnp.broadcast_to(block[None], (4, 384, 256)), 'y', 0, 0, t...  16.4 us
    all_to_all x1, waiting for transfers between devices, on_device(): got = lax.all_to_all(terms, COL, 0, 0, tiled=True)  14.7 us
    all_to_all x1, waiting for transfers between devices, col_gather(): return lax.all_to_all(copies, COL, 0, 0, tiled=True)  13.5 us
    pallas_call x1, Pallas kernels, expert(): pl.pallas_call(expert_kernel, in_specs=in_hbm(3), out_specs=in_hbm(1)[0],...  9.83 us
    ppermute x4, starting transfers between devices, on_device(): received.append(lax.ppermute(layer_out, ('zh', 'y'), pairs))  8.64 us
  transfers between devices with their start and end apart: 23, of which 12 were waited for; matrix products, arithmetic and copies ran while one was open for 4% of the time, Pallas kernels for 3%

profile of v5, /device:TPU:97, one launch (start us, length us, event | category | flops | bytes accessed | tf_op | source)
XLA Modules:
  0.0 243.5 jit_solution(18227483178514601277)
XLA Ops:
  3.9 20.9 %all_to_all.35.came_ref = bf16[8,608,128]{2,1,0:T(8,128)(2,1)S(1)} all-to-all(bf16[8,608,128]{2,1,0:T(8,128)(2,1)S(1)} %pad_maximum_fusion), channel_id=1, replica_groups=mesh['zh'=2,'y'=4,'k'=2,'zl'=2,'x'=4] {'zl','x'}, dimensions={0} | all-to-all | bytes 2490368 | tf_op jit(solution)/shard_map/all_to_all | solution.py:483
  26.1 25.2 %all_to_all.36.mine_ref.out_mine_ref = bf16[8,768,128]{2,1,0:T(8,128)(2,1)S(1)} all-to-all(bf16[8,768,128]{2,1,0:T(8,128)(2,1)S(1)} %broadcast_in_dim.177), channel_id=1, replica_groups=mesh['zh'=2,'y'=4,'k'=2,'zl'=2,'x'=4] {'zh','y'}, dimensions={0} | all-to-all | bytes 3145728 | tf_op jit(solution)/shard_map/all_to_all | solution.py:493
  51.3 2.6 %collective-permute-start = (bf16[8,768,128]{2,1,0:T(8,128)(2,1)S(1)}, bf16[8,768,128]{2,1,0:T(8,128)(2,1)S(1)}, u32[]{:S(2)}, u32[]{:S(2)}) collective-permute-start(bf16[8,768,128]{2,1,0:T(8,128)(2,1)S(1)} %all_to_all.36.mine_ref.out_mine_ref), channel_id=1, source_target_pairs={{0,8},{8,0},{1,9},{9,1},{2,10},{10,2},{3,11},{11,3},{4,12},{12,4},... | collective-permute-start | bytes 4718600 | tf_op jit(solution)/shard_map/ppermute | solution.py:60
  55.1 1.8 collective-permute-done.other_ref.out_other_ref
  60.2 16.4 %all_to_all.37.mine_ref = bf16[4,384,256]{2,1,0:T(8,128)(2,1)S(1)} all-to-all(bf16[4,384,256]{2,1,0:T(8,128)(2,1)S(1)} %broadcast_in_dim.180), channel_id=1, replica_groups=mesh['zh'=2,'y'=4,'k'=2,'zl'=2,'x'=4] {'y'}, dimensions={0} | all-to-all | bytes 1572864 | tf_op jit(solution)/shard_map/all_to_all | solution.py:505
  76.7 2.3 collective-permute-done.2.other_ref
  78.9 4.3 %attention.1 = (bf16[8,256,256]{2,1,0:T(8,128)(2,1)S(1)}, bf16[128,512]{1,0:T(8,128)(2,1)}, bf16[256,128]{1,0:T(8,128)(2,1)}) custom-call(bf16[2,256,128]{2,1,0:T(8,128)(2,1)S(1)} %get-tuple-element.22.q_hbm, bf16[4,384,256]{2,1,0:T(8,128)(2,1)S(1)} %all_to_all.37.mine_ref, bf16[4,384,256]{2,1,0:T(8,128)(2,1)S(1)} %collective-permute-done.2.other_ref, ...), custom_call_target="tpu_custom_call" | custom-call | tf_op jit(solution)/shard_map/attention/pallas_call | solution.py:215
  84.2 5.1 %all-to-all-start.3 = ((bf16[8,256,256]{2,1,0:T(8,128)(2,1)}), bf16[8,256,256]{2,1,0:T(8,128)(2,1)S(1)}, u32[]{:S(2)}, u32[]{:S(2)}) async-start(bf16[8,256,256]{2,1,0:T(8,128)(2,1)} %copy-done.3), calls=%async_computation.3 | async-start | bytes 2097152 | tf_op jit(solution)/shard_map/all_to_all | solution.py:510
  89.3 14.7 %all-to-all-done.3 = bf16[8,256,256]{2,1,0:T(8,128)(2,1)S(1)} async-done(((bf16[8,256,256]{2,1,0:T(8,128)(2,1)}), bf16[8,256,256]{2,1,0:T(8,128)(2,1)S(1)}, u32[]{:S(2)}, u32[]{:S(2)}) %all-to-all-start.3) | async-done | bytes 1048608 | tf_op jit(solution)/shard_map/all_to_all | solution.py:510
  105.2 4.7 %all-to-all-start.4 = ((bf16[8,256,256]{2,1,0:T(8,128)(2,1)}), bf16[8,256,256]{2,1,0:T(8,128)(2,1)S(1)}, u32[]{:S(2)}, u32[]{:S(2)}) async-start(bf16[8,256,256]{2,1,0:T(8,128)(2,1)} %broadcast_in_dim.181), calls=%async_computation.4 | async-start | bytes 2097152 | tf_op jit(solution)/shard_map/all_to_all | solution.py:65
  111.0 13.5 %all-to-all-done.4.resid_ref.resid_hbm = bf16[8,256,256]{2,1,0:T(8,128)(2,1)S(1)} async-done(((bf16[8,256,256]{2,1,0:T(8,128)(2,1)}), bf16[8,256,256]{2,1,0:T(8,128)(2,1)S(1)}, u32[]{:S(2)}, u32[]{:S(2)}) %all-to-all-start.4) | async-done | bytes 1048608 | tf_op jit(solution)/shard_map/all_to_all | solution.py:65
  124.6 2.6 %dispatch.1 = bf16[16,40,2048]{2,1,0:T(8,128)(2,1)} custom-call(bf16[8,256,256]{2,1,0:T(8,128)(2,1)S(1)} %all-to-all-done.4.resid_ref.resid_hbm, f32[1,2048]{1,0:T(1,128)S(1)} %bitcast.127, s32[16,256]{1,0:T(8,128)S(1)} %fusion.6.slots_ref), custom_call_target="tpu_custom_call" | custom-call | tf_op jit(solution)/shard_map/dispatch/pallas_call | solution.py:255
  127.2 7.4 %all-to-all-start.5 = ((bf16[16,40,2048]{2,1,0:T(8,128)(2,1)}), bf16[16,40,2048]{2,1,0:T(8,128)(2,1)}, u32[]{:S(2)}, u32[]{:S(2)}) async-start(bf16[16,40,2048]{2,1,0:T(8,128)(2,1)} %dispatch.1), calls=%async_computation.5 | async-start | bytes 5242880 | tf_op jit(solution)/shard_map/all_to_all | solution.py:527
  135.6 6.6 %shared.1 = (bf16[8,256,256]{2,1,0:T(8,128)(2,1)}, f32[256,64]{1,0:T(8,128)}) custom-call(bf16[8,256,256]{2,1,0:T(8,128)(2,1)} %copy-done, f32[1,2048]{1,0:T(1,128)} %bitcast.126, bf16[64,2048]{1,0:T(8,128)(2,1)} %bitcast.138, bf16[352,2048]{1,0:T(8,128)(2,1)} %bitcast.132, bf16[352,2048]{1,0:T(8,128)(2,1)} %bitcast.133, bf16[352,2048]{1,0:T(8,128)(2,1)} %down_hbm.1), custom_call_target="tpu_custom_call" | custom-call | tf_op jit(solution)/shard_map/shared/pallas_call | solution.py:315
  142.3 2.1 slice_bitcast_fusion
  144.9 2.7 %collective-permute-start.8 = (bf16[256,256]{1,0:T(8,128)(2,1)S(1)}, bf16[256,256]{1,0:T(8,128)(2,1)S(1)}, u32[]{:S(2)}, u32[]{:S(2)}) collective-permute-start(bf16[256,256]{1,0:T(8,128)(2,1)S(1)} %get-tuple-element.45), channel_id=1, source_target_pairs={{0,6},{1,7},{2,4},{3,5},{4,2},{5,3},{6,0},{7,1},{8,14},{9,15},{10,... | collective-permute-start | bytes 393224 | tf_op jit(solution)/shard_map/ppermute | solution.py:549
  147.9 1.8 collective-permute-start.6
  153.2 2.2 collective-permute-done.9
  157.4 3.0 %collective-permute-done.6 = bf16[256,256]{1,0:T(8,128)(2,1)} collective-permute-done((bf16[256,256]{1,0:T(8,128)(2,1)}, bf16[256,256]{1,0:T(8,128)(2,1)}, u32[]{:S(2)}, u32[]{:S(2)}) %collective-permute-start.6) | collective-permute-done | bytes 131104 | tf_op jit(solution)/shard_map/ppermute | solution.py:549
  161.1 7.7 %all-to-all-done.5 = bf16[16,40,2048]{2,1,0:T(8,128)(2,1)} async-done(((bf16[16,40,2048]{2,1,0:T(8,128)(2,1)}), bf16[16,40,2048]{2,1,0:T(8,128)(2,1)}, u32[]{:S(2)}, u32[]{:S(2)}) %all-to-all-start.5) | async-done | bytes 2621472 | tf_op jit(solution)/shard_map/all_to_all | solution.py:527
  168.8 9.8 %expert.1 = bf16[16,8,40,256]{3,2,1,0:T(8,128)(2,1)} custom-call(bf16[640,2048]{1,0:T(8,128)(2,1)} %bitcast.44.rows_hbm, bf16[2048,1408]{1,0:T(8,128)(2,1)} %bitcast.130, bf16[704,2048]{1,0:T(8,128)(2,1)} %bitcast.131), custom_call_target="tpu_custom_call" | custom-call | tf_op jit(solution)/shard_map/expert/pallas_call | solution.py:400
  178.6 7.9 %all-to-all-start.6 = ((bf16[128,40,256]{2,1,0:T(8,128)(2,1)}), bf16[128,40,256]{2,1,0:T(8,128)(2,1)}, u32[]{:S(2)}, u32[]{:S(2)}) async-start(bf16[128,40,256]{2,1,0:T(8,128)(2,1)} %bitcast.129), calls=%async_computation.6 | async-start | bytes 5242880 | tf_op jit(solution)/shard_map/all_to_all | solution.py:559
  187.0 32.4 %all-to-all-done.6 = bf16[128,40,256]{2,1,0:T(8,128)(2,1)} async-done(((bf16[128,40,256]{2,1,0:T(8,128)(2,1)}), bf16[128,40,256]{2,1,0:T(8,128)(2,1)}, u32[]{:S(2)}, u32[]{:S(2)}) %all-to-all-start.6) | async-done | bytes 2621472 | tf_op jit(solution)/shard_map/all_to_all | solution.py:559
  219.4 2.8 %fusion.1 = bf16[256,256]{1,0:T(8,128)(2,1)S(1)} fusion(bf16[256,5120]{0,1:T(8,128)(2,1)S(1)} %fusion, bf16[5120,256]{1,0:T(8,128)(2,1)} %bitcast.48, bf16[256,256]{1,0:T(8,128)(2,1)S(1)} %copy-done.10, bf16[256,256]{1,0:T(8,128)(2,1)S(1)} %copy-done.12, bf16[256,256]{1,0:T(8,128)(2,1)} %collective-permute-done.7, ...), kind=kOutput, calls=%fused_computation.5 | convolution fusion | flops 672333824 | bytes 6553600 | tf_op jit(solution)/shard_map/dot_general | solution.py:562
  222.2 1.3 collective-permute-start.13
  223.5 1.3 collective-permute-start.12
  224.8 1.3 collective-permute-start.11
  226.1 4.8 %collective-permute-start.10 = (bf16[256,256]{1,0:T(8,128)(2,1)S(1)}, bf16[256,256]{1,0:T(8,128)(2,1)S(1)}, u32[]{:S(2)}, u32[]{:S(2)}) collective-permute-start(bf16[256,256]{1,0:T(8,128)(2,1)S(1)} %fusion.1), channel_id=1, source_target_pairs={{0,64},{16,80},{32,96},{48,112},{64,0},{80,16},{96,32},{112,48},{1... | collective-permute-start | bytes 393224 | tf_op jit(solution)/shard_map/ppermute | solution.py:576
  231.0 2.5 %collective-permute-start.18 = (bf16[128,256]{1,0:T(8,128)(2,1)S(1)}, bf16[128,256]{1,0:T(8,128)(2,1)S(1)}, u32[]{:S(2)}, u32[]{:S(2)}) collective-permute-start(bf16[128,256]{1,0:T(8,128)(2,1)S(1)} %slice.171), channel_id=1, source_target_pairs={{56,0},{72,16},{88,32},{104,48},{120,64},{57,1},{73,17},{89,33},{1... | collective-permute-start | bytes 196616 | tf_op jit(solution)/shard_map/ppermute | solution.py:577
  234.2 2.2 collective-permute-start.16
  236.4 1.6 collective-permute-done.11.refs_1_
  238.9 2.1 collective-permute-done.10.refs_0_
  (133 shorter events, 24.7 us)
Async XLA Ops:
  25.9 28.0 %copy-start.8 = (s32[8]{0:T(128)S(1)}, s32[8]{0:T(128)}, u32[]{:S(2)}) copy-start(s32[8]{0:T(128)} %param.26) | copy-start | bytes 100
  25.9 28.0 %copy-start.13 = (s32[8]{0:T(128)S(1)}, s32[8]{0:T(128)}, u32[]{:S(2)}) copy-start(s32[8]{0:T(128)} %param.25) | copy-start | bytes 100
  26.1 30.8 %copy-start.5 = (f32[2048]{0:T(1024)S(1)}, f32[2048]{0:T(1024)}, u32[]{:S(2)}) copy-start(f32[2048]{0:T(1024)} %param.15) | copy-start | bytes 24580
  51.3 5.6 %collective-permute-start = (bf16[8,768,128]{2,1,0:T(8,128)(2,1)S(1)}, bf16[8,768,128]{2,1,0:T(8,128)(2,1)S(1)}, u32[]{:S(2)}, u32[]{:S(2)}) collective-permute-start(bf16[8,768,128]{2,1,0:T(8,128)(2,1)S(1)} %all_to_all.36.mine_ref.out_mine_ref), channel_id=1, source_target_pairs={{0,8},{8,0},{1,9},{9,1},{2,10},{10,2},{3,11},{11,3},{4,12},{12,4},... | collective-permute-start | bytes 4718600 | tf_op jit(solution)/shard_map/ppermute | solution.py:60
  59.5 0.7 collective-permute-start.1
  76.6 2.3 collective-permute-start.2
  78.9 10.3 %copy-start.7 = (s32[256,6]{0,1:T(8,128)S(1)}, s32[256,6]{0,1:T(8,128)}, u32[]{:S(2)}) copy-start(s32[256,6]{0,1:T(8,128)} %param.27) | copy-start | bytes 18436
  84.2 20.0 %copy-start.6 = (bf16[256,256]{1,0:T(8,128)(2,1)S(1)}, bf16[256,256]{1,0:T(8,128)(2,1)}, u32[]{:S(2)}) copy-start(bf16[256,256]{1,0:T(8,128)(2,1)} %param.14) | copy-start | bytes 393220
  84.2 19.8 %all-to-all-start.3 = ((bf16[8,256,256]{2,1,0:T(8,128)(2,1)}), bf16[8,256,256]{2,1,0:T(8,128)(2,1)S(1)}, u32[]{:S(2)}, u32[]{:S(2)}) async-start(bf16[8,256,256]{2,1,0:T(8,128)(2,1)} %copy-done.3), calls=%async_computation.3 | async-start | bytes 2097152 | tf_op jit(solution)/shard_map/all_to_all | solution.py:510
  104.1 20.4 %copy-start.4 = (f32[2048]{0:T(1024)S(1)}, f32[2048]{0:T(1024)}, u32[]{:S(2)}) copy-start(f32[2048]{0:T(1024)} %param.16) | copy-start | bytes 24580
  105.2 19.4 %all-to-all-start.4 = ((bf16[8,256,256]{2,1,0:T(8,128)(2,1)}), bf16[8,256,256]{2,1,0:T(8,128)(2,1)S(1)}, u32[]{:S(2)}, u32[]{:S(2)}) async-start(bf16[8,256,256]{2,1,0:T(8,128)(2,1)} %broadcast_in_dim.181), calls=%async_computation.4 | async-start | bytes 2097152 | tf_op jit(solution)/shard_map/all_to_all | solution.py:65
  124.6 2.6 %copy-start = (bf16[8,256,256]{2,1,0:T(8,128)(2,1)}, bf16[8,256,256]{2,1,0:T(8,128)(2,1)S(1)}, u32[]{:S(2)}) copy-start(bf16[8,256,256]{2,1,0:T(8,128)(2,1)S(1)} %all-to-all-done.4.resid_ref.resid_hbm) | copy-start | bytes 3145732
  127.2 41.6 %all-to-all-start.5 = ((bf16[16,40,2048]{2,1,0:T(8,128)(2,1)}), bf16[16,40,2048]{2,1,0:T(8,128)(2,1)}, u32[]{:S(2)}, u32[]{:S(2)}) async-start(bf16[16,40,2048]{2,1,0:T(8,128)(2,1)} %dispatch.1), calls=%async_computation.5 | async-start | bytes 5242880 | tf_op jit(solution)/shard_map/all_to_all | solution.py:527
  144.3 11.0 %collective-permute-start.9 = (bf16[256,256]{1,0:T(8,128)(2,1)S(1)}, bf16[256,256]{1,0:T(8,128)(2,1)S(1)}, u32[]{:S(2)}, u32[]{:S(2)}) collective-permute-start(bf16[256,256]{1,0:T(8,128)(2,1)S(1)} %get-tuple-element.44), channel_id=1, source_target_pairs={{0,7},{1,6},{2,5},{3,4},{4,3},{5,2},{6,1},{7,0},{8,15},{9,14},{10,... | collective-permute-start | bytes 393224 | tf_op jit(solution)/shard_map/ppermute | solution.py:549
  144.9 10.5 %collective-permute-start.8 = (bf16[256,256]{1,0:T(8,128)(2,1)S(1)}, bf16[256,256]{1,0:T(8,128)(2,1)S(1)}, u32[]{:S(2)}, u32[]{:S(2)}) collective-permute-start(bf16[256,256]{1,0:T(8,128)(2,1)S(1)} %get-tuple-element.45), channel_id=1, source_target_pairs={{0,6},{1,7},{2,4},{3,5},{4,2},{5,3},{6,0},{7,1},{8,14},{9,15},{10,... | collective-permute-start | bytes 393224 | tf_op jit(solution)/shard_map/ppermute | solution.py:549
  147.6 9.7 %collective-permute-start.7 = (bf16[256,256]{1,0:T(8,128)(2,1)}, bf16[256,256]{1,0:T(8,128)(2,1)}, u32[]{:S(2)}, u32[]{:S(2)}) collective-permute-start(bf16[256,256]{1,0:T(8,128)(2,1)} %get-tuple-element.46), channel_id=1, source_target_pairs={{0,5},{1,4},{2,7},{3,6},{4,1},{5,0},{6,3},{7,2},{8,13},{9,12},{10,... | collective-permute-start | bytes 393224 | tf_op jit(solution)/shard_map/ppermute | solution.py:549
  147.9 12.5 %collective-permute-start.6 = (bf16[256,256]{1,0:T(8,128)(2,1)}, bf16[256,256]{1,0:T(8,128)(2,1)}, u32[]{:S(2)}, u32[]{:S(2)}) collective-permute-start(bf16[256,256]{1,0:T(8,128)(2,1)} %get-tuple-element.47), channel_id=1, source_target_pairs={{0,4},{1,5},{2,6},{3,7},{4,0},{5,1},{6,2},{7,3},{8,12},{9,13},{10,... | collective-permute-start | bytes 393224 | tf_op jit(solution)/shard_map/ppermute | solution.py:549
  149.7 10.7 %collective-permute-start.5 = (bf16[256,256]{1,0:T(8,128)(2,1)S(1)}, bf16[256,256]{1,0:T(8,128)(2,1)}, u32[]{:S(2)}, u32[]{:S(2)}) collective-permute-start(bf16[256,256]{1,0:T(8,128)(2,1)S(1)} %get-tuple-element.48), channel_id=1, source_target_pairs={{0,3},{1,2},{2,1},{3,0},{4,7},{5,6},{6,5},{7,4},{8,11},{9,10},{10,... | collective-permute-start | bytes 393224 | tf_op jit(solution)/shard_map/ppermute | solution.py:549
  155.3 5.7 %collective-permute-start.4 = (bf16[256,256]{1,0:T(8,128)(2,1)S(1)}, bf16[256,256]{1,0:T(8,128)(2,1)}, u32[]{:S(2)}, u32[]{:S(2)}) collective-permute-start(bf16[256,256]{1,0:T(8,128)(2,1)S(1)} %get-tuple-element.49), channel_id=1, source_target_pairs={{0,2},{1,3},{2,0},{3,1},{4,6},{5,7},{6,4},{7,5},{8,10},{9,11},{10,... | collective-permute-start | bytes 393224 | tf_op jit(solution)/shard_map/ppermute | solution.py:549
  155.4 5.7 %collective-permute-start.3 = (bf16[256,256]{1,0:T(8,128)(2,1)S(1)}, bf16[256,256]{1,0:T(8,128)(2,1)}, u32[]{:S(2)}, u32[]{:S(2)}) collective-permute-start(bf16[256,256]{1,0:T(8,128)(2,1)S(1)} %get-tuple-element.50), channel_id=1, source_target_pairs={{0,1},{1,0},{2,3},{3,2},{4,5},{5,4},{6,7},{7,6},{8,9},{9,8},{10,11... | collective-permute-start | bytes 393224 | tf_op jit(solution)/shard_map/ppermute | solution.py:549
  178.6 40.8 %copy-start.10 = (bf16[256,256]{1,0:T(8,128)(2,1)S(1)}, bf16[256,256]{1,0:T(8,128)(2,1)}, u32[]{:S(2)}) copy-start(bf16[256,256]{1,0:T(8,128)(2,1)} %copy-done.9) | copy-start | bytes 393220
  178.6 40.7 %copy-start.12 = (bf16[256,256]{1,0:T(8,128)(2,1)S(1)}, bf16[256,256]{1,0:T(8,128)(2,1)}, u32[]{:S(2)}) copy-start(bf16[256,256]{1,0:T(8,128)(2,1)} %copy-done.11) | copy-start | bytes 393220
  178.6 40.7 %all-to-all-start.6 = ((bf16[128,40,256]{2,1,0:T(8,128)(2,1)}), bf16[128,40,256]{2,1,0:T(8,128)(2,1)}, u32[]{:S(2)}, u32[]{:S(2)}) async-start(bf16[128,40,256]{2,1,0:T(8,128)(2,1)} %bitcast.129), calls=%async_computation.6 | async-start | bytes 5242880 | tf_op jit(solution)/shard_map/all_to_all | solution.py:559
  222.2 11.3 %collective-permute-start.13 = (bf16[256,256]{1,0:T(8,128)(2,1)S(1)}, bf16[256,256]{1,0:T(8,128)(2,1)S(1)}, u32[]{:S(2)}, u32[]{:S(2)}) collective-permute-start(bf16[256,256]{1,0:T(8,128)(2,1)S(1)} %fusion.1), channel_id=1, source_target_pairs={{0,112},{16,64},{32,80},{48,96},{1,113},{17,65},{33,81},{49,97},{2... | collective-permute-start | bytes 393224 | tf_op jit(solution)/shard_map/ppermute | solution.py:576
  223.5 10.7 %collective-permute-start.12 = (bf16[256,256]{1,0:T(8,128)(2,1)S(1)}, bf16[256,256]{1,0:T(8,128)(2,1)S(1)}, u32[]{:S(2)}, u32[]{:S(2)}) collective-permute-start(bf16[256,256]{1,0:T(8,128)(2,1)S(1)} %fusion.1), channel_id=1, source_target_pairs={{0,96},{16,112},{32,64},{48,80},{1,97},{17,113},{33,65},{49,81},{2... | collective-permute-start | bytes 393224 | tf_op jit(solution)/shard_map/ppermute | solution.py:576
  224.8 13.2 %collective-permute-start.11 = (bf16[256,256]{1,0:T(8,128)(2,1)S(1)}, bf16[256,256]{1,0:T(8,128)(2,1)S(1)}, u32[]{:S(2)}, u32[]{:S(2)}) collective-permute-start(bf16[256,256]{1,0:T(8,128)(2,1)S(1)} %fusion.1), channel_id=1, source_target_pairs={{0,80},{16,96},{32,112},{48,64},{1,81},{17,97},{33,113},{49,65},{2... | collective-permute-start | bytes 393224 | tf_op jit(solution)/shard_map/ppermute | solution.py:576
  226.1 14.8 %collective-permute-start.10 = (bf16[256,256]{1,0:T(8,128)(2,1)S(1)}, bf16[256,256]{1,0:T(8,128)(2,1)S(1)}, u32[]{:S(2)}, u32[]{:S(2)}) collective-permute-start(bf16[256,256]{1,0:T(8,128)(2,1)S(1)} %fusion.1), channel_id=1, source_target_pairs={{0,64},{16,80},{32,96},{48,112},{64,0},{80,16},{96,32},{112,48},{1... | collective-permute-start | bytes 393224 | tf_op jit(solution)/shard_map/ppermute | solution.py:576
  231.0 10.4 %collective-permute-start.18 = (bf16[128,256]{1,0:T(8,128)(2,1)S(1)}, bf16[128,256]{1,0:T(8,128)(2,1)S(1)}, u32[]{:S(2)}, u32[]{:S(2)}) collective-permute-start(bf16[128,256]{1,0:T(8,128)(2,1)S(1)} %slice.171), channel_id=1, source_target_pairs={{56,0},{72,16},{88,32},{104,48},{120,64},{57,1},{73,17},{89,33},{1... | collective-permute-start | bytes 196616 | tf_op jit(solution)/shard_map/ppermute | solution.py:577
  233.5 7.9 %collective-permute-start.17 = (bf16[256,256]{1,0:T(8,128)(2,1)S(1)}, bf16[256,256]{1,0:T(8,128)(2,1)S(1)}, u32[]{:S(2)}, u32[]{:S(2)}) collective-permute-start(bf16[256,256]{1,0:T(8,128)(2,1)S(1)} %collective-permute-done.13.refs_3_), channel_id=1, source_target_pairs={{0,8},{8,0},{1,9},{9,1},{2,10},{10,2},{3,11},{11,3},{4,12},{12,4},... | collective-permute-start | bytes 393224 | tf_op jit(solution)/shard_map/ppermute | solution.py:60
  234.2 7.3 %collective-permute-start.16 = (bf16[256,256]{1,0:T(8,128)(2,1)S(1)}, bf16[256,256]{1,0:T(8,128)(2,1)S(1)}, u32[]{:S(2)}, u32[]{:S(2)}) collective-permute-start(bf16[256,256]{1,0:T(8,128)(2,1)S(1)} %collective-permute-done.12.refs_2_), channel_id=1, source_target_pairs={{0,8},{8,0},{1,9},{9,1},{2,10},{10,2},{3,11},{11,3},{4,12},{12,4},... | collective-permute-start | bytes 393224 | tf_op jit(solution)/shard_map/ppermute | solution.py:60
  238.0 3.5 %collective-permute-start.15 = (bf16[256,256]{1,0:T(8,128)(2,1)S(1)}, bf16[256,256]{1,0:T(8,128)(2,1)S(1)}, u32[]{:S(2)}, u32[]{:S(2)}) collective-permute-start(bf16[256,256]{1,0:T(8,128)(2,1)S(1)} %collective-permute-done.11.refs_1_), channel_id=1, source_target_pairs={{0,8},{8,0},{1,9},{9,1},{2,10},{10,2},{3,11},{11,3},{4,12},{12,4},... | collective-permute-start | bytes 393224 | tf_op jit(solution)/shard_map/ppermute | solution.py:60
  241.0 1.4 collective-permute-start.14
  (5 other events, 5.7 us)
